TPU v7x, 128 devices: a whole 4x4x4 slice. The times are simulated.
128 devices in a mesh: dp: 2 (over x_lo), width: 8 (over y, core), hidden: 8 (over z, x_hi).
Axes of the slice: x: 4 (x_hi: 2, x_lo: 2; x = x_hi * 2 + x_lo), y: 4, z: 4, core: 2. Of those that a mesh axis runs over, the one named last changes fastest.
Arguments:
- tokens: bfloat16 [1024, 8192], P('dp', 'width'), may hold values from -6 to 6
- target: bfloat16 [1024, 8192], P('dp', 'width'), may hold values from -6 to 6
- gate_weight: bfloat16 [8192, 14336], P('width', 'hidden'), may hold values from -0.0625 to 0.0625
- up_weight: bfloat16 [8192, 14336], P('width', 'hidden'), may hold values from -0.0625 to 0.0625
- down_weight: bfloat16 [14336, 8192], P('hidden', 'width'), may hold values from -0.046875 to 0.046875
- probe_sign: bfloat16 [8192, 14336], P('width', 'hidden'), may hold values from -1 to 1, as said below
Outputs:
- gate_grad: bfloat16 [8192, 14336], P(('width', 'dp'), 'hidden')
- hess_diag: bfloat16 [8192, 14336], P(('width', 'dp'), 'hidden')
Inputs may be any that keep to these rules, and one draw needn't show every extreme that they name: `probe_sign`: every entry is -1 or +1.
All inputs are finite; a program needn't handle non-finite values.
Results may differ from a plain program's by a relative error of at most 0.019.
Values may be sent and summed in bfloat16 or wider, within the bound.
No kernel may reach another device: no remote copies, remote signals or barrier semaphores. Data moves between devices by JAX's collectives and lax.ppermute only.
A program may use at most 128 MiB of HBM per device.

v0:
```python
import math

import jax
import jax.numpy as jnp
from jax import lax
from jax.sharding import PartitionSpec as P

D = 8192


def matmul(left, right):
    return jnp.dot(left, right, preferred_element_type=jnp.float32)


def right_trans(left, right):
    return lax.dot_general(
        left, right, (((1,), (1,)), ((), ())), preferred_element_type=jnp.float32
    )


def left_trans(left, right):
    return lax.dot_general(
        left, right, (((0,), (0,)), ((), ())), preferred_element_type=jnp.float32
    )


def coefficients(gate_pre, up_pre, tangent):
    sigmoid_gate = jax.nn.sigmoid(gate_pre)
    first = sigmoid_gate * (1.0 + gate_pre * (1.0 - sigmoid_gate))
    second = sigmoid_gate * (1.0 - sigmoid_gate) * (2.0 + gate_pre * (1.0 - 2.0 * sigmoid_gate))
    hidden = (gate_pre * sigmoid_gate * up_pre).astype(jnp.bfloat16)
    hidden_dot = (first * tangent * up_pre).astype(jnp.bfloat16)
    coeff_first = (first * up_pre).astype(jnp.bfloat16)
    coeff_second = (second * tangent * up_pre).astype(jnp.bfloat16)
    return (hidden, hidden_dot, coeff_first, coeff_second)


def errors(back, back_dot, coeff_first, coeff_second):
    first_f = coeff_first.astype(jnp.float32)
    err_grad = (back * first_f).astype(jnp.bfloat16)
    err_hess = (back * coeff_second.astype(jnp.float32) + back_dot * first_f).astype(jnp.bfloat16)
    return (err_grad, err_hess)


def on_device(tokens, target, gate_weight, up_weight, down_weight, probe_sign):
    inv_width = 1.0 / math.sqrt(D)
    token_rows = tokens.shape[0]
    token_scale = 1.0 / math.sqrt(token_rows * lax.axis_size("dp"))
    gate_pre, up_pre, tangent = lax.psum(
        (
            matmul(tokens, gate_weight),
            matmul(tokens, up_weight),
            matmul(tokens, probe_sign) * inv_width,
        ),
        "width",
    )
    hidden, hidden_dot, coeff_first, coeff_second = coefficients(gate_pre, up_pre, tangent)
    output, output_dot = lax.psum(
        (matmul(hidden, down_weight), matmul(hidden_dot, down_weight)), "hidden"
    )
    resid = (output - target.astype(jnp.float32)).astype(jnp.bfloat16)
    output_dot_b = output_dot.astype(jnp.bfloat16)
    back, back_dot = lax.psum(
        (right_trans(resid, down_weight), right_trans(output_dot_b, down_weight)), "width"
    )
    err_grad, err_hess = errors(back, back_dot, coeff_first, coeff_second)
    grad_term = left_trans(tokens, err_grad) * token_scale
    hess_term = left_trans(tokens, err_hess) * token_scale
    grad_sum, hv_sum = (
        lax.psum_scatter(
            grad_term.astype(jnp.bfloat16), "dp", scatter_dimension=0, tiled=True
        ).astype(jnp.float32),
        lax.psum_scatter(
            hess_term.astype(jnp.bfloat16), "dp", scatter_dimension=0, tiled=True
        ).astype(jnp.float32),
    )
    half_rows = grad_sum.shape[0]
    probe_rows = lax.dynamic_slice_in_dim(
        probe_sign, lax.axis_index("dp") * half_rows, half_rows, 0
    )
    gate_grad = grad_sum.astype(jnp.bfloat16)
    hess_diag = (probe_rows.astype(jnp.float32) * hv_sum * inv_width).astype(jnp.bfloat16)
    return (gate_grad, hess_diag)


def solution(mesh):
    return jax.shard_map(
        on_device,
        mesh=mesh,
        in_specs=(
            P("dp", "width"),
            P("dp", "width"),
            P("width", "hidden"),
            P("width", "hidden"),
            P("hidden", "width"),
            P("width", "hidden"),
        ),
        out_specs=(P(("width", "dp"), "hidden"), P(("width", "dp"), "hidden")),
        check_vma=False,
    )
```

profile of v0, /device:TPU:1, one launch (start us, length us, event | category | flops | bytes accessed | tf_op | source)
XLA Modules:
  0.0 563.9 jit_solution(333357687607422016)
XLA Ops:
  7.2 0.0 copy-start
  7.2 0.0 all-reduce.11.cloned.1.call-start
  7.2 1.2 copy-done
  8.4 0.0 copy-start.1
  8.4 6.1 %convolution_multiply_fusion = f32[512,1792]{1,0:T(8,128)} fusion(bf16[512,1024]{1,0:T(8,128)(2,1)S(1)} %copy-done, bf16[1024,1792]{1,0:T(8,128)(2,1)} %param.11), kind=kOutput, calls=%fused_computation.20 | convolution fusion | flops 1879965696 | bytes 8388608 | tf_op jit(solution)/shard_map/dot_general | solution.py:12
  14.5 0.0 copy-done.1
  14.5 3.9 fusion.22
  18.4 0.0 copy-done.2
  18.4 4.0 fusion.23
  22.4 0.0 all-reduce.11.cloned.1.call-update
  22.4 0.0 all-reduce.7.cloned.1.call-start
  22.4 132.1 %all-reduce.11.cloned.1.call-done = (f32[512,1792]{1,0:T(8,128)}, f32[512,1792]{1,0:T(8,128)}, f32[512,1792]{1,0:T(8,128)}) async-done(((f32[512,1792]{1,0:T(8,128)}, f32[512,1792]{1,0:T(8,128)}, f32[512,1792]{1,0:T(8,128)}), (f32[512,1792]{1,0:T(8,128)}, f32[512,1792]{1,0:T(8,128)}, f32[512,1792]{1,0:T(8,128)})) %all-reduce.11.cloned.1.call-update) | async-done | bytes 11010064 | tf_op jit(solution)/shard_map/psum | solution.py:49
  154.6 7.6 %fusion.13 = f32[512,1024]{1,0:T(8,128)} fusion(bf16[1792,1024]{1,0:T(8,128)(2,1)} %param.10, f32[512,1792]{1,0:T(8,128)} %get-tuple-element.4, f32[512,1792]{1,0:T(8,128)} %get-tuple-element.5), kind=kOutput, calls=%fused_computation.25 | convolution fusion | flops 1884553216 | bytes 13107200 | tf_op jit(solution)/shard_map/dot_general | solution.py:12
  162.2 7.9 %fusion.11 = f32[512,1024]{1,0:T(8,128)S(1)} fusion(bf16[1792,1024]{1,0:T(8,128)(2,1)} %param.10, f32[512,1792]{1,0:T(8,128)} %get-tuple-element.4, f32[512,1792]{1,0:T(8,128)} %get-tuple-element.6, f32[512,1792]{1,0:T(8,128)} %get-tuple-element.5), kind=kOutput, calls=%fused_computation.24 | convolution fusion | flops 1888223232 | bytes 16777216 | tf_op jit(solution)/shard_map/dot_general | solution.py:12
  170.1 0.0 all-reduce.7.cloned.1.call-update
  170.1 0.0 all-reduce.9.cloned.1.call-start
  170.2 148.9 %all-reduce.12 = bf16[512,1024]{1,0:T(8,128)(2,1)} all-reduce(f32[512,1024]{1,0:T(8,128)S(1)} %fusion.11), channel_id=1, replica_groups=mesh['dp'=2,'width'=8,'hidden'=8] {'hidden'}, use_global_device_ids=true, to_apply=%region_6.0 | all-reduce | flops 524288 | bytes 3145728 | tf_op jit(solution)/shard_map/psum | solution.py:58
  319.1 6.4 %fusion.24 = f32[512,1792]{1,0:T(8,128)} fusion(bf16[512,1024]{1,0:T(8,128)(2,1)} %all-reduce.12, bf16[1792,1024]{1,0:T(8,128)(2,1)} %param.10), kind=kOutput, calls=%fused_computation.34 | convolution fusion | flops 1879048192 | bytes 8388608 | tf_op jit(solution)/shard_map/dot_general | solution.py:16
  325.5 14.9 %all-reduce.7.cloned.1.call-done = f32[512,1024]{1,0:T(8,128)} async-done(((f32[512,1024]{1,0:T(8,128)}), f32[512,1024]{1,0:T(8,128)}) %all-reduce.7.cloned.1.call-update) | async-done | bytes 2097168 | tf_op jit(solution)/shard_map/psum | solution.py:58
  340.3 0.0 copy-done.3
  340.3 6.6 %fusion.15 = f32[512,1792]{1,0:T(8,128)} fusion(bf16[1792,1024]{1,0:T(8,128)(2,1)} %param.10, f32[512,1024]{1,0:T(8,128)} %all-reduce.7.cloned.1.call-done, bf16[512,1024]{1,0:T(8,128)(2,1)S(1)} %copy-done.3), kind=kOutput, calls=%fused_computation.26 | convolution fusion | flops 1880621056 | bytes 10485760 | tf_op jit(solution)/shard_map/dot_general | solution.py:16
  347.0 0.0 all-reduce.9.cloned.1.call-update
  347.0 0.0 reduce-scatter.5.cloned.1.call-start
  347.1 91.0 %all-reduce.9.cloned.1.call-done = (f32[512,1792]{1,0:T(8,128)}, f32[512,1792]{1,0:T(8,128)}) async-done(((f32[512,1792]{1,0:T(8,128)}, f32[512,1792]{1,0:T(8,128)}), (f32[512,1792]{1,0:T(8,128)}, f32[512,1792]{1,0:T(8,128)})) %all-reduce.9.cloned.1.call-update) | async-done | bytes 7340048 | tf_op jit(solution)/shard_map/psum | solution.py:63
  438.0 11.9 %fusion.10 = bf16[1024,1792]{1,0:T(8,128)(2,1)} fusion(bf16[512,1024]{1,0:T(8,128)(2,1)S(1)} %copy-done, f32[512,1792]{1,0:T(8,128)} %get-tuple-element.3, f32[512,1792]{1,0:T(8,128)} %get-tuple-element.2, f32[512,1792]{1,0:T(8,128)} %get-tuple-element.4, f32[512,1792]{1,0:T(8,128)} %get-tuple-element.6, f32[512,1792]{1,0:T(8,128)} %get-tuple-element.5), kind=kOutput, calls=%fused_computation.22 | convolution fusion | flops 1904738304 | bytes 23068672 | tf_op jit(solution)/shard_map/dot_general | solution.py:22
  449.9 0.0 reduce-scatter.5.cloned.1.call-update
  449.9 0.0 reduce-scatter.3.cloned.1.call-start
  450.0 8.6 %fusion.9 = bf16[1024,1792]{1,0:T(8,128)(2,1)} fusion(bf16[512,1024]{1,0:T(8,128)(2,1)S(1)} %copy-done, f32[512,1792]{1,0:T(8,128)} %get-tuple-element.2, f32[512,1792]{1,0:T(8,128)} %get-tuple-element.4, f32[512,1792]{1,0:T(8,128)} %get-tuple-element.5), kind=kOutput, calls=%fused_computation.21 | convolution fusion | flops 1893728256 | bytes 15728640 | tf_op jit(solution)/shard_map/dot_general | solution.py:22
  458.5 0.0 reduce-scatter.3.cloned.1.call-update
  458.5 43.3 %reduce-scatter.5.cloned.1.call-done = bf16[512,1792]{1,0:T(8,128)(2,1)} async-done(((bf16[1024,1792]{1,0:T(8,128)(2,1)}), bf16[512,1792]{1,0:T(8,128)(2,1)}) %reduce-scatter.5.cloned.1.call-update) | async-done | bytes 1835024 | tf_op jit(solution)/shard_map/reduce_scatter | solution.py:73
  501.8 3.8 multiply_convert_fusion.2
  505.6 51.7 %reduce-scatter.3.cloned.1.call-done = bf16[512,1792]{1,0:T(8,128)(2,1)} async-done(((bf16[1024,1792]{1,0:T(8,128)(2,1)}), bf16[512,1792]{1,0:T(8,128)(2,1)}) %reduce-scatter.3.cloned.1.call-update) | async-done | bytes 1835024 | tf_op jit(solution)/shard_map/reduce_scatter | solution.py:70
  (2 shorter events, 0.0 us)
Async XLA Ops:
  7.2 1.2 copy-start
  7.2 147.4 %all-reduce.11.cloned.1.call-start = ((), (), s32[]{:S(2)}) async-start(), calls=%async_computation.6 | async-start | bytes 22020096 | tf_op jit(solution)/shard_map/psum | solution.py:49
  8.4 6.1 %copy-start.1 = (bf16[1024,1792]{1,0:T(8,128)(2,1)S(1)}, bf16[1024,1792]{1,0:T(8,128)(2,1)}, u32[]{:S(2)}) copy-start(bf16[1024,1792]{1,0:T(8,128)(2,1)} %param.8) | copy-start | bytes 11010052
  14.5 3.9 copy-start.2
  22.4 317.9 %all-reduce.7.cloned.1.call-start = ((), (), s32[]{:S(2)}) async-start(), calls=%async_computation.2 | async-start | bytes 4194304 | tf_op jit(solution)/shard_map/psum | solution.py:58
  170.1 267.9 %all-reduce.9.cloned.1.call-start = ((), (), s32[]{:S(2)}) async-start(), calls=%async_computation.5 | async-start | bytes 14680064 | tf_op jit(solution)/shard_map/psum | solution.py:63
  319.1 21.3 %copy-start.3 = (bf16[512,1024]{1,0:T(8,128)(2,1)S(1)}, bf16[512,1024]{1,0:T(8,128)(2,1)}, u32[]{:S(2)}) copy-start(bf16[512,1024]{1,0:T(8,128)(2,1)} %param.7) | copy-start | bytes 3145732
  347.0 154.8 %reduce-scatter.5.cloned.1.call-start = ((), (), s32[]{:S(2)}) async-start(), calls=%async_computation.4 | async-start | bytes 5505024 | tf_op jit(solution)/shard_map/reduce_scatter | solution.py:73
  449.9 107.5 %reduce-scatter.3.cloned.1.call-start = ((), (), s32[]{:S(2)}) async-start(), calls=%async_computation.3 | async-start | bytes 5505024 | tf_op jit(solution)/shard_map/reduce_scatter | solution.py:70
Sparse Core Ops, SparseCore 0:
  22.5 132.0 all-reduce.10
  170.2 170.0 all-reduce.6
  347.1 90.8 all-reduce.8
  450.0 51.7 reduce-scatter.4
  504.7 52.5 reduce-scatter.2
where the time goes:
time: 564 us
  waiting for transfers between devices  333 us (59%)
  blocking collectives  149 us (26%)
  matrix products  62.9 us (11%)
  between operations  13.8 us (2%)
    psum x1, blocking collectives, on_device(): lax.psum((matmul(hidden, down_weight), matmul(hidden_dot, down_weight)),...  149 us
    psum x1, waiting for transfers between devices, on_device(): lax.psum((matmul(tokens, gate_weight), matmul(tokens, up_weight), matmul(...  132 us
    psum x1, waiting for transfers between devices, on_device(): lax.psum((right_trans(resid, down_weight), right_trans(output_dot_b, down...  91 us
    reduce_scatter x1, waiting for transfers between devices, on_device(): lax.psum_scatter(grad_term.astype(jnp.bfloat16), 'dp', scatter_dimension=...  51.7 us
    reduce_scatter x1, waiting for transfers between devices, on_device(): lax.psum_scatter(hess_term.astype(jnp.bfloat16), 'dp', scatter_dimension=...  43.3 us
    dot_general x5, matrix products, matmul(): return jnp.dot(left, right, preferred_element_type=jnp.float32)  29.5 us
    dot_general x2, matrix products, left_trans(): lax.dot_general(left, right, (((0,), (0,)), ((), ())), preferred_element_...  20.4 us
    psum x1, waiting for transfers between devices, on_device(): lax.psum((matmul(hidden, down_weight), matmul(hidden_dot, down_weight)),...  14.9 us
  transfers between devices with their start and end apart: 5, of which 5 were waited for; matrix products, arithmetic and copies ran while one was open for 3% of the time, Pallas kernels for 0%

commit v1 on v0

v1 whole, which is shorter than its diff:
```python
import functools
import math

import jax
import jax.numpy as jnp
from jax import lax
from jax.experimental import pallas as pl
from jax.experimental.pallas import tpu as pltpu
from jax.sharding import Mesh, PartitionSpec as P

D = 8192
TILE = 256
BF = jnp.bfloat16
F32 = jnp.float32
NY = 4
NZ = 4
MIB = 1024 * 1024


def shift(value, axis, step):
    size = lax.axis_size(axis)
    return lax.ppermute(value, axis, [(i, (i + step) % size) for i in range(size)])


def shape(dims, dtype=BF):
    return jax.ShapeDtypeStruct(dims, dtype)


def nbytes(avals):
    return sum(math.prod(a.shape) * a.dtype.itemsize for a in avals)


def call(body, ids, args, outs, scratch=(), flops=0, limit=8, after=()):
    n = len(args)

    def kernel(ids, *refs):
        body(ids, *refs[:n], *refs[n + len(after):])

    cost = pl.CostEstimate(
        flops=flops, bytes_accessed=nbytes(args) + nbytes(outs), transcendentals=0
    )
    vmem = pl.BlockSpec(memory_space=pltpu.VMEM)
    return pl.pallas_call(
        kernel,
        out_shape=tuple(outs),
        in_specs=[pl.BlockSpec(memory_space=pltpu.SMEM)] + [vmem] * n + [pl.BlockSpec(memory_space=pl.ANY)] * len(after),
        out_specs=tuple([vmem] * len(outs)),
        scratch_shapes=list(scratch),
        compiler_params=pltpu.CompilerParams(vmem_limit_bytes=limit * MIB),
        cost_estimate=cost,
        name=body.__qualname__.split(".")[0],
    )(ids, *args, *after)


def loop_tiles(size, tile, body):
    def step(j, carry):
        body(pl.ds(pl.multiple_of(j * tile, tile), tile))
        return carry

    lax.fori_loop(0, size // tile, step, 0)


def token_row(ids, core_rel, y_rel, rows):
    core = lax.rem(ids[2] + core_rel, 2)
    y = lax.rem(ids[1] + y_rel, NY)
    return pl.multiple_of((core * NY + y) * rows, rows)


def ordered_tokens(ids, rows, tokens):
    width = tokens.shape[1]

    def body(ids, t_ref, o_ref):
        for c in range(2):
            for y in range(NY):
                at = (c * NY + y) * rows
                o_ref[at:at + rows, :] = t_ref[pl.ds(token_row(ids, c, y, rows), rows), :]

    return call(body, ids, (tokens,), [shape((8 * rows, width))])[0]


def pre_products(ids, rows, ordered, weight):
    width, cols = weight.shape

    def body(ids, t_ref, w_ref, own_ref, other_ref):
        def step(at):
            acc = jnp.dot(t_ref[...], w_ref[:, at], preferred_element_type=F32).astype(BF)
            acc = acc.reshape(2, NY, rows, TILE)
            own_ref[:, :, at] = acc[0]
            other_ref[:, :, at] = acc[1]

        loop_tiles(cols, TILE, step)

    out = shape((NY, rows, cols))
    return call(
        body, ids, (ordered, weight), [out, out], flops=2 * 8 * rows * width * cols
    )


def split_pre(ids, owns, recvs):
    n = len(owns)
    _, rows, cols = owns[0].shape
    half = rows // 2

    def body(ids, *refs):
        a_refs, b_refs = refs[:n], refs[n:2 * n]
        o0, o1l, o1h, o2l, o2h, o3l, o3h = refs[2 * n:]

        def step(at):
            for i in range(n):
                o0[i, :, at] = a_refs[i][0, :, at].astype(F32) + b_refs[i][0, :, at].astype(F32)
                for y, l_ref, h_ref in ((1, o1l, o1h), (2, o2l, o2h), (3, o3l, o3h)):
                    total = a_refs[i][y, :, at].astype(F32) + b_refs[i][y, :, at].astype(F32)
                    l_ref[i, :, at] = total[:half].astype(BF)
                    h_ref[i, :, at] = total[half:].astype(BF)

        loop_tiles(cols, TILE, step)

    outs = [shape((n, rows, cols), F32)] + [shape((n, half, cols))] * 6
    return call(body, ids, (*owns, *recvs), outs)


def add_pair(a, b):
    return (a.astype(F32) + b.astype(F32)).astype(BF)


def ring_scatter(blocks):
    own, b1l, b1h, b2l, b2h, b3l, b3h = blocks
    relay_low = shift(b2l, "y", 1)
    relay_high = shift(b2h, "y", -1)
    direct_high = shift(b1h, "y", 1)
    direct_low = shift(b3l, "y", -1)
    both_low = shift(add_pair(b1l, relay_low), "y", 1)
    both_high = shift(add_pair(b3h, relay_high), "y", -1)
    return own, (both_low, direct_low), (both_high, direct_high)


def coefficients(ids, own, lows, highs):
    n, rows, cols = own.shape
    half = rows // 2
    inv_width = 1.0 / math.sqrt(D)

    def body(ids, own_ref, l0, l1, h0, h1, low_ref, high_ref, first_ref, second_ref):
        def step(at):
            for start, a, b, pay_ref in ((0, l0, l1, low_ref), (half, h0, h1, high_ref)):
                to = slice(start, start + half)
                gate, up, tangent = (
                    own_ref[i, to, at] + a[i, :, at].astype(F32) + b[i, :, at].astype(F32)
                    for i in range(3)
                )
                tangent = tangent * inv_width
                sig = jax.nn.sigmoid(gate)
                first = sig * (1.0 + gate * (1.0 - sig)) * up
                second = sig * (1.0 - sig) * (2.0 + gate * (1.0 - 2.0 * sig)) * (tangent * up)
                pay_ref[0, :, at] = (gate * sig * up).astype(BF)
                pay_ref[1, :, at] = (first * tangent).astype(BF)
                first_ref[to, at] = first.astype(BF)
                second_ref[to, at] = second.astype(BF)

        loop_tiles(cols, TILE, step)

    pay = shape((2, half, cols))
    outs = [pay, pay, shape((rows, cols)), shape((rows, cols))]
    return call(body, ids, (own, *lows, *highs), outs)


def gather_y(value):
    return [value, shift(value, "y", -1), shift(value, "y", -2), shift(value, "y", -3)]


def swap_cores(values):
    return [shift(v, "core", 1) for v in values]


def ring_pair(near, far):
    near_low, near_high = shift(near, "y", 1), shift(near, "y", -1)
    far_low, far_high = shift(far, "y", 1), shift(far, "y", -1)
    across = shift(near_low, "y", 1), shift(far_high, "y", -1)
    return [near, far, near_high, far_high, *across, near_low, far_low]


def down_products(ids, pieces, down):
    _, rows, cols = pieces[0].shape
    width = down.shape[1]
    tile = width // NZ
    total = 8 * 2 * rows

    def body(ids, *refs):
        p_refs, d_ref, o_refs, lhs = refs[:8], refs[8], refs[9:13], refs[13]
        for i, p_ref in enumerate(p_refs):
            lhs[2 * rows * i:2 * rows * (i + 1), :] = p_ref[...].reshape(2 * rows, cols)

        def step(k, carry):
            at = pl.multiple_of(lax.rem(ids[3] + k, NZ) * tile, tile)
            acc = jnp.dot(
                lhs[...], d_ref[:, pl.ds(at, tile)], preferred_element_type=F32
            ).astype(BF)
            for i, o_ref in enumerate(o_refs):
                @pl.when(k == i)
                def _(o_ref=o_ref):
                    o_ref[...] = acc
            return carry

        lax.fori_loop(0, NZ, step, 0)

    outs = [shape((total, tile))] * NZ
    return call(
        body, ids, (*pieces, down), outs, [pltpu.VMEM((total, cols), BF)],
        flops=2 * total * width * cols, limit=12)


def spread(axis, blocks):
    first, *rest = blocks
    return [first] + [shift(v, axis, k + 1) for k, v in enumerate(rest)]


def sum_z(ids, parts):
    def body(ids, a, b, c, d, o_ref):
        total = a[...].astype(F32) + b[...].astype(F32) + c[...].astype(F32) + d[...].astype(F32)
        o_ref[...] = total.astype(BF)

    return call(body, ids, parts, [shape(parts[0].shape)])[0]


def residual(ids, chunk, rows, own, recv, target):
    total, cols = own.shape

    def body(ids, own_ref, recv_ref, t_ref, o_ref):
        column = pl.multiple_of(ids[3] * cols, cols)
        for c in range(2):
            for y in range(NY):
                at = (c * NY + y) * 2 * rows
                to = slice(at, at + 2 * rows)
                value = own_ref[to].astype(F32) + recv_ref[to].astype(F32)
                row = pl.multiple_of(token_row(ids, c, y, 2 * rows) + chunk * rows, rows)
                goal = t_ref[pl.ds(row, rows), pl.ds(column, cols)]
                o_ref[at:at + rows] = (value[:rows] - goal.astype(F32)).astype(BF)
                o_ref[at + rows:at + 2 * rows] = value[rows:].astype(BF)

    return call(body, ids, (own, recv, target), [shape((total, cols))])[0]


def back_products(ids, parts, down, rows, after=()):
    total, tile_k = parts[0].shape
    cols, width = down.shape

    def body(ids, *refs):
        f_refs, d_ref, own_ref, other_ref = refs[:NZ], refs[NZ], refs[NZ + 1], refs[NZ + 2]

        def step(at):
            acc = jnp.zeros((total, TILE), F32)
            for k, f_ref in enumerate(f_refs):
                to = pl.multiple_of(lax.rem(ids[3] + k, NZ) * tile_k, tile_k)
                acc += lax.dot_general(
                    f_ref[...], d_ref[at, pl.ds(to, tile_k)], (((1,), (1,)), ((), ())),
                    preferred_element_type=F32,
                )
            acc = acc.astype(BF).reshape(2, NY, 2, rows, TILE)
            own_ref[:, :, :, at] = acc[0]
            other_ref[:, :, :, at] = acc[1]

        loop_tiles(cols, TILE, step)

    out = shape((NY, 2, rows, cols))
    return call(
        body, ids, (*parts, down), [out, out], flops=2 * total * width * cols, limit=12, after=after)


def split_back(ids, own, recv):
    _, n, rows, cols = own.shape

    def body(ids, a_ref, b_ref, *outs):
        def step(at):
            for i in range(n):
                for y in range(NY):
                    total = a_ref[y, i, :, at].astype(F32) + b_ref[y, i, :, at].astype(F32)
                    outs[y][i, :, at] = total.astype(outs[y].dtype)

        loop_tiles(cols, TILE, step)

    outs = [shape((n, rows, cols), F32)] + [shape((n, rows, cols))] * 3
    return call(body, ids, (own, recv), outs)


def sum_at(refs, i, at):
    total = refs[0][i, :, at].astype(F32)
    for ref in refs[1:]:
        total += ref[i, :, at].astype(F32)
    return total


def errors(ids, chunk, terms, first, second, before=()):
    n, rows, cols = terms[0].shape

    def body(ids, *refs):
        (f_ref, s_ref), done, o_ref = refs[len(terms):len(terms) + 2], refs[len(terms) + 2:-1], refs[-1]
        mine = slice(chunk * rows, (chunk + 1) * rows)

        def step(at):
            back, back_dot = (sum_at(refs[:len(terms)], i, at) for i in range(2))
            f = f_ref[mine, at].astype(F32)
            o_ref[0, mine, at] = (back * f).astype(BF)
            o_ref[1, mine, at] = (back * s_ref[mine, at].astype(F32) + back_dot * f).astype(BF)
            for ref in done:
                o_ref[:, :chunk * rows, at] = ref[:, :, at]

        loop_tiles(cols, TILE, step)

    out = shape((n, (chunk + 1) * rows, cols))
    return call(body, ids, (*terms, first, second, *before), [out])[0]


def transposed_tokens(ids, tokens, other, rows):
    count, width = tokens.shape
    half = other.shape[1]

    def body(ids, t_ref, x_ref, o_ref, held):
        cols = pl.ds(pl.multiple_of(ids[0] * half, half), half)
        at = 0
        for c in range(2):
            for y in range(NY):
                row = pl.ds(token_row(ids, c, y, rows), rows)
                held[at:at + rows, :] = t_ref[row, cols]
                held[at + rows:at + 2 * rows, :] = x_ref[row, :]
                at += 2 * rows
        o_ref[...] = held[...].T

    return call(
        body, ids, (tokens, other), [shape((half, 2 * count))],
        [pltpu.VMEM((2 * count, half), BF)],
    )[0]


def outer_products(ids, lhs, pieces, probe):
    out_rows, count = lhs.shape
    _, rows, cols = pieces[0].shape
    token_scale = 1.0 / math.sqrt(count)
    inv_width = 1.0 / math.sqrt(D)
    n = len(pieces)

    def body(ids, l_ref, *refs):
        p_refs, probe_ref, g_ref, h_ref = refs[:n], refs[n], refs[n + 1], refs[n + 2]
        probe_rows = pl.ds(pl.multiple_of(ids[0] * out_rows, out_rows), out_rows)

        def step(at):
            err = jnp.concatenate([p[0, :, at] for p in p_refs], axis=0)
            g = jnp.dot(l_ref[...], err, preferred_element_type=F32) * token_scale
            g_ref[:, at] = g.astype(BF)
            err = jnp.concatenate([p[1, :, at] for p in p_refs], axis=0)
            hv = jnp.dot(l_ref[...], err, preferred_element_type=F32) * token_scale
            h_ref[:, at] = (probe_ref[probe_rows, at].astype(F32) * hv * inv_width).astype(BF)

        loop_tiles(cols, TILE, step)

    out = shape((out_rows, cols))
    return call(
        body, ids, (lhs, *pieces, probe), [out, out],
        flops=4 * out_rows * count * cols, limit=12,
    )


def on_device(tokens, target, gate_weight, up_weight, down_weight, probe_sign):
    ids = jnp.stack([lax.axis_index(a) for a in ("dp", "y", "core", "z", "xh")]).astype(jnp.int32)
    count, width = tokens.shape
    rows = count // 8
    half = width // 2
    other_cols = lax.dynamic_slice_in_dim(tokens, (1 - ids[0]) * half, half, 1)
    other_tokens = shift(other_cols, "dp", 1)
    lhs = transposed_tokens(ids, tokens, other_tokens, rows)
    ordered = ordered_tokens(ids, rows, tokens)
    pairs = [pre_products(ids, rows, ordered, w) for w in (gate_weight, up_weight, probe_sign)]
    recvs = swap_cores([other for _, other in pairs])
    own, lows, highs = ring_scatter(split_pre(ids, [own for own, _ in pairs], recvs))
    *pays, first, second = coefficients(ids, own, lows, highs)
    done = ()
    for c, pay in enumerate(pays):
        near = gather_y(pay)
        parts = spread("z", down_products(ids, near + swap_cores(near), down_weight))
        part = sum_z(ids, parts)
        err = residual(ids, c, rows // 2, part, shift(part, "xh", 1), target)
        parts = [err] + [shift(err, "z", -k) for k in range(1, NZ)]
        own, other = back_products(ids, parts, down_weight, rows // 2, () if c else (lhs,))
        terms = spread("y", split_back(ids, own, shift(other, "core", 1)))
        done = (errors(ids, c, terms, first, second, done),)
    near = ring_pair(done[0], shift(done[0], "dp", 1))
    return outer_products(ids, lhs, near + swap_cores(near), probe_sign)


def solution(mesh):
    fine = Mesh(mesh.devices.reshape(2, 4, 2, 4, 2), ("dp", "y", "core", "z", "xh"))
    width, hidden = ("y", "core"), ("z", "xh")
    return jax.shard_map(
        on_device,
        mesh=fine,
        in_specs=(
            P("dp", width),
            P("dp", width),
            P(width, hidden),
            P(width, hidden),
            P(hidden, width),
            P(width, hidden),
        ),
        out_specs=(P(("y", "core", "dp"), hidden), P(("y", "core", "dp"), hidden)),
        check_vma=False,
    )
```

time: 564 us -> 220 us (0.39)
  waiting for transfers between devices: 333 us -> 83.8 us
  blocking collectives: 149 us -> 0 us
  starting transfers between devices: 0.21 us -> 84.1 us
  matrix products: 62.9 us -> 0 us
  Pallas kernels: 0 us -> 43.1 us
  between operations: 13.8 us -> 0.93 us
  local copies, waits for them, and re-layouts: 1.19 us -> 7.22 us
    psum x3 -> x0, waiting for transfers between devices: 238 us -> none  [the longest x1 132 us: on_device(): lax.psum((matmul(tokens, gate_weight), matmul(tokens, up_weight), matmul(...]
    psum x1 -> x0, blocking collectives: 149 us -> none  [on_device(): lax.psum((matmul(hidden, down_weight), matmul(hidden_dot, down_weight)),...]
    reduce_scatter x2 -> x0, waiting for transfers between devices: 95 us -> none  [the longest x1 51.7 us: on_device(): lax.psum_scatter(grad_term.astype(jnp.bfloat16), 'dp', scatter_dimension=...]
    ppermute x0 -> x61, starting transfers between devices: none -> 84.1 us  [shift(): lax.ppermute(value, axis, [(i, (i + step) % size) for i in range(size)])]
    ppermute x0 -> x61, waiting for transfers between devices: none -> 83.8 us  [shift(): lax.ppermute(value, axis, [(i, (i + step) % size) for i in range(size)])]
    dot_general x9 -> x0, matrix products: 62.9 us -> none  [the longest x5 29.5 us: matmul(): return jnp.dot(left, right, preferred_element_type=jnp.float32)]
    pallas_call x0 -> x20, Pallas kernels: none -> 43.1 us  [call(): pl.pallas_call(kernel, out_shape=tuple(outs), in_specs=[pl.BlockSpec(memo...]
    unnamed x8 -> x24, local copies, waits for them, and re-layouts: 1.19 us -> 7.1 us
  transfers between devices with their start and end apart: 5 -> 61, of which waited for: 5 -> 26; matrix products, arithmetic and copies ran while one was open for 3% -> 0% of each run, Pallas kernels for 0% -> 13%
where the time goes in v1:
time: 220 us; the launch traced here: 219 us
  starting transfers between devices  84.1 us (38%)
  waiting for transfers between devices  83.8 us (38%)
  Pallas kernels  43.1 us (20%)
  local copies, waits for them, and re-layouts  7.22 us (3%)
    ppermute x61, starting transfers between devices, shift(): lax.ppermute(value, axis, [(i, (i + step) % size) for i in range(size)])  84.1 us
    ppermute x61, waiting for transfers between devices, shift(): lax.ppermute(value, axis, [(i, (i + step) % size) for i in range(size)])  83.8 us
    pallas_call x20, Pallas kernels, call(): pl.pallas_call(kernel, out_shape=tuple(outs), in_specs=[pl.BlockSpec(memo...  43.1 us
    unnamed x24, local copies, waits for them, and re-layouts  7.1 us
  transfers between devices with their start and end apart: 61, of which 26 were waited for; matrix products, arithmetic and copies ran while one was open for 0% of the time, Pallas kernels for 13%

profile of v1, /device:TPU:1, one launch (start us, length us, event | category | flops | bytes accessed | tf_op | source)
XLA Modules:
  0.0 219.3 jit_solution(12675566527338794542)
XLA Ops:
  4.6 3.6 %pre_products.5 = (bf16[4,64,1792]{2,1,0:T(8,128)(2,1)S(1)}, bf16[4,64,1792]{2,1,0:T(8,128)(2,1)S(1)}) custom-call(s32[5]{0:T(128)S(1)} %stack.23.ids, bf16[512,1024]{1,0:T(8,128)(2,1)S(1)} %ordered_tokens.1.refs_0_, bf16[1024,1792]{1,0:T(8,128)(2,1)S(1)} %copy-done.8), custom_call_target="tpu_custom_call" | custom-call | flops 1879048192 | bytes 6553600 | tf_op jit(solution)/shard_map/pre_products/pallas_call | solution.py:43
  9.8 3.6 %pre_products.3 = (bf16[4,64,1792]{2,1,0:T(8,128)(2,1)S(1)}, bf16[4,64,1792]{2,1,0:T(8,128)(2,1)S(1)}) custom-call(s32[5]{0:T(128)S(1)} %stack.23.ids, bf16[512,1024]{1,0:T(8,128)(2,1)S(1)} %ordered_tokens.1.refs_0_, bf16[1024,1792]{1,0:T(8,128)(2,1)S(1)} %copy-done.3), custom_call_target="tpu_custom_call" | custom-call | flops 1879048192 | bytes 6553600 | tf_op jit(solution)/shard_map/pre_products/pallas_call | solution.py:43
  13.5 3.6 %pre_products.4 = (bf16[4,64,1792]{2,1,0:T(8,128)(2,1)S(1)}, bf16[4,64,1792]{2,1,0:T(8,128)(2,1)S(1)}) custom-call(s32[5]{0:T(128)S(1)} %stack.23.ids, bf16[512,1024]{1,0:T(8,128)(2,1)S(1)} %ordered_tokens.1.refs_0_, bf16[1024,1792]{1,0:T(8,128)(2,1)S(1)} %copy-done.4), custom_call_target="tpu_custom_call" | custom-call | flops 1879048192 | bytes 6553600 | tf_op jit(solution)/shard_map/pre_products/pallas_call | solution.py:43
  25.5 6.4 %collective-permute-done.4 = bf16[3,32,1792]{2,1,0:T(8,128)(2,1)S(1)} collective-permute-done((bf16[3,32,1792]{2,1,0:T(8,128)(2,1)S(1)}, bf16[3,32,1792]{2,1,0:T(8,128)(2,1)S(1)}, u32[]{:S(2)}, u32[]{:S(2)}) %collective-permute-start.4) | collective-permute-done | bytes 344096 | tf_op jit(solution)/shard_map/ppermute | solution.py:22
  32.1 6.7 %collective-permute-done.7 = bf16[3,32,1792]{2,1,0:T(8,128)(2,1)S(1)} collective-permute-done((bf16[3,32,1792]{2,1,0:T(8,128)(2,1)S(1)}, bf16[3,32,1792]{2,1,0:T(8,128)(2,1)S(1)}, u32[]{:S(2)}, u32[]{:S(2)}) %collective-permute-start.7) | collective-permute-done | bytes 344096 | tf_op jit(solution)/shard_map/ppermute | solution.py:22
  38.9 3.1 %collective-permute-start.8 = (bf16[3,32,1792]{2,1,0:T(8,128)(2,1)S(1)}, bf16[3,32,1792]{2,1,0:T(8,128)(2,1)S(1)}, u32[]{:S(2)}, u32[]{:S(2)}) collective-permute-start(bf16[3,32,1792]{2,1,0:T(8,128)(2,1)S(1)} %add_convert_fusion), channel_id=1, source_target_pairs={{0,48},{16,0},{32,16},{48,32},{1,49},{17,1},{33,17},{49,33},{2,50}... | collective-permute-start | bytes 1032200 | tf_op jit(solution)/shard_map/ppermute | solution.py:22
  42.0 4.7 %collective-permute-done.5.refs_1_ = bf16[3,32,1792]{2,1,0:T(8,128)(2,1)S(1)} collective-permute-done((bf16[3,32,1792]{2,1,0:T(8,128)(2,1)S(1)}, bf16[3,32,1792]{2,1,0:T(8,128)(2,1)S(1)}, u32[]{:S(2)}, u32[]{:S(2)}) %collective-permute-start.5) | collective-permute-done | bytes 344096 | tf_op jit(solution)/shard_map/ppermute | solution.py:22
  49.5 4.3 %collective-permute-start.11 = (bf16[2,32,1792]{2,1,0:T(8,128)(2,1)S(1)}, bf16[2,32,1792]{2,1,0:T(8,128)(2,1)S(1)}, u32[]{:S(2)}, u32[]{:S(2)}) collective-permute-start(bf16[2,32,1792]{2,1,0:T(8,128)(2,1)S(1)} %get-tuple-element.52.refs_0_), channel_id=1, source_target_pairs={{0,32},{16,48},{32,0},{48,16},{1,33},{17,49},{33,1},{49,17},{2,34}... | collective-permute-start | bytes 688136 | tf_op jit(solution)/shard_map/ppermute | solution.py:22
  57.5 4.4 %collective-permute-done.11.refs_2_ = bf16[2,32,1792]{2,1,0:T(8,128)(2,1)S(1)} collective-permute-done((bf16[2,32,1792]{2,1,0:T(8,128)(2,1)S(1)}, bf16[2,32,1792]{2,1,0:T(8,128)(2,1)S(1)}, u32[]{:S(2)}, u32[]{:S(2)}) %collective-permute-start.11) | collective-permute-done | bytes 229408 | tf_op jit(solution)/shard_map/ppermute | solution.py:22
  61.9 6.2 %collective-permute-start.31 = (bf16[2,32,1792]{2,1,0:T(8,128)(2,1)S(1)}, bf16[2,32,1792]{2,1,0:T(8,128)(2,1)S(1)}, u32[]{:S(2)}, u32[]{:S(2)}) collective-permute-start(bf16[2,32,1792]{2,1,0:T(8,128)(2,1)S(1)} %get-tuple-element.65.refs_0_), channel_id=1, source_target_pairs={{0,8},{8,0},{1,9},{9,1},{2,10},{10,2},{3,11},{11,3},{4,12},{12,4},... | collective-permute-start | bytes 688136 | tf_op jit(solution)/shard_map/ppermute | solution.py:22
  71.8 3.4 %collective-permute-start.33 = (bf16[2,32,1792]{2,1,0:T(8,128)(2,1)S(1)}, bf16[2,32,1792]{2,1,0:T(8,128)(2,1)S(1)}, u32[]{:S(2)}, u32[]{:S(2)}) collective-permute-start(bf16[2,32,1792]{2,1,0:T(8,128)(2,1)S(1)} %collective-permute-done.29.refs_2_), channel_id=1, source_target_pairs={{0,8},{8,0},{1,9},{9,1},{2,10},{10,2},{3,11},{11,3},{4,12},{12,4},... | collective-permute-start | bytes 688136 | tf_op jit(solution)/shard_map/ppermute | solution.py:22
  76.7 3.4 %down_products.3 = (bf16[512,256]{1,0:T(8,128)(2,1)S(1)}, bf16[512,256]{1,0:T(8,128)(2,1)S(1)}, bf16[512,256]{1,0:T(8,128)(2,1)S(1)}, bf16[512,256]{1,0:T(8,128)(2,1)S(1)}) custom-call(s32[5]{0:T(128)S(1)} %stack.23.ids, bf16[2,32,1792]{2,1,0:T(8,128)(2,1)S(1)} %get-tuple-element.65.refs_0_, bf16[2,32,1792]{2,1,0:T(8,128)(2,1)S(1)} %collective-permute-done.28.refs_1_, ...), custom_call_target="tpu_custom_call" | custom-call | flops 1879048192 | bytes 6553600 | tf_op jit(solution)/shard_map/down_products/pallas_call | solution.py:43
  81.6 3.3 %collective-permute-start.36 = (bf16[512,256]{1,0:T(8,128)(2,1)S(1)}, bf16[512,256]{1,0:T(8,128)(2,1)S(1)}, u32[]{:S(2)}, u32[]{:S(2)}) collective-permute-start(bf16[512,256]{1,0:T(8,128)(2,1)S(1)} %get-tuple-element.68), channel_id=1, source_target_pairs={{0,4},{2,6},{4,0},{6,2},{1,5},{3,7},{5,1},{7,3},{8,12},{10,14},{12... | collective-permute-start | bytes 786440 | tf_op jit(solution)/shard_map/ppermute | solution.py:22
  89.5 3.9 %down_products.2 = (bf16[512,256]{1,0:T(8,128)(2,1)S(1)}, bf16[512,256]{1,0:T(8,128)(2,1)S(1)}, bf16[512,256]{1,0:T(8,128)(2,1)S(1)}, bf16[512,256]{1,0:T(8,128)(2,1)S(1)}) custom-call(s32[5]{0:T(128)S(1)} %stack.23.ids, bf16[2,32,1792]{2,1,0:T(8,128)(2,1)S(1)} %get-tuple-element.52.refs_0_, bf16[2,32,1792]{2,1,0:T(8,128)(2,1)S(1)} %collective-permute-done.10.refs_1_, ...), custom_call_target="tpu_custom_call" | custom-call | flops 1879048192 | bytes 6553600 | tf_op jit(solution)/shard_map/down_products/pallas_call | solution.py:43
  97.6 2.8 %collective-permute-start.38 = (bf16[512,256]{1,0:T(8,128)(2,1)S(1)}, bf16[512,256]{1,0:T(8,128)(2,1)S(1)}, u32[]{:S(2)}, u32[]{:S(2)}) collective-permute-start(bf16[512,256]{1,0:T(8,128)(2,1)S(1)} %sum_z.3.refs_0_), channel_id=1, source_target_pairs={{0,1},{1,0},{2,3},{3,2},{4,5},{5,4},{6,7},{7,6},{8,9},{9,8},{10,11... | collective-permute-start | bytes 786440 | tf_op jit(solution)/shard_map/ppermute | solution.py:22
  102.1 5.8 %collective-permute-done.18.refs_2_ = bf16[512,256]{1,0:T(8,128)(2,1)S(1)} collective-permute-done((bf16[512,256]{1,0:T(8,128)(2,1)S(1)}, bf16[512,256]{1,0:T(8,128)(2,1)S(1)}, u32[]{:S(2)}, u32[]{:S(2)}) %collective-permute-start.18) | collective-permute-done | bytes 262176 | tf_op jit(solution)/shard_map/ppermute | solution.py:22
  108.8 2.9 %collective-permute-start.20 = (bf16[512,256]{1,0:T(8,128)(2,1)S(1)}, bf16[512,256]{1,0:T(8,128)(2,1)S(1)}, u32[]{:S(2)}, u32[]{:S(2)}) collective-permute-start(bf16[512,256]{1,0:T(8,128)(2,1)S(1)} %sum_z.2.refs_0_), channel_id=1, source_target_pairs={{0,1},{1,0},{2,3},{3,2},{4,5},{5,4},{6,7},{7,6},{8,9},{9,8},{10,11... | collective-permute-start | bytes 786440 | tf_op jit(solution)/shard_map/ppermute | solution.py:22
  114.1 2.8 %collective-permute-start.40 = (bf16[512,256]{1,0:T(8,128)(2,1)S(1)}, bf16[512,256]{1,0:T(8,128)(2,1)S(1)}, u32[]{:S(2)}, u32[]{:S(2)}) collective-permute-start(bf16[512,256]{1,0:T(8,128)(2,1)S(1)} %residual.3.refs_0_), channel_id=1, source_target_pairs={{0,4},{2,6},{4,0},{6,2},{1,5},{3,7},{5,1},{7,3},{8,12},{10,14},{12... | collective-permute-start | bytes 786440 | tf_op jit(solution)/shard_map/ppermute | solution.py:22
  117.0 5.1 %collective-permute-done.20.refs_1_ = bf16[512,256]{1,0:T(8,128)(2,1)S(1)} collective-permute-done((bf16[512,256]{1,0:T(8,128)(2,1)S(1)}, bf16[512,256]{1,0:T(8,128)(2,1)S(1)}, u32[]{:S(2)}, u32[]{:S(2)}) %collective-permute-start.20) | collective-permute-done | bytes 262176 | tf_op jit(solution)/shard_map/ppermute | solution.py:22
  122.7 3.0 %collective-permute-start.23 = (bf16[512,256]{1,0:T(8,128)(2,1)S(1)}, bf16[512,256]{1,0:T(8,128)(2,1)S(1)}, u32[]{:S(2)}, u32[]{:S(2)}) collective-permute-start(bf16[512,256]{1,0:T(8,128)(2,1)S(1)} %residual.2.refs_0_), channel_id=1, source_target_pairs={{0,2},{2,4},{4,6},{6,0},{1,3},{3,5},{5,7},{7,1},{8,10},{10,12},{12... | collective-permute-start | bytes 786440 | tf_op jit(solution)/shard_map/ppermute | solution.py:22
  129.2 4.0 %back_products.3 = (bf16[4,2,32,1792]{3,2,1,0:T(8,128)(2,1)S(1)}, bf16[4,2,32,1792]{3,2,1,0:T(8,128)(2,1)S(1)}) custom-call(s32[5]{0:T(128)S(1)} %stack.23.ids, bf16[512,256]{1,0:T(8,128)(2,1)S(1)} %residual.3.refs_0_, bf16[512,256]{1,0:T(8,128)(2,1)S(1)} %collective-permute-done.39.refs_1_, bf16[512,256]{1,0:T(8,128)(2,1)S(1)} %collective-permute-done.40.refs_2_, ...), custom_call_target="tpu_custom_call" | custom-call | flops 1879048192 | bytes 6553600 | tf_op jit(solution)/shard_map/back_products/pallas_call | solution.py:43
  135.2 4.2 %collective-permute-done.22.refs_2_ = bf16[512,256]{1,0:T(8,128)(2,1)S(1)} collective-permute-done((bf16[512,256]{1,0:T(8,128)(2,1)S(1)}, bf16[512,256]{1,0:T(8,128)(2,1)S(1)}, u32[]{:S(2)}, u32[]{:S(2)}) %collective-permute-start.22) | collective-permute-done | bytes 262176 | tf_op jit(solution)/shard_map/ppermute | solution.py:22
  139.4 4.0 %back_products.2 = (bf16[4,2,32,1792]{3,2,1,0:T(8,128)(2,1)S(1)}, bf16[4,2,32,1792]{3,2,1,0:T(8,128)(2,1)S(1)}) custom-call(s32[5]{0:T(128)S(1)} %stack.23.ids, bf16[512,256]{1,0:T(8,128)(2,1)S(1)} %residual.2.refs_0_, bf16[512,256]{1,0:T(8,128)(2,1)S(1)} %collective-permute-done.21.refs_1_, bf16[512,256]{1,0:T(8,128)(2,1)S(1)} %collective-permute-done.22.refs_2_, ...), custom_call_target="tpu_custom_call" | custom-call | flops 1879048192 | bytes 6553600 | tf_op jit(solution)/shard_map/back_products/pallas_call | solution.py:43
  154.6 4.5 %collective-permute-done.44.refs_2_ = bf16[2,32,1792]{2,1,0:T(8,128)(2,1)S(1)} collective-permute-done((bf16[2,32,1792]{2,1,0:T(8,128)(2,1)S(1)}, bf16[2,32,1792]{2,1,0:T(8,128)(2,1)S(1)}, u32[]{:S(2)}, u32[]{:S(2)}) %collective-permute-start.44) | collective-permute-done | bytes 229408 | tf_op jit(solution)/shard_map/ppermute | solution.py:22
  160.4 4.1 %collective-permute-done.25.refs_1_ = bf16[2,32,1792]{2,1,0:T(8,128)(2,1)S(1)} collective-permute-done((bf16[2,32,1792]{2,1,0:T(8,128)(2,1)S(1)}, bf16[2,32,1792]{2,1,0:T(8,128)(2,1)S(1)}, u32[]{:S(2)}, u32[]{:S(2)}) %collective-permute-start.25) | collective-permute-done | bytes 229408 | tf_op jit(solution)/shard_map/ppermute | solution.py:22
  164.4 4.6 %collective-permute-done.26.refs_2_ = bf16[2,32,1792]{2,1,0:T(8,128)(2,1)S(1)} collective-permute-done((bf16[2,32,1792]{2,1,0:T(8,128)(2,1)S(1)}, bf16[2,32,1792]{2,1,0:T(8,128)(2,1)S(1)}, u32[]{:S(2)}, u32[]{:S(2)}) %collective-permute-start.26) | collective-permute-done | bytes 229408 | tf_op jit(solution)/shard_map/ppermute | solution.py:22
  175.5 5.7 %collective-permute-done.46.refs_2_ = bf16[2,64,1792]{2,1,0:T(8,128)(2,1)S(1)} collective-permute-done((bf16[2,64,1792]{2,1,0:T(8,128)(2,1)S(1)}, bf16[2,64,1792]{2,1,0:T(8,128)(2,1)S(1)}, u32[]{:S(2)}, u32[]{:S(2)}) %collective-permute-start.46) | collective-permute-done | bytes 458784 | tf_op jit(solution)/shard_map/ppermute | solution.py:22
  185.9 5.8 %collective-permute-done.48.refs_4_ = bf16[2,64,1792]{2,1,0:T(8,128)(2,1)S(1)} collective-permute-done((bf16[2,64,1792]{2,1,0:T(8,128)(2,1)S(1)}, bf16[2,64,1792]{2,1,0:T(8,128)(2,1)S(1)}, u32[]{:S(2)}, u32[]{:S(2)}) %collective-permute-start.48) | collective-permute-done | bytes 458784 | tf_op jit(solution)/shard_map/ppermute | solution.py:22
  191.7 3.4 %collective-permute-start.51 = (bf16[2,64,1792]{2,1,0:T(8,128)(2,1)S(1)}, bf16[2,64,1792]{2,1,0:T(8,128)(2,1)S(1)}, u32[]{:S(2)}, u32[]{:S(2)}) collective-permute-start(bf16[2,64,1792]{2,1,0:T(8,128)(2,1)S(1)} %collective-permute-done.48.refs_4_), channel_id=1, source_target_pairs={{0,48},{16,0},{32,16},{48,32},{1,49},{17,1},{33,17},{49,33},{2,50}... | collective-permute-start | bytes 1376264 | tf_op jit(solution)/shard_map/ppermute | solution.py:22
  195.1 3.0 %collective-permute-start.54 = (bf16[2,64,1792]{2,1,0:T(8,128)(2,1)S(1)}, bf16[2,64,1792]{2,1,0:T(8,128)(2,1)S(1)}, u32[]{:S(2)}, u32[]{:S(2)}) collective-permute-start(bf16[2,64,1792]{2,1,0:T(8,128)(2,1)S(1)} %collective-permute-done.46.refs_2_), channel_id=1, source_target_pairs={{0,8},{8,0},{1,9},{9,1},{2,10},{10,2},{3,11},{11,3},{4,12},{12,4},... | collective-permute-start | bytes 1376264 | tf_op jit(solution)/shard_map/ppermute | solution.py:22
  200.3 8.7 %collective-permute-done.52.refs_8_ = bf16[2,64,1792]{2,1,0:T(8,128)(2,1)S(1)} collective-permute-done((bf16[2,64,1792]{2,1,0:T(8,128)(2,1)S(1)}, bf16[2,64,1792]{2,1,0:T(8,128)(2,1)S(1)}, u32[]{:S(2)}, u32[]{:S(2)}) %collective-permute-start.52) | collective-permute-done | bytes 458784 | tf_op jit(solution)/shard_map/ppermute | solution.py:22
  211.9 7.4 %outer_products.1 = (bf16[512,1792]{1,0:T(8,128)(2,1)}, bf16[512,1792]{1,0:T(8,128)(2,1)}) custom-call(s32[5]{0:T(128)S(1)} %stack.23.ids, bf16[512,1024]{1,0:T(8,128)(2,1)S(1)} %transposed_tokens.1.refs_5_.refs_0_, bf16[2,64,1792]{2,1,0:T(8,128)(2,1)S(1)} %errors.3.refs_1_, bf16[2,64,1792]{2,1,0:T(8,128)(2,1)S(1)} %collective-permute-done.46.refs_2_, ...), custom_call_target="tpu_custom_call" | custom-call | flops 3758096384 | bytes 15728640 | tf_op jit(solution)/shard_map/outer_products/pallas_call | solution.py:43
  (138 shorter events, 75.7 us)
Async XLA Ops:
  22.5 19.5 %collective-permute-start.6 = (bf16[3,32,1792]{2,1,0:T(8,128)(2,1)S(1)}, bf16[3,32,1792]{2,1,0:T(8,128)(2,1)S(1)}, u32[]{:S(2)}, u32[]{:S(2)}) collective-permute-start(bf16[3,32,1792]{2,1,0:T(8,128)(2,1)S(1)} %get-tuple-element.48), channel_id=1, source_target_pairs={{0,48},{16,0},{32,16},{48,32},{1,49},{17,1},{33,17},{49,33},{2,50}... | collective-permute-start | bytes 1032200 | tf_op jit(solution)/shard_map/ppermute | solution.py:22
  24.0 14.8 %collective-permute-start.7 = (bf16[3,32,1792]{2,1,0:T(8,128)(2,1)S(1)}, bf16[3,32,1792]{2,1,0:T(8,128)(2,1)S(1)}, u32[]{:S(2)}, u32[]{:S(2)}) collective-permute-start(bf16[3,32,1792]{2,1,0:T(8,128)(2,1)S(1)} %get-tuple-element.50), channel_id=1, source_target_pairs={{0,48},{16,0},{32,16},{48,32},{1,49},{17,1},{33,17},{49,33},{2,50}... | collective-permute-start | bytes 1032200 | tf_op jit(solution)/shard_map/ppermute | solution.py:22
  25.4 16.6 %collective-permute-start.9 = (bf16[3,32,1792]{2,1,0:T(8,128)(2,1)S(1)}, bf16[3,32,1792]{2,1,0:T(8,128)(2,1)S(1)}, u32[]{:S(2)}, u32[]{:S(2)}) collective-permute-start(bf16[3,32,1792]{2,1,0:T(8,128)(2,1)S(1)} %get-tuple-element.51), channel_id=1, source_target_pairs={{0,16},{16,32},{32,48},{48,0},{1,17},{17,33},{33,49},{49,1},{2,18}... | collective-permute-start | bytes 1032200 | tf_op jit(solution)/shard_map/ppermute | solution.py:22
  32.0 14.7 %collective-permute-start.5 = (bf16[3,32,1792]{2,1,0:T(8,128)(2,1)S(1)}, bf16[3,32,1792]{2,1,0:T(8,128)(2,1)S(1)}, u32[]{:S(2)}, u32[]{:S(2)}) collective-permute-start(bf16[3,32,1792]{2,1,0:T(8,128)(2,1)S(1)} %add_convert_fusion.1), channel_id=1, source_target_pairs={{0,16},{16,32},{32,48},{48,0},{1,17},{17,33},{33,49},{49,1},{2,18}... | collective-permute-start | bytes 1032200 | tf_op jit(solution)/shard_map/ppermute | solution.py:22
  49.5 12.4 %collective-permute-start.11 = (bf16[2,32,1792]{2,1,0:T(8,128)(2,1)S(1)}, bf16[2,32,1792]{2,1,0:T(8,128)(2,1)S(1)}, u32[]{:S(2)}, u32[]{:S(2)}) collective-permute-start(bf16[2,32,1792]{2,1,0:T(8,128)(2,1)S(1)} %get-tuple-element.52.refs_0_), channel_id=1, source_target_pairs={{0,32},{16,48},{32,0},{48,16},{1,33},{17,49},{33,1},{49,17},{2,34}... | collective-permute-start | bytes 688136 | tf_op jit(solution)/shard_map/ppermute | solution.py:22
  53.9 14.2 %collective-permute-start.30 = (bf16[2,32,1792]{2,1,0:T(8,128)(2,1)S(1)}, bf16[2,32,1792]{2,1,0:T(8,128)(2,1)S(1)}, u32[]{:S(2)}, u32[]{:S(2)}) collective-permute-start(bf16[2,32,1792]{2,1,0:T(8,128)(2,1)S(1)} %get-tuple-element.65.refs_0_), channel_id=1, source_target_pairs={{0,16},{16,32},{32,48},{48,0},{1,17},{17,33},{33,49},{49,1},{2,18}... | collective-permute-start | bytes 688136 | tf_op jit(solution)/shard_map/ppermute | solution.py:22
  53.9 17.9 %collective-permute-start.29 = (bf16[2,32,1792]{2,1,0:T(8,128)(2,1)S(1)}, bf16[2,32,1792]{2,1,0:T(8,128)(2,1)S(1)}, u32[]{:S(2)}, u32[]{:S(2)}) collective-permute-start(bf16[2,32,1792]{2,1,0:T(8,128)(2,1)S(1)} %get-tuple-element.65.refs_0_), channel_id=1, source_target_pairs={{0,32},{16,48},{32,0},{48,16},{1,33},{17,49},{33,1},{49,17},{2,34}... | collective-permute-start | bytes 688136 | tf_op jit(solution)/shard_map/ppermute | solution.py:22
  54.3 20.9 %collective-permute-start.28 = (bf16[2,32,1792]{2,1,0:T(8,128)(2,1)S(1)}, bf16[2,32,1792]{2,1,0:T(8,128)(2,1)S(1)}, u32[]{:S(2)}, u32[]{:S(2)}) collective-permute-start(bf16[2,32,1792]{2,1,0:T(8,128)(2,1)S(1)} %get-tuple-element.65.refs_0_), channel_id=1, source_target_pairs={{0,48},{16,0},{32,16},{48,32},{1,49},{17,1},{33,17},{49,33},{2,50}... | collective-permute-start | bytes 688136 | tf_op jit(solution)/shard_map/ppermute | solution.py:22
  56.5 18.6 %collective-permute-start.10 = (bf16[2,32,1792]{2,1,0:T(8,128)(2,1)S(1)}, bf16[2,32,1792]{2,1,0:T(8,128)(2,1)S(1)}, u32[]{:S(2)}, u32[]{:S(2)}) collective-permute-start(bf16[2,32,1792]{2,1,0:T(8,128)(2,1)S(1)} %get-tuple-element.52.refs_0_), channel_id=1, source_target_pairs={{0,48},{16,0},{32,16},{48,32},{1,49},{17,1},{33,17},{49,33},{2,50}... | collective-permute-start | bytes 688136 | tf_op jit(solution)/shard_map/ppermute | solution.py:22
  61.9 13.8 %collective-permute-start.31 = (bf16[2,32,1792]{2,1,0:T(8,128)(2,1)S(1)}, bf16[2,32,1792]{2,1,0:T(8,128)(2,1)S(1)}, u32[]{:S(2)}, u32[]{:S(2)}) collective-permute-start(bf16[2,32,1792]{2,1,0:T(8,128)(2,1)S(1)} %get-tuple-element.65.refs_0_), channel_id=1, source_target_pairs={{0,8},{8,0},{1,9},{9,1},{2,10},{10,2},{3,11},{11,3},{4,12},{12,4},... | collective-permute-start | bytes 688136 | tf_op jit(solution)/shard_map/ppermute | solution.py:22
  80.1 14.6 %collective-permute-start.35 = (bf16[512,256]{1,0:T(8,128)(2,1)S(1)}, bf16[512,256]{1,0:T(8,128)(2,1)S(1)}, u32[]{:S(2)}, u32[]{:S(2)}) collective-permute-start(bf16[512,256]{1,0:T(8,128)(2,1)S(1)} %get-tuple-element.67), channel_id=1, source_target_pairs={{0,2},{2,4},{4,6},{6,0},{1,3},{3,5},{5,7},{7,1},{8,10},{10,12},{12... | collective-permute-start | bytes 786440 | tf_op jit(solution)/shard_map/ppermute | solution.py:22
  81.6 15.3 %collective-permute-start.36 = (bf16[512,256]{1,0:T(8,128)(2,1)S(1)}, bf16[512,256]{1,0:T(8,128)(2,1)S(1)}, u32[]{:S(2)}, u32[]{:S(2)}) collective-permute-start(bf16[512,256]{1,0:T(8,128)(2,1)S(1)} %get-tuple-element.68), channel_id=1, source_target_pairs={{0,4},{2,6},{4,0},{6,2},{1,5},{3,7},{5,1},{7,3},{8,12},{10,14},{12... | collective-permute-start | bytes 786440 | tf_op jit(solution)/shard_map/ppermute | solution.py:22
  94.3 13.7 %collective-permute-start.18 = (bf16[512,256]{1,0:T(8,128)(2,1)S(1)}, bf16[512,256]{1,0:T(8,128)(2,1)S(1)}, u32[]{:S(2)}, u32[]{:S(2)}) collective-permute-start(bf16[512,256]{1,0:T(8,128)(2,1)S(1)} %get-tuple-element.55), channel_id=1, source_target_pairs={{0,4},{2,6},{4,0},{6,2},{1,5},{3,7},{5,1},{7,3},{8,12},{10,14},{12... | collective-permute-start | bytes 786440 | tf_op jit(solution)/shard_map/ppermute | solution.py:22
  94.7 13.4 %collective-permute-start.19 = (bf16[512,256]{1,0:T(8,128)(2,1)S(1)}, bf16[512,256]{1,0:T(8,128)(2,1)S(1)}, u32[]{:S(2)}, u32[]{:S(2)}) collective-permute-start(bf16[512,256]{1,0:T(8,128)(2,1)S(1)} %get-tuple-element.56), channel_id=1, source_target_pairs={{0,6},{2,0},{4,2},{6,4},{1,7},{3,1},{5,3},{7,5},{8,14},{10,8},{12,... | collective-permute-start | bytes 786440 | tf_op jit(solution)/shard_map/ppermute | solution.py:22
  97.6 14.1 %collective-permute-start.38 = (bf16[512,256]{1,0:T(8,128)(2,1)S(1)}, bf16[512,256]{1,0:T(8,128)(2,1)S(1)}, u32[]{:S(2)}, u32[]{:S(2)}) collective-permute-start(bf16[512,256]{1,0:T(8,128)(2,1)S(1)} %sum_z.3.refs_0_), channel_id=1, source_target_pairs={{0,1},{1,0},{2,3},{3,2},{4,5},{5,4},{6,7},{7,6},{8,9},{9,8},{10,11... | collective-permute-start | bytes 786440 | tf_op jit(solution)/shard_map/ppermute | solution.py:22
  100.4 25.3 %collective-permute-start = (bf16[512,512]{1,0:T(8,128)(2,1)S(1)}, bf16[512,512]{1,0:T(8,128)(2,1)S(1)}, u32[]{:S(2)}, u32[]{:S(2)}) collective-permute-start(bf16[512,512]{1,0:T(8,128)(2,1)S(1)} %constant_dynamic-slice_fusion), channel_id=1, source_target_pairs={{0,64},{64,0},{1,65},{65,1},{2,66},{66,2},{3,67},{67,3},{4,68},{68... | collective-permute-start | bytes 1572872 | tf_op jit(solution)/shard_map/ppermute | solution.py:22
  108.8 13.3 %collective-permute-start.20 = (bf16[512,256]{1,0:T(8,128)(2,1)S(1)}, bf16[512,256]{1,0:T(8,128)(2,1)S(1)}, u32[]{:S(2)}, u32[]{:S(2)}) collective-permute-start(bf16[512,256]{1,0:T(8,128)(2,1)S(1)} %sum_z.2.refs_0_), channel_id=1, source_target_pairs={{0,1},{1,0},{2,3},{3,2},{4,5},{5,4},{6,7},{7,6},{8,9},{9,8},{10,11... | collective-permute-start | bytes 786440 | tf_op jit(solution)/shard_map/ppermute | solution.py:22
  112.3 15.3 %collective-permute-start.41 = (bf16[512,256]{1,0:T(8,128)(2,1)S(1)}, bf16[512,256]{1,0:T(8,128)(2,1)S(1)}, u32[]{:S(2)}, u32[]{:S(2)}) collective-permute-start(bf16[512,256]{1,0:T(8,128)(2,1)S(1)} %residual.3.refs_0_), channel_id=1, source_target_pairs={{0,2},{2,4},{4,6},{6,0},{1,3},{3,5},{5,7},{7,1},{8,10},{10,12},{12... | collective-permute-start | bytes 786440 | tf_op jit(solution)/shard_map/ppermute | solution.py:22
  114.1 15.0 %collective-permute-start.40 = (bf16[512,256]{1,0:T(8,128)(2,1)S(1)}, bf16[512,256]{1,0:T(8,128)(2,1)S(1)}, u32[]{:S(2)}, u32[]{:S(2)}) collective-permute-start(bf16[512,256]{1,0:T(8,128)(2,1)S(1)} %residual.3.refs_0_), channel_id=1, source_target_pairs={{0,4},{2,6},{4,0},{6,2},{1,5},{3,7},{5,1},{7,3},{8,12},{10,14},{12... | collective-permute-start | bytes 786440 | tf_op jit(solution)/shard_map/ppermute | solution.py:22
  122.7 12.5 %collective-permute-start.23 = (bf16[512,256]{1,0:T(8,128)(2,1)S(1)}, bf16[512,256]{1,0:T(8,128)(2,1)S(1)}, u32[]{:S(2)}, u32[]{:S(2)}) collective-permute-start(bf16[512,256]{1,0:T(8,128)(2,1)S(1)} %residual.2.refs_0_), channel_id=1, source_target_pairs={{0,2},{2,4},{4,6},{6,0},{1,3},{3,5},{5,7},{7,1},{8,10},{10,12},{12... | collective-permute-start | bytes 786440 | tf_op jit(solution)/shard_map/ppermute | solution.py:22
  125.8 13.7 %collective-permute-start.22 = (bf16[512,256]{1,0:T(8,128)(2,1)S(1)}, bf16[512,256]{1,0:T(8,128)(2,1)S(1)}, u32[]{:S(2)}, u32[]{:S(2)}) collective-permute-start(bf16[512,256]{1,0:T(8,128)(2,1)S(1)} %residual.2.refs_0_), channel_id=1, source_target_pairs={{0,4},{2,6},{4,0},{6,2},{1,5},{3,7},{5,1},{7,3},{8,12},{10,14},{12... | collective-permute-start | bytes 786440 | tf_op jit(solution)/shard_map/ppermute | solution.py:22
  146.0 13.1 %collective-permute-start.44 = (bf16[2,32,1792]{2,1,0:T(8,128)(2,1)S(1)}, bf16[2,32,1792]{2,1,0:T(8,128)(2,1)S(1)}, u32[]{:S(2)}, u32[]{:S(2)}) collective-permute-start(bf16[2,32,1792]{2,1,0:T(8,128)(2,1)S(1)} %get-tuple-element.74), channel_id=1, source_target_pairs={{0,32},{16,48},{32,0},{48,16},{1,33},{17,49},{33,1},{49,17},{2,34}... | collective-permute-start | bytes 688136 | tf_op jit(solution)/shard_map/ppermute | solution.py:22
  149.5 15.0 %collective-permute-start.25 = (bf16[2,32,1792]{2,1,0:T(8,128)(2,1)S(1)}, bf16[2,32,1792]{2,1,0:T(8,128)(2,1)S(1)}, u32[]{:S(2)}, u32[]{:S(2)}) collective-permute-start(bf16[2,32,1792]{2,1,0:T(8,128)(2,1)S(1)} %get-tuple-element.60), channel_id=1, source_target_pairs={{0,16},{16,32},{32,48},{48,0},{1,17},{17,33},{33,49},{49,1},{2,18}... | collective-permute-start | bytes 688136 | tf_op jit(solution)/shard_map/ppermute | solution.py:22
  150.8 18.2 %collective-permute-start.26 = (bf16[2,32,1792]{2,1,0:T(8,128)(2,1)S(1)}, bf16[2,32,1792]{2,1,0:T(8,128)(2,1)S(1)}, u32[]{:S(2)}, u32[]{:S(2)}) collective-permute-start(bf16[2,32,1792]{2,1,0:T(8,128)(2,1)S(1)} %get-tuple-element.61), channel_id=1, source_target_pairs={{0,32},{16,48},{32,0},{48,16},{1,33},{17,49},{33,1},{49,17},{2,34}... | collective-permute-start | bytes 688136 | tf_op jit(solution)/shard_map/ppermute | solution.py:22
  154.6 14.9 %collective-permute-start.27 = (bf16[2,32,1792]{2,1,0:T(8,128)(2,1)S(1)}, bf16[2,32,1792]{2,1,0:T(8,128)(2,1)S(1)}, u32[]{:S(2)}, u32[]{:S(2)}) collective-permute-start(bf16[2,32,1792]{2,1,0:T(8,128)(2,1)S(1)} %get-tuple-element.62), channel_id=1, source_target_pairs={{0,48},{16,0},{32,16},{48,32},{1,49},{17,1},{33,17},{49,33},{2,50}... | collective-permute-start | bytes 688136 | tf_op jit(solution)/shard_map/ppermute | solution.py:22
  170.8 12.9 %collective-permute-start.49 = (bf16[2,64,1792]{2,1,0:T(8,128)(2,1)S(1)}, bf16[2,64,1792]{2,1,0:T(8,128)(2,1)S(1)}, u32[]{:S(2)}, u32[]{:S(2)}) collective-permute-start(bf16[2,64,1792]{2,1,0:T(8,128)(2,1)S(1)} %errors.3.refs_1_), channel_id=1, source_target_pairs={{0,16},{16,32},{32,48},{48,0},{1,17},{17,33},{33,49},{49,1},{2,18}... | collective-permute-start | bytes 1376264 | tf_op jit(solution)/shard_map/ppermute | solution.py:22
  171.4 14.4 %collective-permute-start.47 = (bf16[2,64,1792]{2,1,0:T(8,128)(2,1)S(1)}, bf16[2,64,1792]{2,1,0:T(8,128)(2,1)S(1)}, u32[]{:S(2)}, u32[]{:S(2)}) collective-permute-start(bf16[2,64,1792]{2,1,0:T(8,128)(2,1)S(1)} %errors.3.refs_1_), channel_id=1, source_target_pairs={{0,48},{16,0},{32,16},{48,32},{1,49},{17,1},{33,17},{49,33},{2,50}... | collective-permute-start | bytes 1376264 | tf_op jit(solution)/shard_map/ppermute | solution.py:22
  185.8 13.4 %collective-permute-start.50 = (bf16[2,64,1792]{2,1,0:T(8,128)(2,1)S(1)}, bf16[2,64,1792]{2,1,0:T(8,128)(2,1)S(1)}, u32[]{:S(2)}, u32[]{:S(2)}) collective-permute-start(bf16[2,64,1792]{2,1,0:T(8,128)(2,1)S(1)} %collective-permute-done.49.refs_7_), channel_id=1, source_target_pairs={{0,16},{16,32},{32,48},{48,0},{1,17},{17,33},{33,49},{49,1},{2,18}... | collective-permute-start | bytes 1376264 | tf_op jit(solution)/shard_map/ppermute | solution.py:22
  185.8 14.5 %collective-permute-start.55 = (bf16[2,64,1792]{2,1,0:T(8,128)(2,1)S(1)}, bf16[2,64,1792]{2,1,0:T(8,128)(2,1)S(1)}, u32[]{:S(2)}, u32[]{:S(2)}) collective-permute-start(bf16[2,64,1792]{2,1,0:T(8,128)(2,1)S(1)} %collective-permute-done.47.refs_3_), channel_id=1, source_target_pairs={{0,8},{8,0},{1,9},{9,1},{2,10},{10,2},{3,11},{11,3},{4,12},{12,4},... | collective-permute-start | bytes 1376264 | tf_op jit(solution)/shard_map/ppermute | solution.py:22
  185.9 23.1 %collective-permute-start.52 = (bf16[2,64,1792]{2,1,0:T(8,128)(2,1)S(1)}, bf16[2,64,1792]{2,1,0:T(8,128)(2,1)S(1)}, u32[]{:S(2)}, u32[]{:S(2)}) collective-permute-start(bf16[2,64,1792]{2,1,0:T(8,128)(2,1)S(1)} %collective-permute-done.46.refs_2_), channel_id=1, source_target_pairs={{0,16},{16,32},{32,48},{48,0},{1,17},{17,33},{33,49},{49,1},{2,18}... | collective-permute-start | bytes 1376264 | tf_op jit(solution)/shard_map/ppermute | solution.py:22
  191.7 18.0 %collective-permute-start.51 = (bf16[2,64,1792]{2,1,0:T(8,128)(2,1)S(1)}, bf16[2,64,1792]{2,1,0:T(8,128)(2,1)S(1)}, u32[]{:S(2)}, u32[]{:S(2)}) collective-permute-start(bf16[2,64,1792]{2,1,0:T(8,128)(2,1)S(1)} %collective-permute-done.48.refs_4_), channel_id=1, source_target_pairs={{0,48},{16,0},{32,16},{48,32},{1,49},{17,1},{33,17},{49,33},{2,50}... | collective-permute-start | bytes 1376264 | tf_op jit(solution)/shard_map/ppermute | solution.py:22
  195.1 14.6 %collective-permute-start.54 = (bf16[2,64,1792]{2,1,0:T(8,128)(2,1)S(1)}, bf16[2,64,1792]{2,1,0:T(8,128)(2,1)S(1)}, u32[]{:S(2)}, u32[]{:S(2)}) collective-permute-start(bf16[2,64,1792]{2,1,0:T(8,128)(2,1)S(1)} %collective-permute-done.46.refs_2_), channel_id=1, source_target_pairs={{0,8},{8,0},{1,9},{9,1},{2,10},{10,2},{3,11},{11,3},{4,12},{12,4},... | collective-permute-start | bytes 1376264 | tf_op jit(solution)/shard_map/ppermute | solution.py:22
  (41 other events, 446.6 us)

commit v2 on v1

--- a/solution.py
+++ b/solution.py
@@ -134,33 +134,31 @@
     return own, (both_low, direct_low), (both_high, direct_high)
 
 
-def coefficients(ids, own, lows, highs):
+def coefficients(ids, chunk, own, sums, after=()):
     n, rows, cols = own.shape
     half = rows // 2
+    mine = slice(chunk * half, (chunk + 1) * half)
     inv_width = 1.0 / math.sqrt(D)
 
-    def body(ids, own_ref, l0, l1, h0, h1, low_ref, high_ref, first_ref, second_ref):
-        def step(at):
-            for start, a, b, pay_ref in ((0, l0, l1, low_ref), (half, h0, h1, high_ref)):
-                to = slice(start, start + half)
-                gate, up, tangent = (
-                    own_ref[i, to, at] + a[i, :, at].astype(F32) + b[i, :, at].astype(F32)
-                    for i in range(3)
-                )
-                tangent = tangent * inv_width
-                sig = jax.nn.sigmoid(gate)
-                first = sig * (1.0 + gate * (1.0 - sig)) * up
-                second = sig * (1.0 - sig) * (2.0 + gate * (1.0 - 2.0 * sig)) * (tangent * up)
-                pay_ref[0, :, at] = (gate * sig * up).astype(BF)
-                pay_ref[1, :, at] = (first * tangent).astype(BF)
-                first_ref[to, at] = first.astype(BF)
-                second_ref[to, at] = second.astype(BF)
-
-        loop_tiles(cols, TILE, step)
-
-    pay = shape((2, half, cols))
-    outs = [pay, pay, shape((rows, cols)), shape((rows, cols))]
-    return call(body, ids, (own, *lows, *highs), outs)
+    def body(ids, own_ref, a, b, pay_ref, first_ref, second_ref):
+        def step(at):
+            gate, up, tangent = (
+                own_ref[i, mine, at] + a[i, :, at].astype(F32) + b[i, :, at].astype(F32)
+                for i in range(n)
+            )
+            tangent = tangent * inv_width
+            sig = jax.nn.sigmoid(gate)
+            first = sig * (1.0 + gate * (1.0 - sig)) * up
+            second = sig * (1.0 - sig) * (2.0 + gate * (1.0 - 2.0 * sig)) * (tangent * up)
+            pay_ref[0, :, at] = (gate * sig * up).astype(BF)
+            pay_ref[1, :, at] = (first * tangent).astype(BF)
+            first_ref[:, at] = first.astype(BF)
+            second_ref[:, at] = second.astype(BF)
+
+        loop_tiles(cols, TILE, step)
+
+    outs = [shape((2, half, cols)), shape((half, cols)), shape((half, cols))]
+    return call(body, ids, (own, *sums), outs, after=after)
 
 
 def gather_y(value):
@@ -174,8 +172,9 @@
 def ring_pair(near, far):
     near_low, near_high = shift(near, "y", 1), shift(near, "y", -1)
     far_low, far_high = shift(far, "y", 1), shift(far, "y", -1)
-    across = shift(near_low, "y", 1), shift(far_high, "y", -1)
-    return [near, far, near_high, far_high, *across, near_low, far_low]
+    across = [shift(near_low[0], "y", 1), shift(near_high[1], "y", -1)]
+    beyond = [shift(v, "dp", 1) for v in across]
+    return [near, far, near_high, far_high, near_low, far_low], across + beyond
 
 
 def down_products(ids, pieces, down):
@@ -297,9 +296,9 @@
 
         def step(at):
             back, back_dot = (sum_at(refs[:len(terms)], i, at) for i in range(2))
-            f = f_ref[mine, at].astype(F32)
+            f = f_ref[:, at].astype(F32)
             o_ref[0, mine, at] = (back * f).astype(BF)
-            o_ref[1, mine, at] = (back * s_ref[mine, at].astype(F32) + back_dot * f).astype(BF)
+            o_ref[1, mine, at] = (back * s_ref[:, at].astype(F32) + back_dot * f).astype(BF)
             for ref in done:
                 o_ref[:, :chunk * rows, at] = ref[:, :, at]
 
@@ -316,12 +315,11 @@
     def body(ids, t_ref, x_ref, o_ref, held):
         cols = pl.ds(pl.multiple_of(ids[0] * half, half), half)
         at = 0
-        for c in range(2):
-            for y in range(NY):
-                row = pl.ds(token_row(ids, c, y, rows), rows)
-                held[at:at + rows, :] = t_ref[row, cols]
-                held[at + rows:at + 2 * rows, :] = x_ref[row, :]
-                at += 2 * rows
+        for c, y in [(c, y) for c in range(2) for y in (0, 1, 3)] + [(0, 2), (1, 2)]:
+            row = pl.ds(token_row(ids, c, y, rows), rows)
+            held[at:at + rows, :] = t_ref[row, cols]
+            held[at + rows:at + 2 * rows, :] = x_ref[row, :]
+            at += 2 * rows
         o_ref[...] = held[...].T
 
     return call(
@@ -330,22 +328,22 @@
     )[0]
 
 
-def outer_products(ids, lhs, pieces, probe):
+def outer_products(ids, lhs, pieces, halves, probe):
     out_rows, count = lhs.shape
     _, rows, cols = pieces[0].shape
     token_scale = 1.0 / math.sqrt(count)
     inv_width = 1.0 / math.sqrt(D)
-    n = len(pieces)
+    n, m = len(pieces), len(pieces) + len(halves)
 
     def body(ids, l_ref, *refs):
-        p_refs, probe_ref, g_ref, h_ref = refs[:n], refs[n], refs[n + 1], refs[n + 2]
+        p_refs, probe_ref, g_ref, h_ref = refs[:n], refs[m], refs[m + 1], refs[m + 2]
         probe_rows = pl.ds(pl.multiple_of(ids[0] * out_rows, out_rows), out_rows)
 
         def step(at):
-            err = jnp.concatenate([p[0, :, at] for p in p_refs], axis=0)
+            err = jnp.concatenate([p[0, :, at] for p in p_refs] + [p[:, at] for p in refs[n:m:2]], axis=0)
             g = jnp.dot(l_ref[...], err, preferred_element_type=F32) * token_scale
             g_ref[:, at] = g.astype(BF)
-            err = jnp.concatenate([p[1, :, at] for p in p_refs], axis=0)
+            err = jnp.concatenate([p[1, :, at] for p in p_refs] + [p[:, at] for p in refs[n + 1:m:2]], axis=0)
             hv = jnp.dot(l_ref[...], err, preferred_element_type=F32) * token_scale
             h_ref[:, at] = (probe_ref[probe_rows, at].astype(F32) * hv * inv_width).astype(BF)
 
@@ -353,7 +351,7 @@
 
     out = shape((out_rows, cols))
     return call(
-        body, ids, (lhs, *pieces, probe), [out, out],
+        body, ids, (lhs, *pieces, *halves, probe), [out, out],
         flops=4 * out_rows * count * cols, limit=12,
     )
 
@@ -369,10 +367,11 @@
     ordered = ordered_tokens(ids, rows, tokens)
     pairs = [pre_products(ids, rows, ordered, w) for w in (gate_weight, up_weight, probe_sign)]
     recvs = swap_cores([other for _, other in pairs])
-    own, lows, highs = ring_scatter(split_pre(ids, [own for own, _ in pairs], recvs))
-    *pays, first, second = coefficients(ids, own, lows, highs)
-    done = ()
-    for c, pay in enumerate(pays):
+    whole, *sums = ring_scatter(split_pre(ids, [own for own, _ in pairs], recvs))
+    done, before = (), ()
+    for c in range(2):
+        pay, first, second = coefficients(ids, c, whole, sums[c], before)
+        before = (pay,)
         near = gather_y(pay)
         parts = spread("z", down_products(ids, near + swap_cores(near), down_weight))
         part = sum_z(ids, parts)
@@ -381,8 +380,10 @@
         own, other = back_products(ids, parts, down_weight, rows // 2, () if c else (lhs,))
         terms = spread("y", split_back(ids, own, shift(other, "core", 1)))
         done = (errors(ids, c, terms, first, second, done),)
-    near = ring_pair(done[0], shift(done[0], "dp", 1))
-    return outer_products(ids, lhs, near + swap_cores(near), probe_sign)
+    near, across = ring_pair(done[0], shift(done[0], "dp", 1))
+    return outer_products(
+        ids, lhs, near + swap_cores(near), across + swap_cores(across), probe_sign
+    )
 
 
 def solution(mesh):

time: 220 us -> 215 us (0.977)
  waiting for transfers between devices: 83.8 us -> 79.7 us
    ppermute x61 -> x65, waiting for transfers between devices: 83.8 us -> 79.7 us  [shift(): lax.ppermute(value, axis, [(i, (i + step) % size) for i in range(size)])]
    ppermute x61 -> x65, starting transfers between devices: 84.1 us -> 83.1 us  [shift(): lax.ppermute(value, axis, [(i, (i + step) % size) for i in range(size)])]
    pallas_call x20 -> x21, Pallas kernels: 43.1 us -> 43.6 us  [call(): pl.pallas_call(kernel, out_shape=tuple(outs), in_specs=[pl.BlockSpec(memo...]
  transfers between devices with their start and end apart: 61 -> 65, of which waited for: 26 -> 26; matrix products, arithmetic and copies ran while one was open for 0% -> 0% of each run, Pallas kernels for 13% -> 14%
where the time goes in v2:
time: 215 us
  starting transfers between devices  83.1 us (39%)
  waiting for transfers between devices  79.7 us (37%)
  Pallas kernels  43.6 us (20%)
  local copies, waits for them, and re-layouts  7.25 us (3%)
    ppermute x65, starting transfers between devices, shift(): lax.ppermute(value, axis, [(i, (i + step) % size) for i in range(size)])  83.1 us
    ppermute x65, waiting for transfers between devices, shift(): lax.ppermute(value, axis, [(i, (i + step) % size) for i in range(size)])  79.7 us
    pallas_call x21, Pallas kernels, call(): pl.pallas_call(kernel, out_shape=tuple(outs), in_specs=[pl.BlockSpec(memo...  43.6 us
    unnamed x24, local copies, waits for them, and re-layouts  7.1 us
  transfers between devices with their start and end apart: 65, of which 26 were waited for; matrix products, arithmetic and copies ran while one was open for 0% of the time, Pallas kernels for 14%

profile of v2, /device:TPU:1, one launch (start us, length us, event | category | flops | bytes accessed | tf_op | source)
XLA Modules:
  0.0 214.8 jit_solution(8909061059231804651)
XLA Ops:
  4.6 3.6 %pre_products.5 = (bf16[4,64,1792]{2,1,0:T(8,128)(2,1)S(1)}, bf16[4,64,1792]{2,1,0:T(8,128)(2,1)S(1)}) custom-call(s32[5]{0:T(128)S(1)} %stack.23.ids, bf16[512,1024]{1,0:T(8,128)(2,1)S(1)} %ordered_tokens.1.refs_0_, bf16[1024,1792]{1,0:T(8,128)(2,1)S(1)} %copy-done.8), custom_call_target="tpu_custom_call" | custom-call | flops 1879048192 | bytes 6553600 | tf_op jit(solution)/shard_map/pre_products/pallas_call | solution.py:43
  9.8 3.6 %pre_products.3 = (bf16[4,64,1792]{2,1,0:T(8,128)(2,1)S(1)}, bf16[4,64,1792]{2,1,0:T(8,128)(2,1)S(1)}) custom-call(s32[5]{0:T(128)S(1)} %stack.23.ids, bf16[512,1024]{1,0:T(8,128)(2,1)S(1)} %ordered_tokens.1.refs_0_, bf16[1024,1792]{1,0:T(8,128)(2,1)S(1)} %copy-done.3), custom_call_target="tpu_custom_call" | custom-call | flops 1879048192 | bytes 6553600 | tf_op jit(solution)/shard_map/pre_products/pallas_call | solution.py:43
  13.5 3.6 %pre_products.4 = (bf16[4,64,1792]{2,1,0:T(8,128)(2,1)S(1)}, bf16[4,64,1792]{2,1,0:T(8,128)(2,1)S(1)}) custom-call(s32[5]{0:T(128)S(1)} %stack.23.ids, bf16[512,1024]{1,0:T(8,128)(2,1)S(1)} %ordered_tokens.1.refs_0_, bf16[1024,1792]{1,0:T(8,128)(2,1)S(1)} %copy-done.4), custom_call_target="tpu_custom_call" | custom-call | flops 1879048192 | bytes 6553600 | tf_op jit(solution)/shard_map/pre_products/pallas_call | solution.py:43
  24.0 2.7 %collective-permute-start.9 = (bf16[3,32,1792]{2,1,0:T(8,128)(2,1)S(1)}, bf16[3,32,1792]{2,1,0:T(8,128)(2,1)S(1)}, u32[]{:S(2)}, u32[]{:S(2)}) collective-permute-start(bf16[3,32,1792]{2,1,0:T(8,128)(2,1)S(1)} %get-tuple-element.53), channel_id=1, source_target_pairs={{0,48},{16,0},{32,16},{48,32},{1,49},{17,1},{33,17},{49,33},{2,50}... | collective-permute-start | bytes 1032200 | tf_op jit(solution)/shard_map/ppermute | solution.py:22
  26.7 5.2 %collective-permute-done.7 = bf16[3,32,1792]{2,1,0:T(8,128)(2,1)S(1)} collective-permute-done((bf16[3,32,1792]{2,1,0:T(8,128)(2,1)S(1)}, bf16[3,32,1792]{2,1,0:T(8,128)(2,1)S(1)}, u32[]{:S(2)}, u32[]{:S(2)}) %collective-permute-start.7) | collective-permute-done | bytes 344096 | tf_op jit(solution)/shard_map/ppermute | solution.py:22
  32.2 2.7 %collective-permute-start.5 = (bf16[3,32,1792]{2,1,0:T(8,128)(2,1)S(1)}, bf16[3,32,1792]{2,1,0:T(8,128)(2,1)S(1)}, u32[]{:S(2)}, u32[]{:S(2)}) collective-permute-start(bf16[3,32,1792]{2,1,0:T(8,128)(2,1)S(1)} %add_convert_fusion.1), channel_id=1, source_target_pairs={{0,48},{16,0},{32,16},{48,32},{1,49},{17,1},{33,17},{49,33},{2,50}... | collective-permute-start | bytes 1032200 | tf_op jit(solution)/shard_map/ppermute | solution.py:22
  34.9 3.9 %collective-permute-done.9.refs_2_ = bf16[3,32,1792]{2,1,0:T(8,128)(2,1)S(1)} collective-permute-done((bf16[3,32,1792]{2,1,0:T(8,128)(2,1)S(1)}, bf16[3,32,1792]{2,1,0:T(8,128)(2,1)S(1)}, u32[]{:S(2)}, u32[]{:S(2)}) %collective-permute-start.9) | collective-permute-done | bytes 344096 | tf_op jit(solution)/shard_map/ppermute | solution.py:22
  38.8 7.8 %collective-permute-done.8.refs_1_ = bf16[3,32,1792]{2,1,0:T(8,128)(2,1)S(1)} collective-permute-done((bf16[3,32,1792]{2,1,0:T(8,128)(2,1)S(1)}, bf16[3,32,1792]{2,1,0:T(8,128)(2,1)S(1)}, u32[]{:S(2)}, u32[]{:S(2)}) %collective-permute-start.8) | collective-permute-done | bytes 344096 | tf_op jit(solution)/shard_map/ppermute | solution.py:22
  48.5 2.8 %collective-permute-start.11 = (bf16[2,32,1792]{2,1,0:T(8,128)(2,1)S(1)}, bf16[2,32,1792]{2,1,0:T(8,128)(2,1)S(1)}, u32[]{:S(2)}, u32[]{:S(2)}) collective-permute-start(bf16[2,32,1792]{2,1,0:T(8,128)(2,1)S(1)} %get-tuple-element.55.refs_0_), channel_id=1, source_target_pairs={{0,32},{16,48},{32,0},{48,16},{1,33},{17,49},{33,1},{49,17},{2,34}... | collective-permute-start | bytes 688136 | tf_op jit(solution)/shard_map/ppermute | solution.py:22
  56.0 4.7 %collective-permute-done.11.refs_2_ = bf16[2,32,1792]{2,1,0:T(8,128)(2,1)S(1)} collective-permute-done((bf16[2,32,1792]{2,1,0:T(8,128)(2,1)S(1)}, bf16[2,32,1792]{2,1,0:T(8,128)(2,1)S(1)}, u32[]{:S(2)}, u32[]{:S(2)}) %collective-permute-start.11) | collective-permute-done | bytes 229408 | tf_op jit(solution)/shard_map/ppermute | solution.py:22
  60.6 4.0 %collective-permute-start.31 = (bf16[2,32,1792]{2,1,0:T(8,128)(2,1)S(1)}, bf16[2,32,1792]{2,1,0:T(8,128)(2,1)S(1)}, u32[]{:S(2)}, u32[]{:S(2)}) collective-permute-start(bf16[2,32,1792]{2,1,0:T(8,128)(2,1)S(1)} %get-tuple-element.54.refs_3_.refs_0_), channel_id=1, source_target_pairs={{0,8},{8,0},{1,9},{9,1},{2,10},{10,2},{3,11},{11,3},{4,12},{12,4},... | collective-permute-start | bytes 688136 | tf_op jit(solution)/shard_map/ppermute | solution.py:22
  65.6 3.5 %collective-permute-start.34 = (bf16[2,32,1792]{2,1,0:T(8,128)(2,1)S(1)}, bf16[2,32,1792]{2,1,0:T(8,128)(2,1)S(1)}, u32[]{:S(2)}, u32[]{:S(2)}) collective-permute-start(bf16[2,32,1792]{2,1,0:T(8,128)(2,1)S(1)} %collective-permute-done.30.refs_3_), channel_id=1, source_target_pairs={{0,8},{8,0},{1,9},{9,1},{2,10},{10,2},{3,11},{11,3},{4,12},{12,4},... | collective-permute-start | bytes 688136 | tf_op jit(solution)/shard_map/ppermute | solution.py:22
  74.1 3.4 %down_products.3 = (bf16[512,256]{1,0:T(8,128)(2,1)S(1)}, bf16[512,256]{1,0:T(8,128)(2,1)S(1)}, bf16[512,256]{1,0:T(8,128)(2,1)S(1)}, bf16[512,256]{1,0:T(8,128)(2,1)S(1)}) custom-call(s32[5]{0:T(128)S(1)} %stack.23.ids, bf16[2,32,1792]{2,1,0:T(8,128)(2,1)S(1)} %get-tuple-element.54.refs_3_.refs_0_, ...), custom_call_target="tpu_custom_call" | custom-call | flops 1879048192 | bytes 6553600 | tf_op jit(solution)/shard_map/down_products/pallas_call | solution.py:43
  79.2 3.3 %collective-permute-start.36 = (bf16[512,256]{1,0:T(8,128)(2,1)S(1)}, bf16[512,256]{1,0:T(8,128)(2,1)S(1)}, u32[]{:S(2)}, u32[]{:S(2)}) collective-permute-start(bf16[512,256]{1,0:T(8,128)(2,1)S(1)} %get-tuple-element.70), channel_id=1, source_target_pairs={{0,4},{2,6},{4,0},{6,2},{1,5},{3,7},{5,1},{7,3},{8,12},{10,14},{12... | collective-permute-start | bytes 786440 | tf_op jit(solution)/shard_map/ppermute | solution.py:22
  87.1 3.9 %down_products.2 = (bf16[512,256]{1,0:T(8,128)(2,1)S(1)}, bf16[512,256]{1,0:T(8,128)(2,1)S(1)}, bf16[512,256]{1,0:T(8,128)(2,1)S(1)}, bf16[512,256]{1,0:T(8,128)(2,1)S(1)}) custom-call(s32[5]{0:T(128)S(1)} %stack.23.ids, bf16[2,32,1792]{2,1,0:T(8,128)(2,1)S(1)} %get-tuple-element.55.refs_0_, bf16[2,32,1792]{2,1,0:T(8,128)(2,1)S(1)} %collective-permute-done.10.refs_1_, ...), custom_call_target="tpu_custom_call" | custom-call | flops 1879048192 | bytes 6553600 | tf_op jit(solution)/shard_map/down_products/pallas_call | solution.py:43
  95.2 2.8 %collective-permute-start.38 = (bf16[512,256]{1,0:T(8,128)(2,1)S(1)}, bf16[512,256]{1,0:T(8,128)(2,1)S(1)}, u32[]{:S(2)}, u32[]{:S(2)}) collective-permute-start(bf16[512,256]{1,0:T(8,128)(2,1)S(1)} %sum_z.3.refs_0_), channel_id=1, source_target_pairs={{0,1},{1,0},{2,3},{3,2},{4,5},{5,4},{6,7},{7,6},{8,9},{9,8},{10,11... | collective-permute-start | bytes 786440 | tf_op jit(solution)/shard_map/ppermute | solution.py:22
  99.7 5.8 %collective-permute-done.18.refs_2_ = bf16[512,256]{1,0:T(8,128)(2,1)S(1)} collective-permute-done((bf16[512,256]{1,0:T(8,128)(2,1)S(1)}, bf16[512,256]{1,0:T(8,128)(2,1)S(1)}, u32[]{:S(2)}, u32[]{:S(2)}) %collective-permute-start.18) | collective-permute-done | bytes 262176 | tf_op jit(solution)/shard_map/ppermute | solution.py:22
  106.4 2.9 %collective-permute-start.20 = (bf16[512,256]{1,0:T(8,128)(2,1)S(1)}, bf16[512,256]{1,0:T(8,128)(2,1)S(1)}, u32[]{:S(2)}, u32[]{:S(2)}) collective-permute-start(bf16[512,256]{1,0:T(8,128)(2,1)S(1)} %sum_z.2.refs_0_), channel_id=1, source_target_pairs={{0,1},{1,0},{2,3},{3,2},{4,5},{5,4},{6,7},{7,6},{8,9},{9,8},{10,11... | collective-permute-start | bytes 786440 | tf_op jit(solution)/shard_map/ppermute | solution.py:22
  111.7 2.8 %collective-permute-start.40 = (bf16[512,256]{1,0:T(8,128)(2,1)S(1)}, bf16[512,256]{1,0:T(8,128)(2,1)S(1)}, u32[]{:S(2)}, u32[]{:S(2)}) collective-permute-start(bf16[512,256]{1,0:T(8,128)(2,1)S(1)} %residual.3.refs_0_), channel_id=1, source_target_pairs={{0,4},{2,6},{4,0},{6,2},{1,5},{3,7},{5,1},{7,3},{8,12},{10,14},{12... | collective-permute-start | bytes 786440 | tf_op jit(solution)/shard_map/ppermute | solution.py:22
  114.5 5.2 %collective-permute-done.20.refs_1_ = bf16[512,256]{1,0:T(8,128)(2,1)S(1)} collective-permute-done((bf16[512,256]{1,0:T(8,128)(2,1)S(1)}, bf16[512,256]{1,0:T(8,128)(2,1)S(1)}, u32[]{:S(2)}, u32[]{:S(2)}) %collective-permute-start.20) | collective-permute-done | bytes 262176 | tf_op jit(solution)/shard_map/ppermute | solution.py:22
  120.3 3.1 %collective-permute-start.23 = (bf16[512,256]{1,0:T(8,128)(2,1)S(1)}, bf16[512,256]{1,0:T(8,128)(2,1)S(1)}, u32[]{:S(2)}, u32[]{:S(2)}) collective-permute-start(bf16[512,256]{1,0:T(8,128)(2,1)S(1)} %residual.2.refs_0_), channel_id=1, source_target_pairs={{0,2},{2,4},{4,6},{6,0},{1,3},{3,5},{5,7},{7,1},{8,10},{10,12},{12... | collective-permute-start | bytes 786440 | tf_op jit(solution)/shard_map/ppermute | solution.py:22
  126.8 4.0 %back_products.3 = (bf16[4,2,32,1792]{3,2,1,0:T(8,128)(2,1)S(1)}, bf16[4,2,32,1792]{3,2,1,0:T(8,128)(2,1)S(1)}) custom-call(s32[5]{0:T(128)S(1)} %stack.23.ids, bf16[512,256]{1,0:T(8,128)(2,1)S(1)} %residual.3.refs_0_, bf16[512,256]{1,0:T(8,128)(2,1)S(1)} %collective-permute-done.39.refs_1_, bf16[512,256]{1,0:T(8,128)(2,1)S(1)} %collective-permute-done.40.refs_2_, ...), custom_call_target="tpu_custom_call" | custom-call | flops 1879048192 | bytes 6553600 | tf_op jit(solution)/shard_map/back_products/pallas_call | solution.py:43
  132.8 4.2 %collective-permute-done.22.refs_2_ = bf16[512,256]{1,0:T(8,128)(2,1)S(1)} collective-permute-done((bf16[512,256]{1,0:T(8,128)(2,1)S(1)}, bf16[512,256]{1,0:T(8,128)(2,1)S(1)}, u32[]{:S(2)}, u32[]{:S(2)}) %collective-permute-start.22) | collective-permute-done | bytes 262176 | tf_op jit(solution)/shard_map/ppermute | solution.py:22
  137.0 4.0 %back_products.2 = (bf16[4,2,32,1792]{3,2,1,0:T(8,128)(2,1)S(1)}, bf16[4,2,32,1792]{3,2,1,0:T(8,128)(2,1)S(1)}) custom-call(s32[5]{0:T(128)S(1)} %stack.23.ids, bf16[512,256]{1,0:T(8,128)(2,1)S(1)} %residual.2.refs_0_, bf16[512,256]{1,0:T(8,128)(2,1)S(1)} %collective-permute-done.21.refs_1_, bf16[512,256]{1,0:T(8,128)(2,1)S(1)} %collective-permute-done.22.refs_2_, ...), custom_call_target="tpu_custom_call" | custom-call | flops 1879048192 | bytes 6553600 | tf_op jit(solution)/shard_map/back_products/pallas_call | solution.py:43
  152.7 4.7 %collective-permute-done.44.refs_2_ = bf16[2,32,1792]{2,1,0:T(8,128)(2,1)S(1)} collective-permute-done((bf16[2,32,1792]{2,1,0:T(8,128)(2,1)S(1)}, bf16[2,32,1792]{2,1,0:T(8,128)(2,1)S(1)}, u32[]{:S(2)}, u32[]{:S(2)}) %collective-permute-start.44) | collective-permute-done | bytes 229408 | tf_op jit(solution)/shard_map/ppermute | solution.py:22
  158.1 3.7 %collective-permute-done.25.refs_1_ = bf16[2,32,1792]{2,1,0:T(8,128)(2,1)S(1)} collective-permute-done((bf16[2,32,1792]{2,1,0:T(8,128)(2,1)S(1)}, bf16[2,32,1792]{2,1,0:T(8,128)(2,1)S(1)}, u32[]{:S(2)}, u32[]{:S(2)}) %collective-permute-start.25) | collective-permute-done | bytes 229408 | tf_op jit(solution)/shard_map/ppermute | solution.py:22
  161.8 5.4 %collective-permute-done.26.refs_2_ = bf16[2,32,1792]{2,1,0:T(8,128)(2,1)S(1)} collective-permute-done((bf16[2,32,1792]{2,1,0:T(8,128)(2,1)S(1)}, bf16[2,32,1792]{2,1,0:T(8,128)(2,1)S(1)}, u32[]{:S(2)}, u32[]{:S(2)}) %collective-permute-start.26) | collective-permute-done | bytes 229408 | tf_op jit(solution)/shard_map/ppermute | solution.py:22
  172.5 8.0 %collective-permute-done.49.refs_5_ = bf16[2,64,1792]{2,1,0:T(8,128)(2,1)S(1)} collective-permute-done((bf16[2,64,1792]{2,1,0:T(8,128)(2,1)S(1)}, bf16[2,64,1792]{2,1,0:T(8,128)(2,1)S(1)}, u32[]{:S(2)}, u32[]{:S(2)}) %collective-permute-start.49) | collective-permute-done | bytes 458784 | tf_op jit(solution)/shard_map/ppermute | solution.py:22
  181.9 3.5 %collective-permute-start.58 = (bf16[64,1792]{1,0:T(8,128)(2,1)S(1)}, bf16[64,1792]{1,0:T(8,128)(2,1)S(1)}, u32[]{:S(2)}, u32[]{:S(2)}) collective-permute-start(bf16[64,1792]{1,0:T(8,128)(2,1)S(1)} %slice_bitcast_fusion), channel_id=1, source_target_pairs={{0,48},{16,0},{32,16},{48,32},{1,49},{17,1},{33,17},{49,33},{2,50}... | collective-permute-start | bytes 688136 | tf_op jit(solution)/shard_map/ppermute | solution.py:22
  187.2 2.7 %collective-permute-start.61 = (bf16[64,1792]{1,0:T(8,128)(2,1)S(1)}, bf16[64,1792]{1,0:T(8,128)(2,1)S(1)}, u32[]{:S(2)}, u32[]{:S(2)}) collective-permute-start(bf16[64,1792]{1,0:T(8,128)(2,1)S(1)} %collective-permute-done.57.refs_13_), channel_id=1, source_target_pairs={{0,8},{8,0},{1,9},{9,1},{2,10},{10,2},{3,11},{11,3},{4,12},{12,4},... | collective-permute-start | bytes 688136 | tf_op jit(solution)/shard_map/ppermute | solution.py:22
  198.7 4.7 %collective-permute-done.50.refs_6_ = bf16[2,64,1792]{2,1,0:T(8,128)(2,1)S(1)} collective-permute-done((bf16[2,64,1792]{2,1,0:T(8,128)(2,1)S(1)}, bf16[2,64,1792]{2,1,0:T(8,128)(2,1)S(1)}, u32[]{:S(2)}, u32[]{:S(2)}) %collective-permute-start.50) | collective-permute-done | bytes 458784 | tf_op jit(solution)/shard_map/ppermute | solution.py:22
  207.4 7.4 %outer_products.1 = (bf16[512,1792]{1,0:T(8,128)(2,1)}, bf16[512,1792]{1,0:T(8,128)(2,1)}) custom-call(s32[5]{0:T(128)S(1)} %stack.23.ids, bf16[512,1024]{1,0:T(8,128)(2,1)S(1)} %transposed_tokens.1.refs_5_.refs_0_, bf16[2,64,1792]{2,1,0:T(8,128)(2,1)S(1)} %errors.3.refs_1_, bf16[2,64,1792]{2,1,0:T(8,128)(2,1)S(1)} %collective-permute-done.46.refs_2_, ...), custom_call_target="tpu_custom_call" | custom-call | flops 3758096384 | bytes 15728640 | tf_op jit(solution)/shard_map/outer_products/pallas_call | solution.py:43
  (149 shorter events, 80.1 us)
Async XLA Ops:
  24.0 23.5 %collective-permute-start.6 = (bf16[3,32,1792]{2,1,0:T(8,128)(2,1)S(1)}, bf16[3,32,1792]{2,1,0:T(8,128)(2,1)S(1)}, u32[]{:S(2)}, u32[]{:S(2)}) collective-permute-start(bf16[3,32,1792]{2,1,0:T(8,128)(2,1)S(1)} %get-tuple-element.50), channel_id=1, source_target_pairs={{0,16},{16,32},{32,48},{48,0},{1,17},{17,33},{33,49},{49,1},{2,18}... | collective-permute-start | bytes 1032200 | tf_op jit(solution)/shard_map/ppermute | solution.py:22
  24.0 14.8 %collective-permute-start.9 = (bf16[3,32,1792]{2,1,0:T(8,128)(2,1)S(1)}, bf16[3,32,1792]{2,1,0:T(8,128)(2,1)S(1)}, u32[]{:S(2)}, u32[]{:S(2)}) collective-permute-start(bf16[3,32,1792]{2,1,0:T(8,128)(2,1)S(1)} %get-tuple-element.53), channel_id=1, source_target_pairs={{0,48},{16,0},{32,16},{48,32},{1,49},{17,1},{33,17},{49,33},{2,50}... | collective-permute-start | bytes 1032200 | tf_op jit(solution)/shard_map/ppermute | solution.py:22
  32.0 14.7 %collective-permute-start.8 = (bf16[3,32,1792]{2,1,0:T(8,128)(2,1)S(1)}, bf16[3,32,1792]{2,1,0:T(8,128)(2,1)S(1)}, u32[]{:S(2)}, u32[]{:S(2)}) collective-permute-start(bf16[3,32,1792]{2,1,0:T(8,128)(2,1)S(1)} %add_convert_fusion), channel_id=1, source_target_pairs={{0,16},{16,32},{32,48},{48,0},{1,17},{17,33},{33,49},{49,1},{2,18}... | collective-permute-start | bytes 1032200 | tf_op jit(solution)/shard_map/ppermute | solution.py:22
  32.2 15.4 %collective-permute-start.5 = (bf16[3,32,1792]{2,1,0:T(8,128)(2,1)S(1)}, bf16[3,32,1792]{2,1,0:T(8,128)(2,1)S(1)}, u32[]{:S(2)}, u32[]{:S(2)}) collective-permute-start(bf16[3,32,1792]{2,1,0:T(8,128)(2,1)S(1)} %add_convert_fusion.1), channel_id=1, source_target_pairs={{0,48},{16,0},{32,16},{48,32},{1,49},{17,1},{33,17},{49,33},{2,50}... | collective-permute-start | bytes 1032200 | tf_op jit(solution)/shard_map/ppermute | solution.py:22
  51.3 14.3 %collective-permute-start.30 = (bf16[2,32,1792]{2,1,0:T(8,128)(2,1)S(1)}, bf16[2,32,1792]{2,1,0:T(8,128)(2,1)S(1)}, u32[]{:S(2)}, u32[]{:S(2)}) collective-permute-start(bf16[2,32,1792]{2,1,0:T(8,128)(2,1)S(1)} %get-tuple-element.54.refs_3_.refs_0_), channel_id=1, source_target_pairs={{0,16},{16,32},{32,48},{48,0},{1,17},{17,33},{33,49},{49,1},{2,18}... | collective-permute-start | bytes 688136 | tf_op jit(solution)/shard_map/ppermute | solution.py:22
  51.7 18.7 %collective-permute-start.29 = (bf16[2,32,1792]{2,1,0:T(8,128)(2,1)S(1)}, bf16[2,32,1792]{2,1,0:T(8,128)(2,1)S(1)}, u32[]{:S(2)}, u32[]{:S(2)}) collective-permute-start(bf16[2,32,1792]{2,1,0:T(8,128)(2,1)S(1)} %get-tuple-element.54.refs_3_.refs_0_), channel_id=1, source_target_pairs={{0,32},{16,48},{32,0},{48,16},{1,33},{17,49},{33,1},{49,17},{2,34}... | collective-permute-start | bytes 688136 | tf_op jit(solution)/shard_map/ppermute | solution.py:22
  53.2 19.4 %collective-permute-start.28 = (bf16[2,32,1792]{2,1,0:T(8,128)(2,1)S(1)}, bf16[2,32,1792]{2,1,0:T(8,128)(2,1)S(1)}, u32[]{:S(2)}, u32[]{:S(2)}) collective-permute-start(bf16[2,32,1792]{2,1,0:T(8,128)(2,1)S(1)} %get-tuple-element.54.refs_3_.refs_0_), channel_id=1, source_target_pairs={{0,48},{16,0},{32,16},{48,32},{1,49},{17,1},{33,17},{49,33},{2,50}... | collective-permute-start | bytes 688136 | tf_op jit(solution)/shard_map/ppermute | solution.py:22
  55.8 16.8 %collective-permute-start.10 = (bf16[2,32,1792]{2,1,0:T(8,128)(2,1)S(1)}, bf16[2,32,1792]{2,1,0:T(8,128)(2,1)S(1)}, u32[]{:S(2)}, u32[]{:S(2)}) collective-permute-start(bf16[2,32,1792]{2,1,0:T(8,128)(2,1)S(1)} %get-tuple-element.55.refs_0_), channel_id=1, source_target_pairs={{0,48},{16,0},{32,16},{48,32},{1,49},{17,1},{33,17},{49,33},{2,50}... | collective-permute-start | bytes 688136 | tf_op jit(solution)/shard_map/ppermute | solution.py:22
  60.6 12.5 %collective-permute-start.31 = (bf16[2,32,1792]{2,1,0:T(8,128)(2,1)S(1)}, bf16[2,32,1792]{2,1,0:T(8,128)(2,1)S(1)}, u32[]{:S(2)}, u32[]{:S(2)}) collective-permute-start(bf16[2,32,1792]{2,1,0:T(8,128)(2,1)S(1)} %get-tuple-element.54.refs_3_.refs_0_), channel_id=1, source_target_pairs={{0,8},{8,0},{1,9},{9,1},{2,10},{10,2},{3,11},{11,3},{4,12},{12,4},... | collective-permute-start | bytes 688136 | tf_op jit(solution)/shard_map/ppermute | solution.py:22
  77.6 14.7 %collective-permute-start.35 = (bf16[512,256]{1,0:T(8,128)(2,1)S(1)}, bf16[512,256]{1,0:T(8,128)(2,1)S(1)}, u32[]{:S(2)}, u32[]{:S(2)}) collective-permute-start(bf16[512,256]{1,0:T(8,128)(2,1)S(1)} %get-tuple-element.69), channel_id=1, source_target_pairs={{0,2},{2,4},{4,6},{6,0},{1,3},{3,5},{5,7},{7,1},{8,10},{10,12},{12... | collective-permute-start | bytes 786440 | tf_op jit(solution)/shard_map/ppermute | solution.py:22
  79.2 15.3 %collective-permute-start.36 = (bf16[512,256]{1,0:T(8,128)(2,1)S(1)}, bf16[512,256]{1,0:T(8,128)(2,1)S(1)}, u32[]{:S(2)}, u32[]{:S(2)}) collective-permute-start(bf16[512,256]{1,0:T(8,128)(2,1)S(1)} %get-tuple-element.70), channel_id=1, source_target_pairs={{0,4},{2,6},{4,0},{6,2},{1,5},{3,7},{5,1},{7,3},{8,12},{10,14},{12... | collective-permute-start | bytes 786440 | tf_op jit(solution)/shard_map/ppermute | solution.py:22
  91.8 13.7 %collective-permute-start.18 = (bf16[512,256]{1,0:T(8,128)(2,1)S(1)}, bf16[512,256]{1,0:T(8,128)(2,1)S(1)}, u32[]{:S(2)}, u32[]{:S(2)}) collective-permute-start(bf16[512,256]{1,0:T(8,128)(2,1)S(1)} %get-tuple-element.58), channel_id=1, source_target_pairs={{0,4},{2,6},{4,0},{6,2},{1,5},{3,7},{5,1},{7,3},{8,12},{10,14},{12... | collective-permute-start | bytes 786440 | tf_op jit(solution)/shard_map/ppermute | solution.py:22
  92.3 13.4 %collective-permute-start.19 = (bf16[512,256]{1,0:T(8,128)(2,1)S(1)}, bf16[512,256]{1,0:T(8,128)(2,1)S(1)}, u32[]{:S(2)}, u32[]{:S(2)}) collective-permute-start(bf16[512,256]{1,0:T(8,128)(2,1)S(1)} %get-tuple-element.59), channel_id=1, source_target_pairs={{0,6},{2,0},{4,2},{6,4},{1,7},{3,1},{5,3},{7,5},{8,14},{10,8},{12,... | collective-permute-start | bytes 786440 | tf_op jit(solution)/shard_map/ppermute | solution.py:22
  95.2 14.1 %collective-permute-start.38 = (bf16[512,256]{1,0:T(8,128)(2,1)S(1)}, bf16[512,256]{1,0:T(8,128)(2,1)S(1)}, u32[]{:S(2)}, u32[]{:S(2)}) collective-permute-start(bf16[512,256]{1,0:T(8,128)(2,1)S(1)} %sum_z.3.refs_0_), channel_id=1, source_target_pairs={{0,1},{1,0},{2,3},{3,2},{4,5},{5,4},{6,7},{7,6},{8,9},{9,8},{10,11... | collective-permute-start | bytes 786440 | tf_op jit(solution)/shard_map/ppermute | solution.py:22
  98.0 25.3 %collective-permute-start = (bf16[512,512]{1,0:T(8,128)(2,1)S(1)}, bf16[512,512]{1,0:T(8,128)(2,1)S(1)}, u32[]{:S(2)}, u32[]{:S(2)}) collective-permute-start(bf16[512,512]{1,0:T(8,128)(2,1)S(1)} %constant_dynamic-slice_fusion), channel_id=1, source_target_pairs={{0,64},{64,0},{1,65},{65,1},{2,66},{66,2},{3,67},{67,3},{4,68},{68... | collective-permute-start | bytes 1572872 | tf_op jit(solution)/shard_map/ppermute | solution.py:22
  106.4 13.3 %collective-permute-start.20 = (bf16[512,256]{1,0:T(8,128)(2,1)S(1)}, bf16[512,256]{1,0:T(8,128)(2,1)S(1)}, u32[]{:S(2)}, u32[]{:S(2)}) collective-permute-start(bf16[512,256]{1,0:T(8,128)(2,1)S(1)} %sum_z.2.refs_0_), channel_id=1, source_target_pairs={{0,1},{1,0},{2,3},{3,2},{4,5},{5,4},{6,7},{7,6},{8,9},{9,8},{10,11... | collective-permute-start | bytes 786440 | tf_op jit(solution)/shard_map/ppermute | solution.py:22
  109.9 15.3 %collective-permute-start.41 = (bf16[512,256]{1,0:T(8,128)(2,1)S(1)}, bf16[512,256]{1,0:T(8,128)(2,1)S(1)}, u32[]{:S(2)}, u32[]{:S(2)}) collective-permute-start(bf16[512,256]{1,0:T(8,128)(2,1)S(1)} %residual.3.refs_0_), channel_id=1, source_target_pairs={{0,2},{2,4},{4,6},{6,0},{1,3},{3,5},{5,7},{7,1},{8,10},{10,12},{12... | collective-permute-start | bytes 786440 | tf_op jit(solution)/shard_map/ppermute | solution.py:22
  111.7 15.1 %collective-permute-start.40 = (bf16[512,256]{1,0:T(8,128)(2,1)S(1)}, bf16[512,256]{1,0:T(8,128)(2,1)S(1)}, u32[]{:S(2)}, u32[]{:S(2)}) collective-permute-start(bf16[512,256]{1,0:T(8,128)(2,1)S(1)} %residual.3.refs_0_), channel_id=1, source_target_pairs={{0,4},{2,6},{4,0},{6,2},{1,5},{3,7},{5,1},{7,3},{8,12},{10,14},{12... | collective-permute-start | bytes 786440 | tf_op jit(solution)/shard_map/ppermute | solution.py:22
  114.5 12.3 %collective-permute-start.39 = (bf16[512,256]{1,0:T(8,128)(2,1)S(1)}, bf16[512,256]{1,0:T(8,128)(2,1)S(1)}, u32[]{:S(2)}, u32[]{:S(2)}) collective-permute-start(bf16[512,256]{1,0:T(8,128)(2,1)S(1)} %residual.3.refs_0_), channel_id=1, source_target_pairs={{0,6},{2,0},{4,2},{6,4},{1,7},{3,1},{5,3},{7,5},{8,14},{10,8},{12,... | collective-permute-start | bytes 786440 | tf_op jit(solution)/shard_map/ppermute | solution.py:22
  120.3 12.5 %collective-permute-start.23 = (bf16[512,256]{1,0:T(8,128)(2,1)S(1)}, bf16[512,256]{1,0:T(8,128)(2,1)S(1)}, u32[]{:S(2)}, u32[]{:S(2)}) collective-permute-start(bf16[512,256]{1,0:T(8,128)(2,1)S(1)} %residual.2.refs_0_), channel_id=1, source_target_pairs={{0,2},{2,4},{4,6},{6,0},{1,3},{3,5},{5,7},{7,1},{8,10},{10,12},{12... | collective-permute-start | bytes 786440 | tf_op jit(solution)/shard_map/ppermute | solution.py:22
  123.4 13.6 %collective-permute-start.22 = (bf16[512,256]{1,0:T(8,128)(2,1)S(1)}, bf16[512,256]{1,0:T(8,128)(2,1)S(1)}, u32[]{:S(2)}, u32[]{:S(2)}) collective-permute-start(bf16[512,256]{1,0:T(8,128)(2,1)S(1)} %residual.2.refs_0_), channel_id=1, source_target_pairs={{0,4},{2,6},{4,0},{6,2},{1,5},{3,7},{5,1},{7,3},{8,12},{10,14},{12... | collective-permute-start | bytes 786440 | tf_op jit(solution)/shard_map/ppermute | solution.py:22
  144.0 13.3 %collective-permute-start.44 = (bf16[2,32,1792]{2,1,0:T(8,128)(2,1)S(1)}, bf16[2,32,1792]{2,1,0:T(8,128)(2,1)S(1)}, u32[]{:S(2)}, u32[]{:S(2)}) collective-permute-start(bf16[2,32,1792]{2,1,0:T(8,128)(2,1)S(1)} %get-tuple-element.76), channel_id=1, source_target_pairs={{0,32},{16,48},{32,0},{48,16},{1,33},{17,49},{33,1},{49,17},{2,34}... | collective-permute-start | bytes 688136 | tf_op jit(solution)/shard_map/ppermute | solution.py:22
  147.5 14.3 %collective-permute-start.25 = (bf16[2,32,1792]{2,1,0:T(8,128)(2,1)S(1)}, bf16[2,32,1792]{2,1,0:T(8,128)(2,1)S(1)}, u32[]{:S(2)}, u32[]{:S(2)}) collective-permute-start(bf16[2,32,1792]{2,1,0:T(8,128)(2,1)S(1)} %get-tuple-element.63), channel_id=1, source_target_pairs={{0,16},{16,32},{32,48},{48,0},{1,17},{17,33},{33,49},{49,1},{2,18}... | collective-permute-start | bytes 688136 | tf_op jit(solution)/shard_map/ppermute | solution.py:22
  149.0 18.2 %collective-permute-start.26 = (bf16[2,32,1792]{2,1,0:T(8,128)(2,1)S(1)}, bf16[2,32,1792]{2,1,0:T(8,128)(2,1)S(1)}, u32[]{:S(2)}, u32[]{:S(2)}) collective-permute-start(bf16[2,32,1792]{2,1,0:T(8,128)(2,1)S(1)} %get-tuple-element.64), channel_id=1, source_target_pairs={{0,32},{16,48},{32,0},{48,16},{1,33},{17,49},{33,1},{49,17},{2,34}... | collective-permute-start | bytes 688136 | tf_op jit(solution)/shard_map/ppermute | solution.py:22
  152.0 15.2 %collective-permute-start.27 = (bf16[2,32,1792]{2,1,0:T(8,128)(2,1)S(1)}, bf16[2,32,1792]{2,1,0:T(8,128)(2,1)S(1)}, u32[]{:S(2)}, u32[]{:S(2)}) collective-permute-start(bf16[2,32,1792]{2,1,0:T(8,128)(2,1)S(1)} %get-tuple-element.65), channel_id=1, source_target_pairs={{0,48},{16,0},{32,16},{48,32},{1,49},{17,1},{33,17},{49,33},{2,50}... | collective-permute-start | bytes 688136 | tf_op jit(solution)/shard_map/ppermute | solution.py:22
  167.9 12.6 %collective-permute-start.49 = (bf16[2,64,1792]{2,1,0:T(8,128)(2,1)S(1)}, bf16[2,64,1792]{2,1,0:T(8,128)(2,1)S(1)}, u32[]{:S(2)}, u32[]{:S(2)}) collective-permute-start(bf16[2,64,1792]{2,1,0:T(8,128)(2,1)S(1)} %errors.3.refs_1_), channel_id=1, source_target_pairs={{0,16},{16,32},{32,48},{48,0},{1,17},{17,33},{33,49},{49,1},{2,18}... | collective-permute-start | bytes 1376264 | tf_op jit(solution)/shard_map/ppermute | solution.py:22
  168.9 20.9 %collective-permute-start.51 = (bf16[2,64,1792]{2,1,0:T(8,128)(2,1)S(1)}, bf16[2,64,1792]{2,1,0:T(8,128)(2,1)S(1)}, u32[]{:S(2)}, u32[]{:S(2)}) collective-permute-start(bf16[2,64,1792]{2,1,0:T(8,128)(2,1)S(1)} %errors.3.refs_1_), channel_id=1, source_target_pairs={{0,8},{8,0},{1,9},{9,1},{2,10},{10,2},{3,11},{11,3},{4,12},{12,4},... | collective-permute-start | bytes 1376264 | tf_op jit(solution)/shard_map/ppermute | solution.py:22
  169.7 12.2 %collective-permute-start.47 = (bf16[2,64,1792]{2,1,0:T(8,128)(2,1)S(1)}, bf16[2,64,1792]{2,1,0:T(8,128)(2,1)S(1)}, u32[]{:S(2)}, u32[]{:S(2)}) collective-permute-start(bf16[2,64,1792]{2,1,0:T(8,128)(2,1)S(1)} %errors.3.refs_1_), channel_id=1, source_target_pairs={{0,48},{16,0},{32,16},{48,32},{1,49},{17,1},{33,17},{49,33},{2,50}... | collective-permute-start | bytes 1376264 | tf_op jit(solution)/shard_map/ppermute | solution.py:22
  172.0 18.4 %collective-permute-start.46 = (bf16[2,64,1792]{2,1,0:T(8,128)(2,1)S(1)}, bf16[2,64,1792]{2,1,0:T(8,128)(2,1)S(1)}, u32[]{:S(2)}, u32[]{:S(2)}) collective-permute-start(bf16[2,64,1792]{2,1,0:T(8,128)(2,1)S(1)} %errors.3.refs_1_), channel_id=1, source_target_pairs={{0,64},{64,0},{1,65},{65,1},{2,66},{66,2},{3,67},{67,3},{4,68},{68... | collective-permute-start | bytes 1376264 | tf_op jit(solution)/shard_map/ppermute | solution.py:22
  185.4 12.5 %collective-permute-start.55 = (bf16[2,64,1792]{2,1,0:T(8,128)(2,1)S(1)}, bf16[2,64,1792]{2,1,0:T(8,128)(2,1)S(1)}, u32[]{:S(2)}, u32[]{:S(2)}) collective-permute-start(bf16[2,64,1792]{2,1,0:T(8,128)(2,1)S(1)} %collective-permute-done.49.refs_5_), channel_id=1, source_target_pairs={{0,8},{8,0},{1,9},{9,1},{2,10},{10,2},{3,11},{11,3},{4,12},{12,4},... | collective-permute-start | bytes 1376264 | tf_op jit(solution)/shard_map/ppermute | solution.py:22
  190.4 13.0 %collective-permute-start.50 = (bf16[2,64,1792]{2,1,0:T(8,128)(2,1)S(1)}, bf16[2,64,1792]{2,1,0:T(8,128)(2,1)S(1)}, u32[]{:S(2)}, u32[]{:S(2)}) collective-permute-start(bf16[2,64,1792]{2,1,0:T(8,128)(2,1)S(1)} %collective-permute-done.46.refs_2_), channel_id=1, source_target_pairs={{0,16},{16,32},{32,48},{48,0},{1,17},{17,33},{33,49},{49,1},{2,18}... | collective-permute-start | bytes 1376264 | tf_op jit(solution)/shard_map/ppermute | solution.py:22
  190.4 14.1 %collective-permute-start.48 = (bf16[2,64,1792]{2,1,0:T(8,128)(2,1)S(1)}, bf16[2,64,1792]{2,1,0:T(8,128)(2,1)S(1)}, u32[]{:S(2)}, u32[]{:S(2)}) collective-permute-start(bf16[2,64,1792]{2,1,0:T(8,128)(2,1)S(1)} %collective-permute-done.46.refs_2_), channel_id=1, source_target_pairs={{0,48},{16,0},{32,16},{48,32},{1,49},{17,1},{33,17},{49,33},{2,50}... | collective-permute-start | bytes 1376264 | tf_op jit(solution)/shard_map/ppermute | solution.py:22
  (45 other events, 436.7 us)

commit v3 on v2

--- a/solution.py
+++ b/solution.py
@@ -10,6 +10,7 @@
 
 D = 8192
 TILE = 256
+WIDE = 1792
 BF = jnp.bfloat16
 F32 = jnp.float32
 NY = 4
@@ -84,11 +85,11 @@
     def body(ids, t_ref, w_ref, own_ref, other_ref):
         def step(at):
             acc = jnp.dot(t_ref[...], w_ref[:, at], preferred_element_type=F32).astype(BF)
-            acc = acc.reshape(2, NY, rows, TILE)
+            acc = acc.reshape(2, NY, rows, WIDE)
             own_ref[:, :, at] = acc[0]
             other_ref[:, :, at] = acc[1]
 
-        loop_tiles(cols, TILE, step)
+        loop_tiles(cols, WIDE, step)
 
     out = shape((NY, rows, cols))
     return call(
@@ -171,10 +172,9 @@
 
 def ring_pair(near, far):
     near_low, near_high = shift(near, "y", 1), shift(near, "y", -1)
+    across = shift(near_high, "y", -1)
     far_low, far_high = shift(far, "y", 1), shift(far, "y", -1)
-    across = [shift(near_low[0], "y", 1), shift(near_high[1], "y", -1)]
-    beyond = [shift(v, "dp", 1) for v in across]
-    return [near, far, near_high, far_high, near_low, far_low], across + beyond
+    return [near, far, near_high, far_high, near_low, far_low], [across, shift(across, "dp", 1)]
 
 
 def down_products(ids, pieces, down):
@@ -246,22 +246,22 @@
         f_refs, d_ref, own_ref, other_ref = refs[:NZ], refs[NZ], refs[NZ + 1], refs[NZ + 2]
 
         def step(at):
-            acc = jnp.zeros((total, TILE), F32)
+            acc = jnp.zeros((total, WIDE), F32)
             for k, f_ref in enumerate(f_refs):
                 to = pl.multiple_of(lax.rem(ids[3] + k, NZ) * tile_k, tile_k)
                 acc += lax.dot_general(
                     f_ref[...], d_ref[at, pl.ds(to, tile_k)], (((1,), (1,)), ((), ())),
                     preferred_element_type=F32,
                 )
-            acc = acc.astype(BF).reshape(2, NY, 2, rows, TILE)
+            acc = acc.astype(BF).reshape(2, NY, 2, rows, WIDE)
             own_ref[:, :, :, at] = acc[0]
             other_ref[:, :, :, at] = acc[1]
 
-        loop_tiles(cols, TILE, step)
+        loop_tiles(cols, WIDE, step)
 
     out = shape((NY, 2, rows, cols))
     return call(
-        body, ids, (*parts, down), [out, out], flops=2 * total * width * cols, limit=12, after=after)
+        body, ids, (*parts, down), [out, out], flops=2 * total * width * cols, limit=16, after=after)
 
 
 def split_back(ids, own, recv):
@@ -340,19 +340,19 @@
         probe_rows = pl.ds(pl.multiple_of(ids[0] * out_rows, out_rows), out_rows)
 
         def step(at):
-            err = jnp.concatenate([p[0, :, at] for p in p_refs] + [p[:, at] for p in refs[n:m:2]], axis=0)
+            err = jnp.concatenate([p[0, :, at] for p in p_refs] + [p[0, :, at] for p in refs[n:m]], axis=0)
             g = jnp.dot(l_ref[...], err, preferred_element_type=F32) * token_scale
             g_ref[:, at] = g.astype(BF)
-            err = jnp.concatenate([p[1, :, at] for p in p_refs] + [p[:, at] for p in refs[n + 1:m:2]], axis=0)
+            err = jnp.concatenate([p[1, :, at] for p in p_refs] + [p[1, :, at] for p in refs[n:m]], axis=0)
             hv = jnp.dot(l_ref[...], err, preferred_element_type=F32) * token_scale
             h_ref[:, at] = (probe_ref[probe_rows, at].astype(F32) * hv * inv_width).astype(BF)
 
-        loop_tiles(cols, TILE, step)
+        loop_tiles(cols, WIDE, step)
 
     out = shape((out_rows, cols))
     return call(
         body, ids, (lhs, *pieces, *halves, probe), [out, out],
-        flops=4 * out_rows * count * cols, limit=12,
+        flops=4 * out_rows * count * cols, limit=16,
     )
 
 

time: 215 us -> 208 us (0.967)
  Pallas kernels: 43.6 us -> 36.8 us
    pallas_call x21, Pallas kernels: 43.6 us -> 36.8 us  [call(): pl.pallas_call(kernel, out_shape=tuple(outs), in_specs=[pl.BlockSpec(memo...]
    ppermute x65 -> x61, starting transfers between devices: 83.1 us -> 84.8 us  [shift(): lax.ppermute(value, axis, [(i, (i + step) % size) for i in range(size)])]
    ppermute x65 -> x61, waiting for transfers between devices: 79.7 us -> 78.2 us  [shift(): lax.ppermute(value, axis, [(i, (i + step) % size) for i in range(size)])]
  transfers between devices with their start and end apart: 65 -> 61, of which waited for: 26 -> 25; matrix products, arithmetic and copies ran while one was open for 0% -> 0% of each run, Pallas kernels for 14% -> 12%
where the time goes in v3:
time: 208 us
  starting transfers between devices  84.8 us (41%)
  waiting for transfers between devices  78.2 us (38%)
  Pallas kernels  36.8 us (18%)
  local copies, waits for them, and re-layouts  7.22 us (3%)
    ppermute x61, starting transfers between devices, shift(): lax.ppermute(value, axis, [(i, (i + step) % size) for i in range(size)])  84.8 us
    ppermute x61, waiting for transfers between devices, shift(): lax.ppermute(value, axis, [(i, (i + step) % size) for i in range(size)])  78.2 us
    pallas_call x21, Pallas kernels, call(): pl.pallas_call(kernel, out_shape=tuple(outs), in_specs=[pl.BlockSpec(memo...  36.8 us
    unnamed x24, local copies, waits for them, and re-layouts  7.1 us
  transfers between devices with their start and end apart: 61, of which 25 were waited for; matrix products, arithmetic and copies ran while one was open for 0% of the time, Pallas kernels for 12%

profile of v3, /device:TPU:1, one launch (start us, length us, event | category | flops | bytes accessed | tf_op | source)
XLA Modules:
  0.0 208.2 jit_solution(1285162396233873414)
XLA Ops:
  8.7 2.6 %pre_products.3 = (bf16[4,64,1792]{2,1,0:T(8,128)(2,1)S(1)}, bf16[4,64,1792]{2,1,0:T(8,128)(2,1)S(1)}) custom-call(s32[5]{0:T(128)S(1)} %stack.23.ids, bf16[512,1024]{1,0:T(8,128)(2,1)S(1)} %ordered_tokens.1.refs_0_, bf16[1024,1792]{1,0:T(8,128)(2,1)S(1)} %copy-done.3), custom_call_target="tpu_custom_call" | custom-call | flops 1879048192 | bytes 6553600 | tf_op jit(solution)/shard_map/pre_products/pallas_call | solution.py:44
  20.9 2.7 %collective-permute-start.9 = (bf16[3,32,1792]{2,1,0:T(8,128)(2,1)S(1)}, bf16[3,32,1792]{2,1,0:T(8,128)(2,1)S(1)}, u32[]{:S(2)}, u32[]{:S(2)}) collective-permute-start(bf16[3,32,1792]{2,1,0:T(8,128)(2,1)S(1)} %get-tuple-element.53), channel_id=1, source_target_pairs={{0,48},{16,0},{32,16},{48,32},{1,49},{17,1},{33,17},{49,33},{2,50}... | collective-permute-start | bytes 1032200 | tf_op jit(solution)/shard_map/ppermute | solution.py:23
  23.6 5.2 %collective-permute-done.7 = bf16[3,32,1792]{2,1,0:T(8,128)(2,1)S(1)} collective-permute-done((bf16[3,32,1792]{2,1,0:T(8,128)(2,1)S(1)}, bf16[3,32,1792]{2,1,0:T(8,128)(2,1)S(1)}, u32[]{:S(2)}, u32[]{:S(2)}) %collective-permute-start.7) | collective-permute-done | bytes 344096 | tf_op jit(solution)/shard_map/ppermute | solution.py:23
  29.1 2.7 %collective-permute-start.5 = (bf16[3,32,1792]{2,1,0:T(8,128)(2,1)S(1)}, bf16[3,32,1792]{2,1,0:T(8,128)(2,1)S(1)}, u32[]{:S(2)}, u32[]{:S(2)}) collective-permute-start(bf16[3,32,1792]{2,1,0:T(8,128)(2,1)S(1)} %add_convert_fusion.1), channel_id=1, source_target_pairs={{0,48},{16,0},{32,16},{48,32},{1,49},{17,1},{33,17},{49,33},{2,50}... | collective-permute-start | bytes 1032200 | tf_op jit(solution)/shard_map/ppermute | solution.py:23
  31.8 3.9 %collective-permute-done.9.refs_2_ = bf16[3,32,1792]{2,1,0:T(8,128)(2,1)S(1)} collective-permute-done((bf16[3,32,1792]{2,1,0:T(8,128)(2,1)S(1)}, bf16[3,32,1792]{2,1,0:T(8,128)(2,1)S(1)}, u32[]{:S(2)}, u32[]{:S(2)}) %collective-permute-start.9) | collective-permute-done | bytes 344096 | tf_op jit(solution)/shard_map/ppermute | solution.py:23
  35.7 7.8 %collective-permute-done.8.refs_1_ = bf16[3,32,1792]{2,1,0:T(8,128)(2,1)S(1)} collective-permute-done((bf16[3,32,1792]{2,1,0:T(8,128)(2,1)S(1)}, bf16[3,32,1792]{2,1,0:T(8,128)(2,1)S(1)}, u32[]{:S(2)}, u32[]{:S(2)}) %collective-permute-start.8) | collective-permute-done | bytes 344096 | tf_op jit(solution)/shard_map/ppermute | solution.py:23
  45.4 2.8 %collective-permute-start.11 = (bf16[2,32,1792]{2,1,0:T(8,128)(2,1)S(1)}, bf16[2,32,1792]{2,1,0:T(8,128)(2,1)S(1)}, u32[]{:S(2)}, u32[]{:S(2)}) collective-permute-start(bf16[2,32,1792]{2,1,0:T(8,128)(2,1)S(1)} %get-tuple-element.55.refs_0_), channel_id=1, source_target_pairs={{0,32},{16,48},{32,0},{48,16},{1,33},{17,49},{33,1},{49,17},{2,34}... | collective-permute-start | bytes 688136 | tf_op jit(solution)/shard_map/ppermute | solution.py:23
  52.8 4.7 %collective-permute-done.11.refs_2_ = bf16[2,32,1792]{2,1,0:T(8,128)(2,1)S(1)} collective-permute-done((bf16[2,32,1792]{2,1,0:T(8,128)(2,1)S(1)}, bf16[2,32,1792]{2,1,0:T(8,128)(2,1)S(1)}, u32[]{:S(2)}, u32[]{:S(2)}) %collective-permute-start.11) | collective-permute-done | bytes 229408 | tf_op jit(solution)/shard_map/ppermute | solution.py:23
  57.5 4.0 %collective-permute-start.31 = (bf16[2,32,1792]{2,1,0:T(8,128)(2,1)S(1)}, bf16[2,32,1792]{2,1,0:T(8,128)(2,1)S(1)}, u32[]{:S(2)}, u32[]{:S(2)}) collective-permute-start(bf16[2,32,1792]{2,1,0:T(8,128)(2,1)S(1)} %get-tuple-element.54.refs_3_.refs_0_), channel_id=1, source_target_pairs={{0,8},{8,0},{1,9},{9,1},{2,10},{10,2},{3,11},{11,3},{4,12},{12,4},... | collective-permute-start | bytes 688136 | tf_op jit(solution)/shard_map/ppermute | solution.py:23
  62.5 3.6 %collective-permute-start.34 = (bf16[2,32,1792]{2,1,0:T(8,128)(2,1)S(1)}, bf16[2,32,1792]{2,1,0:T(8,128)(2,1)S(1)}, u32[]{:S(2)}, u32[]{:S(2)}) collective-permute-start(bf16[2,32,1792]{2,1,0:T(8,128)(2,1)S(1)} %collective-permute-done.30.refs_3_), channel_id=1, source_target_pairs={{0,8},{8,0},{1,9},{9,1},{2,10},{10,2},{3,11},{11,3},{4,12},{12,4},... | collective-permute-start | bytes 688136 | tf_op jit(solution)/shard_map/ppermute | solution.py:23
  71.0 3.4 %down_products.3 = (bf16[512,256]{1,0:T(8,128)(2,1)S(1)}, bf16[512,256]{1,0:T(8,128)(2,1)S(1)}, bf16[512,256]{1,0:T(8,128)(2,1)S(1)}, bf16[512,256]{1,0:T(8,128)(2,1)S(1)}) custom-call(s32[5]{0:T(128)S(1)} %stack.23.ids, bf16[2,32,1792]{2,1,0:T(8,128)(2,1)S(1)} %get-tuple-element.54.refs_3_.refs_0_, ...), custom_call_target="tpu_custom_call" | custom-call | flops 1879048192 | bytes 6553600 | tf_op jit(solution)/shard_map/down_products/pallas_call | solution.py:44
  76.1 3.3 %collective-permute-start.36 = (bf16[512,256]{1,0:T(8,128)(2,1)S(1)}, bf16[512,256]{1,0:T(8,128)(2,1)S(1)}, u32[]{:S(2)}, u32[]{:S(2)}) collective-permute-start(bf16[512,256]{1,0:T(8,128)(2,1)S(1)} %get-tuple-element.70), channel_id=1, source_target_pairs={{0,4},{2,6},{4,0},{6,2},{1,5},{3,7},{5,1},{7,3},{8,12},{10,14},{12... | collective-permute-start | bytes 786440 | tf_op jit(solution)/shard_map/ppermute | solution.py:23
  83.9 3.9 %down_products.2 = (bf16[512,256]{1,0:T(8,128)(2,1)S(1)}, bf16[512,256]{1,0:T(8,128)(2,1)S(1)}, bf16[512,256]{1,0:T(8,128)(2,1)S(1)}, bf16[512,256]{1,0:T(8,128)(2,1)S(1)}) custom-call(s32[5]{0:T(128)S(1)} %stack.23.ids, bf16[2,32,1792]{2,1,0:T(8,128)(2,1)S(1)} %get-tuple-element.55.refs_0_, bf16[2,32,1792]{2,1,0:T(8,128)(2,1)S(1)} %collective-permute-done.10.refs_1_, ...), custom_call_target="tpu_custom_call" | custom-call | flops 1879048192 | bytes 6553600 | tf_op jit(solution)/shard_map/down_products/pallas_call | solution.py:44
  91.9 2.8 %collective-permute-start.38 = (bf16[512,256]{1,0:T(8,128)(2,1)S(1)}, bf16[512,256]{1,0:T(8,128)(2,1)S(1)}, u32[]{:S(2)}, u32[]{:S(2)}) collective-permute-start(bf16[512,256]{1,0:T(8,128)(2,1)S(1)} %sum_z.3.refs_0_), channel_id=1, source_target_pairs={{0,1},{1,0},{2,3},{3,2},{4,5},{5,4},{6,7},{7,6},{8,9},{9,8},{10,11... | collective-permute-start | bytes 786440 | tf_op jit(solution)/shard_map/ppermute | solution.py:23
  96.5 5.9 %collective-permute-done.18.refs_2_ = bf16[512,256]{1,0:T(8,128)(2,1)S(1)} collective-permute-done((bf16[512,256]{1,0:T(8,128)(2,1)S(1)}, bf16[512,256]{1,0:T(8,128)(2,1)S(1)}, u32[]{:S(2)}, u32[]{:S(2)}) %collective-permute-start.18) | collective-permute-done | bytes 262176 | tf_op jit(solution)/shard_map/ppermute | solution.py:23
  103.2 2.8 %collective-permute-start.20 = (bf16[512,256]{1,0:T(8,128)(2,1)S(1)}, bf16[512,256]{1,0:T(8,128)(2,1)S(1)}, u32[]{:S(2)}, u32[]{:S(2)}) collective-permute-start(bf16[512,256]{1,0:T(8,128)(2,1)S(1)} %sum_z.2.refs_0_), channel_id=1, source_target_pairs={{0,1},{1,0},{2,3},{3,2},{4,5},{5,4},{6,7},{7,6},{8,9},{9,8},{10,11... | collective-permute-start | bytes 786440 | tf_op jit(solution)/shard_map/ppermute | solution.py:23
  108.5 2.8 %collective-permute-start.40 = (bf16[512,256]{1,0:T(8,128)(2,1)S(1)}, bf16[512,256]{1,0:T(8,128)(2,1)S(1)}, u32[]{:S(2)}, u32[]{:S(2)}) collective-permute-start(bf16[512,256]{1,0:T(8,128)(2,1)S(1)} %residual.3.refs_0_), channel_id=1, source_target_pairs={{0,4},{2,6},{4,0},{6,2},{1,5},{3,7},{5,1},{7,3},{8,12},{10,14},{12... | collective-permute-start | bytes 786440 | tf_op jit(solution)/shard_map/ppermute | solution.py:23
  111.4 4.9 %collective-permute-done.20.refs_1_ = bf16[512,256]{1,0:T(8,128)(2,1)S(1)} collective-permute-done((bf16[512,256]{1,0:T(8,128)(2,1)S(1)}, bf16[512,256]{1,0:T(8,128)(2,1)S(1)}, u32[]{:S(2)}, u32[]{:S(2)}) %collective-permute-start.20) | collective-permute-done | bytes 262176 | tf_op jit(solution)/shard_map/ppermute | solution.py:23
  116.9 3.2 %collective-permute-start.23 = (bf16[512,256]{1,0:T(8,128)(2,1)S(1)}, bf16[512,256]{1,0:T(8,128)(2,1)S(1)}, u32[]{:S(2)}, u32[]{:S(2)}) collective-permute-start(bf16[512,256]{1,0:T(8,128)(2,1)S(1)} %residual.2.refs_0_), channel_id=1, source_target_pairs={{0,2},{2,4},{4,6},{6,0},{1,3},{3,5},{5,7},{7,1},{8,10},{10,12},{12... | collective-permute-start | bytes 786440 | tf_op jit(solution)/shard_map/ppermute | solution.py:23
  123.6 2.8 %back_products.3 = (bf16[4,2,32,1792]{3,2,1,0:T(8,128)(2,1)S(1)}, bf16[4,2,32,1792]{3,2,1,0:T(8,128)(2,1)S(1)}) custom-call(s32[5]{0:T(128)S(1)} %stack.23.ids, bf16[512,256]{1,0:T(8,128)(2,1)S(1)} %residual.3.refs_0_, bf16[512,256]{1,0:T(8,128)(2,1)S(1)} %collective-permute-done.39.refs_1_, bf16[512,256]{1,0:T(8,128)(2,1)S(1)} %collective-permute-done.40.refs_2_, ...), custom_call_target="tpu_custom_call" | custom-call | flops 1879048192 | bytes 6553600 | tf_op jit(solution)/shard_map/back_products/pallas_call | solution.py:44
  129.8 4.0 %collective-permute-done.22.refs_2_ = bf16[512,256]{1,0:T(8,128)(2,1)S(1)} collective-permute-done((bf16[512,256]{1,0:T(8,128)(2,1)S(1)}, bf16[512,256]{1,0:T(8,128)(2,1)S(1)}, u32[]{:S(2)}, u32[]{:S(2)}) %collective-permute-start.22) | collective-permute-done | bytes 262176 | tf_op jit(solution)/shard_map/ppermute | solution.py:23
  133.8 2.8 %back_products.2 = (bf16[4,2,32,1792]{3,2,1,0:T(8,128)(2,1)S(1)}, bf16[4,2,32,1792]{3,2,1,0:T(8,128)(2,1)S(1)}) custom-call(s32[5]{0:T(128)S(1)} %stack.23.ids, bf16[512,256]{1,0:T(8,128)(2,1)S(1)} %residual.2.refs_0_, bf16[512,256]{1,0:T(8,128)(2,1)S(1)} %collective-permute-done.21.refs_1_, bf16[512,256]{1,0:T(8,128)(2,1)S(1)} %collective-permute-done.22.refs_2_, ...), custom_call_target="tpu_custom_call" | custom-call | flops 1879048192 | bytes 6553600 | tf_op jit(solution)/shard_map/back_products/pallas_call | solution.py:44
  148.5 4.7 %collective-permute-done.44.refs_2_ = bf16[2,32,1792]{2,1,0:T(8,128)(2,1)S(1)} collective-permute-done((bf16[2,32,1792]{2,1,0:T(8,128)(2,1)S(1)}, bf16[2,32,1792]{2,1,0:T(8,128)(2,1)S(1)}, u32[]{:S(2)}, u32[]{:S(2)}) %collective-permute-start.44) | collective-permute-done | bytes 229408 | tf_op jit(solution)/shard_map/ppermute | solution.py:23
  153.9 3.5 %collective-permute-done.25.refs_1_ = bf16[2,32,1792]{2,1,0:T(8,128)(2,1)S(1)} collective-permute-done((bf16[2,32,1792]{2,1,0:T(8,128)(2,1)S(1)}, bf16[2,32,1792]{2,1,0:T(8,128)(2,1)S(1)}, u32[]{:S(2)}, u32[]{:S(2)}) %collective-permute-start.25) | collective-permute-done | bytes 229408 | tf_op jit(solution)/shard_map/ppermute | solution.py:23
  157.4 5.5 %collective-permute-done.26.refs_2_ = bf16[2,32,1792]{2,1,0:T(8,128)(2,1)S(1)} collective-permute-done((bf16[2,32,1792]{2,1,0:T(8,128)(2,1)S(1)}, bf16[2,32,1792]{2,1,0:T(8,128)(2,1)S(1)}, u32[]{:S(2)}, u32[]{:S(2)}) %collective-permute-start.26) | collective-permute-done | bytes 229408 | tf_op jit(solution)/shard_map/ppermute | solution.py:23
  163.7 2.7 %collective-permute-start.47 = (bf16[2,64,1792]{2,1,0:T(8,128)(2,1)S(1)}, bf16[2,64,1792]{2,1,0:T(8,128)(2,1)S(1)}, u32[]{:S(2)}, u32[]{:S(2)}) collective-permute-start(bf16[2,64,1792]{2,1,0:T(8,128)(2,1)S(1)} %errors.3.refs_1_), channel_id=1, source_target_pairs={{0,48},{16,0},{32,16},{48,32},{1,49},{17,1},{33,17},{49,33},{2,50}... | collective-permute-start | bytes 1376264 | tf_op jit(solution)/shard_map/ppermute | solution.py:23
  168.2 7.7 %collective-permute-done.47.refs_3_ = bf16[2,64,1792]{2,1,0:T(8,128)(2,1)S(1)} collective-permute-done((bf16[2,64,1792]{2,1,0:T(8,128)(2,1)S(1)}, bf16[2,64,1792]{2,1,0:T(8,128)(2,1)S(1)}, u32[]{:S(2)}, u32[]{:S(2)}) %collective-permute-start.47) | collective-permute-done | bytes 458784 | tf_op jit(solution)/shard_map/ppermute | solution.py:23
  175.9 3.4 %collective-permute-start.57 = (bf16[2,64,1792]{2,1,0:T(8,128)(2,1)S(1)}, bf16[2,64,1792]{2,1,0:T(8,128)(2,1)S(1)}, u32[]{:S(2)}, u32[]{:S(2)}) collective-permute-start(bf16[2,64,1792]{2,1,0:T(8,128)(2,1)S(1)} %collective-permute-done.47.refs_3_), channel_id=1, source_target_pairs={{0,48},{16,0},{32,16},{48,32},{1,49},{17,1},{33,17},{49,33},{2,50}... | collective-permute-start | bytes 1376264 | tf_op jit(solution)/shard_map/ppermute | solution.py:23
  180.9 2.7 %collective-permute-start.48 = (bf16[2,64,1792]{2,1,0:T(8,128)(2,1)S(1)}, bf16[2,64,1792]{2,1,0:T(8,128)(2,1)S(1)}, u32[]{:S(2)}, u32[]{:S(2)}) collective-permute-start(bf16[2,64,1792]{2,1,0:T(8,128)(2,1)S(1)} %collective-permute-done.46.refs_2_), channel_id=1, source_target_pairs={{0,48},{16,0},{32,16},{48,32},{1,49},{17,1},{33,17},{49,33},{2,50}... | collective-permute-start | bytes 1376264 | tf_op jit(solution)/shard_map/ppermute | solution.py:23
  183.6 4.2 %collective-permute-done.57.refs_13_ = bf16[2,64,1792]{2,1,0:T(8,128)(2,1)S(1)} collective-permute-done((bf16[2,64,1792]{2,1,0:T(8,128)(2,1)S(1)}, bf16[2,64,1792]{2,1,0:T(8,128)(2,1)S(1)}, u32[]{:S(2)}, u32[]{:S(2)}) %collective-permute-start.57) | collective-permute-done | bytes 458784 | tf_op jit(solution)/shard_map/ppermute | solution.py:23
  188.4 4.4 %collective-permute-start.52 = (bf16[2,64,1792]{2,1,0:T(8,128)(2,1)S(1)}, bf16[2,64,1792]{2,1,0:T(8,128)(2,1)S(1)}, u32[]{:S(2)}, u32[]{:S(2)}) collective-permute-start(bf16[2,64,1792]{2,1,0:T(8,128)(2,1)S(1)} %collective-permute-done.46.refs_2_), channel_id=1, source_target_pairs={{0,8},{8,0},{1,9},{9,1},{2,10},{10,2},{3,11},{11,3},{4,12},{12,4},... | collective-permute-start | bytes 1376264 | tf_op jit(solution)/shard_map/ppermute | solution.py:23
  202.1 6.0 %outer_products.1 = (bf16[512,1792]{1,0:T(8,128)(2,1)}, bf16[512,1792]{1,0:T(8,128)(2,1)}) custom-call(s32[5]{0:T(128)S(1)} %stack.23.ids, bf16[512,1024]{1,0:T(8,128)(2,1)S(1)} %transposed_tokens.1.refs_5_.refs_0_, bf16[2,64,1792]{2,1,0:T(8,128)(2,1)S(1)} %errors.3.refs_1_, bf16[2,64,1792]{2,1,0:T(8,128)(2,1)S(1)} %collective-permute-done.46.refs_2_, ...), custom_call_target="tpu_custom_call" | custom-call | flops 3758096384 | bytes 15728640 | tf_op jit(solution)/shard_map/outer_products/pallas_call | solution.py:44
  (139 shorter events, 79.6 us)
Async XLA Ops:
  20.9 23.5 %collective-permute-start.6 = (bf16[3,32,1792]{2,1,0:T(8,128)(2,1)S(1)}, bf16[3,32,1792]{2,1,0:T(8,128)(2,1)S(1)}, u32[]{:S(2)}, u32[]{:S(2)}) collective-permute-start(bf16[3,32,1792]{2,1,0:T(8,128)(2,1)S(1)} %get-tuple-element.50), channel_id=1, source_target_pairs={{0,16},{16,32},{32,48},{48,0},{1,17},{17,33},{33,49},{49,1},{2,18}... | collective-permute-start | bytes 1032200 | tf_op jit(solution)/shard_map/ppermute | solution.py:23
  20.9 14.8 %collective-permute-start.9 = (bf16[3,32,1792]{2,1,0:T(8,128)(2,1)S(1)}, bf16[3,32,1792]{2,1,0:T(8,128)(2,1)S(1)}, u32[]{:S(2)}, u32[]{:S(2)}) collective-permute-start(bf16[3,32,1792]{2,1,0:T(8,128)(2,1)S(1)} %get-tuple-element.53), channel_id=1, source_target_pairs={{0,48},{16,0},{32,16},{48,32},{1,49},{17,1},{33,17},{49,33},{2,50}... | collective-permute-start | bytes 1032200 | tf_op jit(solution)/shard_map/ppermute | solution.py:23
  28.9 14.7 %collective-permute-start.8 = (bf16[3,32,1792]{2,1,0:T(8,128)(2,1)S(1)}, bf16[3,32,1792]{2,1,0:T(8,128)(2,1)S(1)}, u32[]{:S(2)}, u32[]{:S(2)}) collective-permute-start(bf16[3,32,1792]{2,1,0:T(8,128)(2,1)S(1)} %add_convert_fusion), channel_id=1, source_target_pairs={{0,16},{16,32},{32,48},{48,0},{1,17},{17,33},{33,49},{49,1},{2,18}... | collective-permute-start | bytes 1032200 | tf_op jit(solution)/shard_map/ppermute | solution.py:23
  29.1 15.4 %collective-permute-start.5 = (bf16[3,32,1792]{2,1,0:T(8,128)(2,1)S(1)}, bf16[3,32,1792]{2,1,0:T(8,128)(2,1)S(1)}, u32[]{:S(2)}, u32[]{:S(2)}) collective-permute-start(bf16[3,32,1792]{2,1,0:T(8,128)(2,1)S(1)} %add_convert_fusion.1), channel_id=1, source_target_pairs={{0,48},{16,0},{32,16},{48,32},{1,49},{17,1},{33,17},{49,33},{2,50}... | collective-permute-start | bytes 1032200 | tf_op jit(solution)/shard_map/ppermute | solution.py:23
  48.2 14.3 %collective-permute-start.30 = (bf16[2,32,1792]{2,1,0:T(8,128)(2,1)S(1)}, bf16[2,32,1792]{2,1,0:T(8,128)(2,1)S(1)}, u32[]{:S(2)}, u32[]{:S(2)}) collective-permute-start(bf16[2,32,1792]{2,1,0:T(8,128)(2,1)S(1)} %get-tuple-element.54.refs_3_.refs_0_), channel_id=1, source_target_pairs={{0,16},{16,32},{32,48},{48,0},{1,17},{17,33},{33,49},{49,1},{2,18}... | collective-permute-start | bytes 688136 | tf_op jit(solution)/shard_map/ppermute | solution.py:23
  48.6 18.7 %collective-permute-start.29 = (bf16[2,32,1792]{2,1,0:T(8,128)(2,1)S(1)}, bf16[2,32,1792]{2,1,0:T(8,128)(2,1)S(1)}, u32[]{:S(2)}, u32[]{:S(2)}) collective-permute-start(bf16[2,32,1792]{2,1,0:T(8,128)(2,1)S(1)} %get-tuple-element.54.refs_3_.refs_0_), channel_id=1, source_target_pairs={{0,32},{16,48},{32,0},{48,16},{1,33},{17,49},{33,1},{49,17},{2,34}... | collective-permute-start | bytes 688136 | tf_op jit(solution)/shard_map/ppermute | solution.py:23
  50.1 19.4 %collective-permute-start.28 = (bf16[2,32,1792]{2,1,0:T(8,128)(2,1)S(1)}, bf16[2,32,1792]{2,1,0:T(8,128)(2,1)S(1)}, u32[]{:S(2)}, u32[]{:S(2)}) collective-permute-start(bf16[2,32,1792]{2,1,0:T(8,128)(2,1)S(1)} %get-tuple-element.54.refs_3_.refs_0_), channel_id=1, source_target_pairs={{0,48},{16,0},{32,16},{48,32},{1,49},{17,1},{33,17},{49,33},{2,50}... | collective-permute-start | bytes 688136 | tf_op jit(solution)/shard_map/ppermute | solution.py:23
  52.7 16.8 %collective-permute-start.10 = (bf16[2,32,1792]{2,1,0:T(8,128)(2,1)S(1)}, bf16[2,32,1792]{2,1,0:T(8,128)(2,1)S(1)}, u32[]{:S(2)}, u32[]{:S(2)}) collective-permute-start(bf16[2,32,1792]{2,1,0:T(8,128)(2,1)S(1)} %get-tuple-element.55.refs_0_), channel_id=1, source_target_pairs={{0,48},{16,0},{32,16},{48,32},{1,49},{17,1},{33,17},{49,33},{2,50}... | collective-permute-start | bytes 688136 | tf_op jit(solution)/shard_map/ppermute | solution.py:23
  57.5 12.6 %collective-permute-start.31 = (bf16[2,32,1792]{2,1,0:T(8,128)(2,1)S(1)}, bf16[2,32,1792]{2,1,0:T(8,128)(2,1)S(1)}, u32[]{:S(2)}, u32[]{:S(2)}) collective-permute-start(bf16[2,32,1792]{2,1,0:T(8,128)(2,1)S(1)} %get-tuple-element.54.refs_3_.refs_0_), channel_id=1, source_target_pairs={{0,8},{8,0},{1,9},{9,1},{2,10},{10,2},{3,11},{11,3},{4,12},{12,4},... | collective-permute-start | bytes 688136 | tf_op jit(solution)/shard_map/ppermute | solution.py:23
  74.4 14.7 %collective-permute-start.35 = (bf16[512,256]{1,0:T(8,128)(2,1)S(1)}, bf16[512,256]{1,0:T(8,128)(2,1)S(1)}, u32[]{:S(2)}, u32[]{:S(2)}) collective-permute-start(bf16[512,256]{1,0:T(8,128)(2,1)S(1)} %get-tuple-element.69), channel_id=1, source_target_pairs={{0,2},{2,4},{4,6},{6,0},{1,3},{3,5},{5,7},{7,1},{8,10},{10,12},{12... | collective-permute-start | bytes 786440 | tf_op jit(solution)/shard_map/ppermute | solution.py:23
  76.1 15.1 %collective-permute-start.36 = (bf16[512,256]{1,0:T(8,128)(2,1)S(1)}, bf16[512,256]{1,0:T(8,128)(2,1)S(1)}, u32[]{:S(2)}, u32[]{:S(2)}) collective-permute-start(bf16[512,256]{1,0:T(8,128)(2,1)S(1)} %get-tuple-element.70), channel_id=1, source_target_pairs={{0,4},{2,6},{4,0},{6,2},{1,5},{3,7},{5,1},{7,3},{8,12},{10,14},{12... | collective-permute-start | bytes 786440 | tf_op jit(solution)/shard_map/ppermute | solution.py:23
  88.7 13.7 %collective-permute-start.18 = (bf16[512,256]{1,0:T(8,128)(2,1)S(1)}, bf16[512,256]{1,0:T(8,128)(2,1)S(1)}, u32[]{:S(2)}, u32[]{:S(2)}) collective-permute-start(bf16[512,256]{1,0:T(8,128)(2,1)S(1)} %get-tuple-element.58), channel_id=1, source_target_pairs={{0,4},{2,6},{4,0},{6,2},{1,5},{3,7},{5,1},{7,3},{8,12},{10,14},{12... | collective-permute-start | bytes 786440 | tf_op jit(solution)/shard_map/ppermute | solution.py:23
  89.1 13.4 %collective-permute-start.19 = (bf16[512,256]{1,0:T(8,128)(2,1)S(1)}, bf16[512,256]{1,0:T(8,128)(2,1)S(1)}, u32[]{:S(2)}, u32[]{:S(2)}) collective-permute-start(bf16[512,256]{1,0:T(8,128)(2,1)S(1)} %get-tuple-element.59), channel_id=1, source_target_pairs={{0,6},{2,0},{4,2},{6,4},{1,7},{3,1},{5,3},{7,5},{8,14},{10,8},{12,... | collective-permute-start | bytes 786440 | tf_op jit(solution)/shard_map/ppermute | solution.py:23
  91.9 14.2 %collective-permute-start.38 = (bf16[512,256]{1,0:T(8,128)(2,1)S(1)}, bf16[512,256]{1,0:T(8,128)(2,1)S(1)}, u32[]{:S(2)}, u32[]{:S(2)}) collective-permute-start(bf16[512,256]{1,0:T(8,128)(2,1)S(1)} %sum_z.3.refs_0_), channel_id=1, source_target_pairs={{0,1},{1,0},{2,3},{3,2},{4,5},{5,4},{6,7},{7,6},{8,9},{9,8},{10,11... | collective-permute-start | bytes 786440 | tf_op jit(solution)/shard_map/ppermute | solution.py:23
  94.7 25.4 %collective-permute-start = (bf16[512,512]{1,0:T(8,128)(2,1)S(1)}, bf16[512,512]{1,0:T(8,128)(2,1)S(1)}, u32[]{:S(2)}, u32[]{:S(2)}) collective-permute-start(bf16[512,512]{1,0:T(8,128)(2,1)S(1)} %constant_dynamic-slice_fusion), channel_id=1, source_target_pairs={{0,64},{64,0},{1,65},{65,1},{2,66},{66,2},{3,67},{67,3},{4,68},{68... | collective-permute-start | bytes 1572872 | tf_op jit(solution)/shard_map/ppermute | solution.py:23
  103.2 13.1 %collective-permute-start.20 = (bf16[512,256]{1,0:T(8,128)(2,1)S(1)}, bf16[512,256]{1,0:T(8,128)(2,1)S(1)}, u32[]{:S(2)}, u32[]{:S(2)}) collective-permute-start(bf16[512,256]{1,0:T(8,128)(2,1)S(1)} %sum_z.2.refs_0_), channel_id=1, source_target_pairs={{0,1},{1,0},{2,3},{3,2},{4,5},{5,4},{6,7},{7,6},{8,9},{9,8},{10,11... | collective-permute-start | bytes 786440 | tf_op jit(solution)/shard_map/ppermute | solution.py:23
  106.7 15.3 %collective-permute-start.41 = (bf16[512,256]{1,0:T(8,128)(2,1)S(1)}, bf16[512,256]{1,0:T(8,128)(2,1)S(1)}, u32[]{:S(2)}, u32[]{:S(2)}) collective-permute-start(bf16[512,256]{1,0:T(8,128)(2,1)S(1)} %residual.3.refs_0_), channel_id=1, source_target_pairs={{0,2},{2,4},{4,6},{6,0},{1,3},{3,5},{5,7},{7,1},{8,10},{10,12},{12... | collective-permute-start | bytes 786440 | tf_op jit(solution)/shard_map/ppermute | solution.py:23
  108.5 15.0 %collective-permute-start.40 = (bf16[512,256]{1,0:T(8,128)(2,1)S(1)}, bf16[512,256]{1,0:T(8,128)(2,1)S(1)}, u32[]{:S(2)}, u32[]{:S(2)}) collective-permute-start(bf16[512,256]{1,0:T(8,128)(2,1)S(1)} %residual.3.refs_0_), channel_id=1, source_target_pairs={{0,4},{2,6},{4,0},{6,2},{1,5},{3,7},{5,1},{7,3},{8,12},{10,14},{12... | collective-permute-start | bytes 786440 | tf_op jit(solution)/shard_map/ppermute | solution.py:23
  111.4 12.2 %collective-permute-start.39 = (bf16[512,256]{1,0:T(8,128)(2,1)S(1)}, bf16[512,256]{1,0:T(8,128)(2,1)S(1)}, u32[]{:S(2)}, u32[]{:S(2)}) collective-permute-start(bf16[512,256]{1,0:T(8,128)(2,1)S(1)} %residual.3.refs_0_), channel_id=1, source_target_pairs={{0,6},{2,0},{4,2},{6,4},{1,7},{3,1},{5,3},{7,5},{8,14},{10,8},{12,... | collective-permute-start | bytes 786440 | tf_op jit(solution)/shard_map/ppermute | solution.py:23
  116.9 12.9 %collective-permute-start.23 = (bf16[512,256]{1,0:T(8,128)(2,1)S(1)}, bf16[512,256]{1,0:T(8,128)(2,1)S(1)}, u32[]{:S(2)}, u32[]{:S(2)}) collective-permute-start(bf16[512,256]{1,0:T(8,128)(2,1)S(1)} %residual.2.refs_0_), channel_id=1, source_target_pairs={{0,2},{2,4},{4,6},{6,0},{1,3},{3,5},{5,7},{7,1},{8,10},{10,12},{12... | collective-permute-start | bytes 786440 | tf_op jit(solution)/shard_map/ppermute | solution.py:23
  120.2 13.6 %collective-permute-start.22 = (bf16[512,256]{1,0:T(8,128)(2,1)S(1)}, bf16[512,256]{1,0:T(8,128)(2,1)S(1)}, u32[]{:S(2)}, u32[]{:S(2)}) collective-permute-start(bf16[512,256]{1,0:T(8,128)(2,1)S(1)} %residual.2.refs_0_), channel_id=1, source_target_pairs={{0,4},{2,6},{4,0},{6,2},{1,5},{3,7},{5,1},{7,3},{8,12},{10,14},{12... | collective-permute-start | bytes 786440 | tf_op jit(solution)/shard_map/ppermute | solution.py:23
  139.9 13.3 %collective-permute-start.44 = (bf16[2,32,1792]{2,1,0:T(8,128)(2,1)S(1)}, bf16[2,32,1792]{2,1,0:T(8,128)(2,1)S(1)}, u32[]{:S(2)}, u32[]{:S(2)}) collective-permute-start(bf16[2,32,1792]{2,1,0:T(8,128)(2,1)S(1)} %get-tuple-element.76), channel_id=1, source_target_pairs={{0,32},{16,48},{32,0},{48,16},{1,33},{17,49},{33,1},{49,17},{2,34}... | collective-permute-start | bytes 688136 | tf_op jit(solution)/shard_map/ppermute | solution.py:23
  143.4 14.1 %collective-permute-start.25 = (bf16[2,32,1792]{2,1,0:T(8,128)(2,1)S(1)}, bf16[2,32,1792]{2,1,0:T(8,128)(2,1)S(1)}, u32[]{:S(2)}, u32[]{:S(2)}) collective-permute-start(bf16[2,32,1792]{2,1,0:T(8,128)(2,1)S(1)} %get-tuple-element.63), channel_id=1, source_target_pairs={{0,16},{16,32},{32,48},{48,0},{1,17},{17,33},{33,49},{49,1},{2,18}... | collective-permute-start | bytes 688136 | tf_op jit(solution)/shard_map/ppermute | solution.py:23
  144.8 18.2 %collective-permute-start.26 = (bf16[2,32,1792]{2,1,0:T(8,128)(2,1)S(1)}, bf16[2,32,1792]{2,1,0:T(8,128)(2,1)S(1)}, u32[]{:S(2)}, u32[]{:S(2)}) collective-permute-start(bf16[2,32,1792]{2,1,0:T(8,128)(2,1)S(1)} %get-tuple-element.64), channel_id=1, source_target_pairs={{0,32},{16,48},{32,0},{48,16},{1,33},{17,49},{33,1},{49,17},{2,34}... | collective-permute-start | bytes 688136 | tf_op jit(solution)/shard_map/ppermute | solution.py:23
  147.6 15.4 %collective-permute-start.27 = (bf16[2,32,1792]{2,1,0:T(8,128)(2,1)S(1)}, bf16[2,32,1792]{2,1,0:T(8,128)(2,1)S(1)}, u32[]{:S(2)}, u32[]{:S(2)}) collective-permute-start(bf16[2,32,1792]{2,1,0:T(8,128)(2,1)S(1)} %get-tuple-element.65), channel_id=1, source_target_pairs={{0,48},{16,0},{32,16},{48,32},{1,49},{17,1},{33,17},{49,33},{2,50}... | collective-permute-start | bytes 688136 | tf_op jit(solution)/shard_map/ppermute | solution.py:23
  163.7 12.1 %collective-permute-start.47 = (bf16[2,64,1792]{2,1,0:T(8,128)(2,1)S(1)}, bf16[2,64,1792]{2,1,0:T(8,128)(2,1)S(1)}, u32[]{:S(2)}, u32[]{:S(2)}) collective-permute-start(bf16[2,64,1792]{2,1,0:T(8,128)(2,1)S(1)} %errors.3.refs_1_), channel_id=1, source_target_pairs={{0,48},{16,0},{32,16},{48,32},{1,49},{17,1},{33,17},{49,33},{2,50}... | collective-permute-start | bytes 1376264 | tf_op jit(solution)/shard_map/ppermute | solution.py:23
  166.5 12.8 %collective-permute-start.49 = (bf16[2,64,1792]{2,1,0:T(8,128)(2,1)S(1)}, bf16[2,64,1792]{2,1,0:T(8,128)(2,1)S(1)}, u32[]{:S(2)}, u32[]{:S(2)}) collective-permute-start(bf16[2,64,1792]{2,1,0:T(8,128)(2,1)S(1)} %errors.3.refs_1_), channel_id=1, source_target_pairs={{0,16},{16,32},{32,48},{48,0},{1,17},{17,33},{33,49},{49,1},{2,18}... | collective-permute-start | bytes 1376264 | tf_op jit(solution)/shard_map/ppermute | solution.py:23
  166.5 14.4 %collective-permute-start.46 = (bf16[2,64,1792]{2,1,0:T(8,128)(2,1)S(1)}, bf16[2,64,1792]{2,1,0:T(8,128)(2,1)S(1)}, u32[]{:S(2)}, u32[]{:S(2)}) collective-permute-start(bf16[2,64,1792]{2,1,0:T(8,128)(2,1)S(1)} %errors.3.refs_1_), channel_id=1, source_target_pairs={{0,64},{64,0},{1,65},{65,1},{2,66},{66,2},{3,67},{67,3},{4,68},{68... | collective-permute-start | bytes 1376264 | tf_op jit(solution)/shard_map/ppermute | solution.py:23
  167.1 13.8 %collective-permute-start.51 = (bf16[2,64,1792]{2,1,0:T(8,128)(2,1)S(1)}, bf16[2,64,1792]{2,1,0:T(8,128)(2,1)S(1)}, u32[]{:S(2)}, u32[]{:S(2)}) collective-permute-start(bf16[2,64,1792]{2,1,0:T(8,128)(2,1)S(1)} %errors.3.refs_1_), channel_id=1, source_target_pairs={{0,8},{8,0},{1,9},{9,1},{2,10},{10,2},{3,11},{11,3},{4,12},{12,4},... | collective-permute-start | bytes 1376264 | tf_op jit(solution)/shard_map/ppermute | solution.py:23
  180.9 12.8 %collective-permute-start.50 = (bf16[2,64,1792]{2,1,0:T(8,128)(2,1)S(1)}, bf16[2,64,1792]{2,1,0:T(8,128)(2,1)S(1)}, u32[]{:S(2)}, u32[]{:S(2)}) collective-permute-start(bf16[2,64,1792]{2,1,0:T(8,128)(2,1)S(1)} %collective-permute-done.46.refs_2_), channel_id=1, source_target_pairs={{0,16},{16,32},{32,48},{48,0},{1,17},{17,33},{33,49},{49,1},{2,18}... | collective-permute-start | bytes 1376264 | tf_op jit(solution)/shard_map/ppermute | solution.py:23
  180.9 16.7 %collective-permute-start.48 = (bf16[2,64,1792]{2,1,0:T(8,128)(2,1)S(1)}, bf16[2,64,1792]{2,1,0:T(8,128)(2,1)S(1)}, u32[]{:S(2)}, u32[]{:S(2)}) collective-permute-start(bf16[2,64,1792]{2,1,0:T(8,128)(2,1)S(1)} %collective-permute-done.46.refs_2_), channel_id=1, source_target_pairs={{0,48},{16,0},{32,16},{48,32},{1,49},{17,1},{33,17},{49,33},{2,50}... | collective-permute-start | bytes 1376264 | tf_op jit(solution)/shard_map/ppermute | solution.py:23
  188.4 12.3 %collective-permute-start.52 = (bf16[2,64,1792]{2,1,0:T(8,128)(2,1)S(1)}, bf16[2,64,1792]{2,1,0:T(8,128)(2,1)S(1)}, u32[]{:S(2)}, u32[]{:S(2)}) collective-permute-start(bf16[2,64,1792]{2,1,0:T(8,128)(2,1)S(1)} %collective-permute-done.46.refs_2_), channel_id=1, source_target_pairs={{0,8},{8,0},{1,9},{9,1},{2,10},{10,2},{3,11},{11,3},{4,12},{12,4},... | collective-permute-start | bytes 1376264 | tf_op jit(solution)/shard_map/ppermute | solution.py:23
  (41 other events, 429.6 us)

commit v4 on v3

--- a/solution.py
+++ b/solution.py
@@ -184,26 +184,18 @@
     total = 8 * 2 * rows
 
     def body(ids, *refs):
-        p_refs, d_ref, o_refs, lhs = refs[:8], refs[8], refs[9:13], refs[13]
+        p_refs, d_ref, o_refs, (lhs, held) = refs[:8], refs[8], refs[9:13], refs[13:]
         for i, p_ref in enumerate(p_refs):
             lhs[2 * rows * i:2 * rows * (i + 1), :] = p_ref[...].reshape(2 * rows, cols)
 
-        def step(k, carry):
+        held[...] = jnp.dot(lhs[...], d_ref[...], preferred_element_type=F32).astype(BF)
+        for k, o_ref in enumerate(o_refs):
             at = pl.multiple_of(lax.rem(ids[3] + k, NZ) * tile, tile)
-            acc = jnp.dot(
-                lhs[...], d_ref[:, pl.ds(at, tile)], preferred_element_type=F32
-            ).astype(BF)
-            for i, o_ref in enumerate(o_refs):
-                @pl.when(k == i)
-                def _(o_ref=o_ref):
-                    o_ref[...] = acc
-            return carry
-
-        lax.fori_loop(0, NZ, step, 0)
+            o_ref[...] = held[:, pl.ds(at, tile)]
 
     outs = [shape((total, tile))] * NZ
     return call(
-        body, ids, (*pieces, down), outs, [pltpu.VMEM((total, cols), BF)],
+        body, ids, (*pieces, down), outs, [pltpu.VMEM((total, cols), BF), pltpu.VMEM((total, width), BF)],
         flops=2 * total * width * cols, limit=12)
 
 

time: 208 us -> 207 us (level)
  starting transfers between devices: 84.8 us -> 87.1 us
  waiting for transfers between devices: 78.2 us -> 76.1 us
    ppermute x61, starting transfers between devices: 84.8 us -> 87.1 us  [shift(): lax.ppermute(value, axis, [(i, (i + step) % size) for i in range(size)])]
    ppermute x61, waiting for transfers between devices: 78.2 us -> 76.1 us  [shift(): lax.ppermute(value, axis, [(i, (i + step) % size) for i in range(size)])]
  transfers between devices with their start and end apart: 61 -> 61, of which waited for: 25 -> 24; matrix products, arithmetic and copies ran while one was open for 0% -> 0% of each run, Pallas kernels for 12% -> 11%
where the time goes in v4:
time: 207 us
  starting transfers between devices  87.1 us (42%)
  waiting for transfers between devices  76.1 us (37%)
  Pallas kernels  35.5 us (17%)
  local copies, waits for them, and re-layouts  7.22 us (3%)
    ppermute x61, starting transfers between devices, shift(): lax.ppermute(value, axis, [(i, (i + step) % size) for i in range(size)])  87.1 us
    ppermute x61, waiting for transfers between devices, shift(): lax.ppermute(value, axis, [(i, (i + step) % size) for i in range(size)])  76.1 us
    pallas_call x21, Pallas kernels, call(): pl.pallas_call(kernel, out_shape=tuple(outs), in_specs=[pl.BlockSpec(memo...  35.5 us
    unnamed x24, local copies, waits for them, and re-layouts  7.1 us
  transfers between devices with their start and end apart: 61, of which 24 were waited for; matrix products, arithmetic and copies ran while one was open for 0% of the time, Pallas kernels for 11%

profile of v4, /device:TPU:1, one launch (start us, length us, event | category | flops | bytes accessed | tf_op | source)
XLA Modules:
  0.0 207.0 jit_solution(10388234546864424239)
XLA Ops:
  8.7 2.6 %pre_products.3 = (bf16[4,64,1792]{2,1,0:T(8,128)(2,1)S(1)}, bf16[4,64,1792]{2,1,0:T(8,128)(2,1)S(1)}) custom-call(s32[5]{0:T(128)S(1)} %stack.23.ids, bf16[512,1024]{1,0:T(8,128)(2,1)S(1)} %ordered_tokens.1.refs_0_, bf16[1024,1792]{1,0:T(8,128)(2,1)S(1)} %copy-done.3), custom_call_target="tpu_custom_call" | custom-call | flops 1879048192 | bytes 6553600 | tf_op jit(solution)/shard_map/pre_products/pallas_call | solution.py:44
  11.5 2.6 %pre_products.4 = (bf16[4,64,1792]{2,1,0:T(8,128)(2,1)S(1)}, bf16[4,64,1792]{2,1,0:T(8,128)(2,1)S(1)}) custom-call(s32[5]{0:T(128)S(1)} %stack.23.ids, bf16[512,1024]{1,0:T(8,128)(2,1)S(1)} %ordered_tokens.1.refs_0_, bf16[1024,1792]{1,0:T(8,128)(2,1)S(1)} %copy-done.4), custom_call_target="tpu_custom_call" | custom-call | flops 1879048192 | bytes 6553600 | tf_op jit(solution)/shard_map/pre_products/pallas_call | solution.py:44
  20.9 2.7 %collective-permute-start.9 = (bf16[3,32,1792]{2,1,0:T(8,128)(2,1)S(1)}, bf16[3,32,1792]{2,1,0:T(8,128)(2,1)S(1)}, u32[]{:S(2)}, u32[]{:S(2)}) collective-permute-start(bf16[3,32,1792]{2,1,0:T(8,128)(2,1)S(1)} %get-tuple-element.53), channel_id=1, source_target_pairs={{0,48},{16,0},{32,16},{48,32},{1,49},{17,1},{33,17},{49,33},{2,50}... | collective-permute-start | bytes 1032200 | tf_op jit(solution)/shard_map/ppermute | solution.py:23
  23.6 5.2 %collective-permute-done.7 = bf16[3,32,1792]{2,1,0:T(8,128)(2,1)S(1)} collective-permute-done((bf16[3,32,1792]{2,1,0:T(8,128)(2,1)S(1)}, bf16[3,32,1792]{2,1,0:T(8,128)(2,1)S(1)}, u32[]{:S(2)}, u32[]{:S(2)}) %collective-permute-start.7) | collective-permute-done | bytes 344096 | tf_op jit(solution)/shard_map/ppermute | solution.py:23
  29.1 2.7 %collective-permute-start.5 = (bf16[3,32,1792]{2,1,0:T(8,128)(2,1)S(1)}, bf16[3,32,1792]{2,1,0:T(8,128)(2,1)S(1)}, u32[]{:S(2)}, u32[]{:S(2)}) collective-permute-start(bf16[3,32,1792]{2,1,0:T(8,128)(2,1)S(1)} %add_convert_fusion.1), channel_id=1, source_target_pairs={{0,48},{16,0},{32,16},{48,32},{1,49},{17,1},{33,17},{49,33},{2,50}... | collective-permute-start | bytes 1032200 | tf_op jit(solution)/shard_map/ppermute | solution.py:23
  31.8 3.9 %collective-permute-done.9.refs_2_ = bf16[3,32,1792]{2,1,0:T(8,128)(2,1)S(1)} collective-permute-done((bf16[3,32,1792]{2,1,0:T(8,128)(2,1)S(1)}, bf16[3,32,1792]{2,1,0:T(8,128)(2,1)S(1)}, u32[]{:S(2)}, u32[]{:S(2)}) %collective-permute-start.9) | collective-permute-done | bytes 344096 | tf_op jit(solution)/shard_map/ppermute | solution.py:23
  35.7 7.8 %collective-permute-done.8.refs_1_ = bf16[3,32,1792]{2,1,0:T(8,128)(2,1)S(1)} collective-permute-done((bf16[3,32,1792]{2,1,0:T(8,128)(2,1)S(1)}, bf16[3,32,1792]{2,1,0:T(8,128)(2,1)S(1)}, u32[]{:S(2)}, u32[]{:S(2)}) %collective-permute-start.8) | collective-permute-done | bytes 344096 | tf_op jit(solution)/shard_map/ppermute | solution.py:23
  45.4 2.8 %collective-permute-start.11 = (bf16[2,32,1792]{2,1,0:T(8,128)(2,1)S(1)}, bf16[2,32,1792]{2,1,0:T(8,128)(2,1)S(1)}, u32[]{:S(2)}, u32[]{:S(2)}) collective-permute-start(bf16[2,32,1792]{2,1,0:T(8,128)(2,1)S(1)} %get-tuple-element.55.refs_0_), channel_id=1, source_target_pairs={{0,32},{16,48},{32,0},{48,16},{1,33},{17,49},{33,1},{49,17},{2,34}... | collective-permute-start | bytes 688136 | tf_op jit(solution)/shard_map/ppermute | solution.py:23
  52.8 4.7 %collective-permute-done.11.refs_2_ = bf16[2,32,1792]{2,1,0:T(8,128)(2,1)S(1)} collective-permute-done((bf16[2,32,1792]{2,1,0:T(8,128)(2,1)S(1)}, bf16[2,32,1792]{2,1,0:T(8,128)(2,1)S(1)}, u32[]{:S(2)}, u32[]{:S(2)}) %collective-permute-start.11) | collective-permute-done | bytes 229408 | tf_op jit(solution)/shard_map/ppermute | solution.py:23
  57.5 4.0 %collective-permute-start.31 = (bf16[2,32,1792]{2,1,0:T(8,128)(2,1)S(1)}, bf16[2,32,1792]{2,1,0:T(8,128)(2,1)S(1)}, u32[]{:S(2)}, u32[]{:S(2)}) collective-permute-start(bf16[2,32,1792]{2,1,0:T(8,128)(2,1)S(1)} %get-tuple-element.54.refs_3_.refs_0_), channel_id=1, source_target_pairs={{0,8},{8,0},{1,9},{9,1},{2,10},{10,2},{3,11},{11,3},{4,12},{12,4},... | collective-permute-start | bytes 688136 | tf_op jit(solution)/shard_map/ppermute | solution.py:23
  62.5 3.6 %collective-permute-start.34 = (bf16[2,32,1792]{2,1,0:T(8,128)(2,1)S(1)}, bf16[2,32,1792]{2,1,0:T(8,128)(2,1)S(1)}, u32[]{:S(2)}, u32[]{:S(2)}) collective-permute-start(bf16[2,32,1792]{2,1,0:T(8,128)(2,1)S(1)} %collective-permute-done.30.refs_3_), channel_id=1, source_target_pairs={{0,8},{8,0},{1,9},{9,1},{2,10},{10,2},{3,11},{11,3},{4,12},{12,4},... | collective-permute-start | bytes 688136 | tf_op jit(solution)/shard_map/ppermute | solution.py:23
  71.0 2.8 %down_products.3 = (bf16[512,256]{1,0:T(8,128)(2,1)S(1)}, bf16[512,256]{1,0:T(8,128)(2,1)S(1)}, bf16[512,256]{1,0:T(8,128)(2,1)S(1)}, bf16[512,256]{1,0:T(8,128)(2,1)S(1)}) custom-call(s32[5]{0:T(128)S(1)} %stack.23.ids, bf16[2,32,1792]{2,1,0:T(8,128)(2,1)S(1)} %get-tuple-element.54.refs_3_.refs_0_, ...), custom_call_target="tpu_custom_call" | custom-call | flops 1879048192 | bytes 6553600 | tf_op jit(solution)/shard_map/down_products/pallas_call | solution.py:44
  75.4 3.3 %collective-permute-start.36 = (bf16[512,256]{1,0:T(8,128)(2,1)S(1)}, bf16[512,256]{1,0:T(8,128)(2,1)S(1)}, u32[]{:S(2)}, u32[]{:S(2)}) collective-permute-start(bf16[512,256]{1,0:T(8,128)(2,1)S(1)} %get-tuple-element.70), channel_id=1, source_target_pairs={{0,4},{2,6},{4,0},{6,2},{1,5},{3,7},{5,1},{7,3},{8,12},{10,14},{12... | collective-permute-start | bytes 786440 | tf_op jit(solution)/shard_map/ppermute | solution.py:23
  83.3 3.3 %down_products.2 = (bf16[512,256]{1,0:T(8,128)(2,1)S(1)}, bf16[512,256]{1,0:T(8,128)(2,1)S(1)}, bf16[512,256]{1,0:T(8,128)(2,1)S(1)}, bf16[512,256]{1,0:T(8,128)(2,1)S(1)}) custom-call(s32[5]{0:T(128)S(1)} %stack.23.ids, bf16[2,32,1792]{2,1,0:T(8,128)(2,1)S(1)} %get-tuple-element.55.refs_0_, bf16[2,32,1792]{2,1,0:T(8,128)(2,1)S(1)} %collective-permute-done.10.refs_1_, ...), custom_call_target="tpu_custom_call" | custom-call | flops 1879048192 | bytes 6553600 | tf_op jit(solution)/shard_map/down_products/pallas_call | solution.py:44
  91.1 2.8 %collective-permute-start.38 = (bf16[512,256]{1,0:T(8,128)(2,1)S(1)}, bf16[512,256]{1,0:T(8,128)(2,1)S(1)}, u32[]{:S(2)}, u32[]{:S(2)}) collective-permute-start(bf16[512,256]{1,0:T(8,128)(2,1)S(1)} %sum_z.3.refs_0_), channel_id=1, source_target_pairs={{0,1},{1,0},{2,3},{3,2},{4,5},{5,4},{6,7},{7,6},{8,9},{9,8},{10,11... | collective-permute-start | bytes 786440 | tf_op jit(solution)/shard_map/ppermute | solution.py:23
  95.9 5.8 %collective-permute-done.18.refs_2_ = bf16[512,256]{1,0:T(8,128)(2,1)S(1)} collective-permute-done((bf16[512,256]{1,0:T(8,128)(2,1)S(1)}, bf16[512,256]{1,0:T(8,128)(2,1)S(1)}, u32[]{:S(2)}, u32[]{:S(2)}) %collective-permute-start.18) | collective-permute-done | bytes 262176 | tf_op jit(solution)/shard_map/ppermute | solution.py:23
  102.4 2.8 %collective-permute-start.20 = (bf16[512,256]{1,0:T(8,128)(2,1)S(1)}, bf16[512,256]{1,0:T(8,128)(2,1)S(1)}, u32[]{:S(2)}, u32[]{:S(2)}) collective-permute-start(bf16[512,256]{1,0:T(8,128)(2,1)S(1)} %sum_z.2.refs_0_), channel_id=1, source_target_pairs={{0,1},{1,0},{2,3},{3,2},{4,5},{5,4},{6,7},{7,6},{8,9},{9,8},{10,11... | collective-permute-start | bytes 786440 | tf_op jit(solution)/shard_map/ppermute | solution.py:23
  110.2 5.3 %collective-permute-done.20.refs_1_ = bf16[512,256]{1,0:T(8,128)(2,1)S(1)} collective-permute-done((bf16[512,256]{1,0:T(8,128)(2,1)S(1)}, bf16[512,256]{1,0:T(8,128)(2,1)S(1)}, u32[]{:S(2)}, u32[]{:S(2)}) %collective-permute-start.20) | collective-permute-done | bytes 262176 | tf_op jit(solution)/shard_map/ppermute | solution.py:23
  116.1 3.8 %collective-permute-start.23 = (bf16[512,256]{1,0:T(8,128)(2,1)S(1)}, bf16[512,256]{1,0:T(8,128)(2,1)S(1)}, u32[]{:S(2)}, u32[]{:S(2)}) collective-permute-start(bf16[512,256]{1,0:T(8,128)(2,1)S(1)} %residual.2.refs_0_), channel_id=1, source_target_pairs={{0,2},{2,4},{4,6},{6,0},{1,3},{3,5},{5,7},{7,1},{8,10},{10,12},{12... | collective-permute-start | bytes 786440 | tf_op jit(solution)/shard_map/ppermute | solution.py:23
  123.4 2.8 %back_products.3 = (bf16[4,2,32,1792]{3,2,1,0:T(8,128)(2,1)S(1)}, bf16[4,2,32,1792]{3,2,1,0:T(8,128)(2,1)S(1)}) custom-call(s32[5]{0:T(128)S(1)} %stack.23.ids, bf16[512,256]{1,0:T(8,128)(2,1)S(1)} %residual.3.refs_0_, bf16[512,256]{1,0:T(8,128)(2,1)S(1)} %collective-permute-done.39.refs_1_, bf16[512,256]{1,0:T(8,128)(2,1)S(1)} %collective-permute-done.40.refs_2_, ...), custom_call_target="tpu_custom_call" | custom-call | flops 1879048192 | bytes 6553600 | tf_op jit(solution)/shard_map/back_products/pallas_call | solution.py:44
  128.6 3.4 %collective-permute-done.22.refs_2_ = bf16[512,256]{1,0:T(8,128)(2,1)S(1)} collective-permute-done((bf16[512,256]{1,0:T(8,128)(2,1)S(1)}, bf16[512,256]{1,0:T(8,128)(2,1)S(1)}, u32[]{:S(2)}, u32[]{:S(2)}) %collective-permute-start.22) | collective-permute-done | bytes 262176 | tf_op jit(solution)/shard_map/ppermute | solution.py:23
  132.0 2.8 %back_products.2 = (bf16[4,2,32,1792]{3,2,1,0:T(8,128)(2,1)S(1)}, bf16[4,2,32,1792]{3,2,1,0:T(8,128)(2,1)S(1)}) custom-call(s32[5]{0:T(128)S(1)} %stack.23.ids, bf16[512,256]{1,0:T(8,128)(2,1)S(1)} %residual.2.refs_0_, bf16[512,256]{1,0:T(8,128)(2,1)S(1)} %collective-permute-done.21.refs_1_, bf16[512,256]{1,0:T(8,128)(2,1)S(1)} %collective-permute-done.22.refs_2_, ...), custom_call_target="tpu_custom_call" | custom-call | flops 1879048192 | bytes 6553600 | tf_op jit(solution)/shard_map/back_products/pallas_call | solution.py:44
  147.2 4.7 %collective-permute-done.44.refs_2_ = bf16[2,32,1792]{2,1,0:T(8,128)(2,1)S(1)} collective-permute-done((bf16[2,32,1792]{2,1,0:T(8,128)(2,1)S(1)}, bf16[2,32,1792]{2,1,0:T(8,128)(2,1)S(1)}, u32[]{:S(2)}, u32[]{:S(2)}) %collective-permute-start.44) | collective-permute-done | bytes 229408 | tf_op jit(solution)/shard_map/ppermute | solution.py:23
  152.7 3.5 %collective-permute-done.25.refs_1_ = bf16[2,32,1792]{2,1,0:T(8,128)(2,1)S(1)} collective-permute-done((bf16[2,32,1792]{2,1,0:T(8,128)(2,1)S(1)}, bf16[2,32,1792]{2,1,0:T(8,128)(2,1)S(1)}, u32[]{:S(2)}, u32[]{:S(2)}) %collective-permute-start.25) | collective-permute-done | bytes 229408 | tf_op jit(solution)/shard_map/ppermute | solution.py:23
  156.2 5.5 %collective-permute-done.26.refs_2_ = bf16[2,32,1792]{2,1,0:T(8,128)(2,1)S(1)} collective-permute-done((bf16[2,32,1792]{2,1,0:T(8,128)(2,1)S(1)}, bf16[2,32,1792]{2,1,0:T(8,128)(2,1)S(1)}, u32[]{:S(2)}, u32[]{:S(2)}) %collective-permute-start.26) | collective-permute-done | bytes 229408 | tf_op jit(solution)/shard_map/ppermute | solution.py:23
  162.5 2.7 %collective-permute-start.47 = (bf16[2,64,1792]{2,1,0:T(8,128)(2,1)S(1)}, bf16[2,64,1792]{2,1,0:T(8,128)(2,1)S(1)}, u32[]{:S(2)}, u32[]{:S(2)}) collective-permute-start(bf16[2,64,1792]{2,1,0:T(8,128)(2,1)S(1)} %errors.3.refs_1_), channel_id=1, source_target_pairs={{0,48},{16,0},{32,16},{48,32},{1,49},{17,1},{33,17},{49,33},{2,50}... | collective-permute-start | bytes 1376264 | tf_op jit(solution)/shard_map/ppermute | solution.py:23
  167.5 7.1 %collective-permute-done.47.refs_3_ = bf16[2,64,1792]{2,1,0:T(8,128)(2,1)S(1)} collective-permute-done((bf16[2,64,1792]{2,1,0:T(8,128)(2,1)S(1)}, bf16[2,64,1792]{2,1,0:T(8,128)(2,1)S(1)}, u32[]{:S(2)}, u32[]{:S(2)}) %collective-permute-start.47) | collective-permute-done | bytes 458784 | tf_op jit(solution)/shard_map/ppermute | solution.py:23
  174.6 3.4 %collective-permute-start.57 = (bf16[2,64,1792]{2,1,0:T(8,128)(2,1)S(1)}, bf16[2,64,1792]{2,1,0:T(8,128)(2,1)S(1)}, u32[]{:S(2)}, u32[]{:S(2)}) collective-permute-start(bf16[2,64,1792]{2,1,0:T(8,128)(2,1)S(1)} %collective-permute-done.47.refs_3_), channel_id=1, source_target_pairs={{0,48},{16,0},{32,16},{48,32},{1,49},{17,1},{33,17},{49,33},{2,50}... | collective-permute-start | bytes 1376264 | tf_op jit(solution)/shard_map/ppermute | solution.py:23
  179.7 2.7 %collective-permute-start.48 = (bf16[2,64,1792]{2,1,0:T(8,128)(2,1)S(1)}, bf16[2,64,1792]{2,1,0:T(8,128)(2,1)S(1)}, u32[]{:S(2)}, u32[]{:S(2)}) collective-permute-start(bf16[2,64,1792]{2,1,0:T(8,128)(2,1)S(1)} %collective-permute-done.46.refs_2_), channel_id=1, source_target_pairs={{0,48},{16,0},{32,16},{48,32},{1,49},{17,1},{33,17},{49,33},{2,50}... | collective-permute-start | bytes 1376264 | tf_op jit(solution)/shard_map/ppermute | solution.py:23
  182.4 4.2 %collective-permute-done.57.refs_13_ = bf16[2,64,1792]{2,1,0:T(8,128)(2,1)S(1)} collective-permute-done((bf16[2,64,1792]{2,1,0:T(8,128)(2,1)S(1)}, bf16[2,64,1792]{2,1,0:T(8,128)(2,1)S(1)}, u32[]{:S(2)}, u32[]{:S(2)}) %collective-permute-start.57) | collective-permute-done | bytes 458784 | tf_op jit(solution)/shard_map/ppermute | solution.py:23
  187.7 4.4 %collective-permute-start.52 = (bf16[2,64,1792]{2,1,0:T(8,128)(2,1)S(1)}, bf16[2,64,1792]{2,1,0:T(8,128)(2,1)S(1)}, u32[]{:S(2)}, u32[]{:S(2)}) collective-permute-start(bf16[2,64,1792]{2,1,0:T(8,128)(2,1)S(1)} %collective-permute-done.46.refs_2_), channel_id=1, source_target_pairs={{0,8},{8,0},{1,9},{9,1},{2,10},{10,2},{3,11},{11,3},{4,12},{12,4},... | collective-permute-start | bytes 1376264 | tf_op jit(solution)/shard_map/ppermute | solution.py:23
  200.9 6.0 %outer_products.1 = (bf16[512,1792]{1,0:T(8,128)(2,1)}, bf16[512,1792]{1,0:T(8,128)(2,1)}) custom-call(s32[5]{0:T(128)S(1)} %stack.23.ids, bf16[512,1024]{1,0:T(8,128)(2,1)S(1)} %transposed_tokens.1.refs_5_.refs_0_, bf16[2,64,1792]{2,1,0:T(8,128)(2,1)S(1)} %errors.3.refs_1_, bf16[2,64,1792]{2,1,0:T(8,128)(2,1)S(1)} %collective-permute-done.46.refs_2_, ...), custom_call_target="tpu_custom_call" | custom-call | flops 3758096384 | bytes 15728640 | tf_op jit(solution)/shard_map/outer_products/pallas_call | solution.py:44
  (139 shorter events, 80.3 us)
Async XLA Ops:
  20.9 23.5 %collective-permute-start.6 = (bf16[3,32,1792]{2,1,0:T(8,128)(2,1)S(1)}, bf16[3,32,1792]{2,1,0:T(8,128)(2,1)S(1)}, u32[]{:S(2)}, u32[]{:S(2)}) collective-permute-start(bf16[3,32,1792]{2,1,0:T(8,128)(2,1)S(1)} %get-tuple-element.50), channel_id=1, source_target_pairs={{0,16},{16,32},{32,48},{48,0},{1,17},{17,33},{33,49},{49,1},{2,18}... | collective-permute-start | bytes 1032200 | tf_op jit(solution)/shard_map/ppermute | solution.py:23
  20.9 14.8 %collective-permute-start.9 = (bf16[3,32,1792]{2,1,0:T(8,128)(2,1)S(1)}, bf16[3,32,1792]{2,1,0:T(8,128)(2,1)S(1)}, u32[]{:S(2)}, u32[]{:S(2)}) collective-permute-start(bf16[3,32,1792]{2,1,0:T(8,128)(2,1)S(1)} %get-tuple-element.53), channel_id=1, source_target_pairs={{0,48},{16,0},{32,16},{48,32},{1,49},{17,1},{33,17},{49,33},{2,50}... | collective-permute-start | bytes 1032200 | tf_op jit(solution)/shard_map/ppermute | solution.py:23
  28.9 14.7 %collective-permute-start.8 = (bf16[3,32,1792]{2,1,0:T(8,128)(2,1)S(1)}, bf16[3,32,1792]{2,1,0:T(8,128)(2,1)S(1)}, u32[]{:S(2)}, u32[]{:S(2)}) collective-permute-start(bf16[3,32,1792]{2,1,0:T(8,128)(2,1)S(1)} %add_convert_fusion), channel_id=1, source_target_pairs={{0,16},{16,32},{32,48},{48,0},{1,17},{17,33},{33,49},{49,1},{2,18}... | collective-permute-start | bytes 1032200 | tf_op jit(solution)/shard_map/ppermute | solution.py:23
  29.1 15.4 %collective-permute-start.5 = (bf16[3,32,1792]{2,1,0:T(8,128)(2,1)S(1)}, bf16[3,32,1792]{2,1,0:T(8,128)(2,1)S(1)}, u32[]{:S(2)}, u32[]{:S(2)}) collective-permute-start(bf16[3,32,1792]{2,1,0:T(8,128)(2,1)S(1)} %add_convert_fusion.1), channel_id=1, source_target_pairs={{0,48},{16,0},{32,16},{48,32},{1,49},{17,1},{33,17},{49,33},{2,50}... | collective-permute-start | bytes 1032200 | tf_op jit(solution)/shard_map/ppermute | solution.py:23
  45.4 12.1 %collective-permute-start.11 = (bf16[2,32,1792]{2,1,0:T(8,128)(2,1)S(1)}, bf16[2,32,1792]{2,1,0:T(8,128)(2,1)S(1)}, u32[]{:S(2)}, u32[]{:S(2)}) collective-permute-start(bf16[2,32,1792]{2,1,0:T(8,128)(2,1)S(1)} %get-tuple-element.55.refs_0_), channel_id=1, source_target_pairs={{0,32},{16,48},{32,0},{48,16},{1,33},{17,49},{33,1},{49,17},{2,34}... | collective-permute-start | bytes 688136 | tf_op jit(solution)/shard_map/ppermute | solution.py:23
  48.2 14.3 %collective-permute-start.30 = (bf16[2,32,1792]{2,1,0:T(8,128)(2,1)S(1)}, bf16[2,32,1792]{2,1,0:T(8,128)(2,1)S(1)}, u32[]{:S(2)}, u32[]{:S(2)}) collective-permute-start(bf16[2,32,1792]{2,1,0:T(8,128)(2,1)S(1)} %get-tuple-element.54.refs_3_.refs_0_), channel_id=1, source_target_pairs={{0,16},{16,32},{32,48},{48,0},{1,17},{17,33},{33,49},{49,1},{2,18}... | collective-permute-start | bytes 688136 | tf_op jit(solution)/shard_map/ppermute | solution.py:23
  48.6 18.7 %collective-permute-start.29 = (bf16[2,32,1792]{2,1,0:T(8,128)(2,1)S(1)}, bf16[2,32,1792]{2,1,0:T(8,128)(2,1)S(1)}, u32[]{:S(2)}, u32[]{:S(2)}) collective-permute-start(bf16[2,32,1792]{2,1,0:T(8,128)(2,1)S(1)} %get-tuple-element.54.refs_3_.refs_0_), channel_id=1, source_target_pairs={{0,32},{16,48},{32,0},{48,16},{1,33},{17,49},{33,1},{49,17},{2,34}... | collective-permute-start | bytes 688136 | tf_op jit(solution)/shard_map/ppermute | solution.py:23
  50.1 19.4 %collective-permute-start.28 = (bf16[2,32,1792]{2,1,0:T(8,128)(2,1)S(1)}, bf16[2,32,1792]{2,1,0:T(8,128)(2,1)S(1)}, u32[]{:S(2)}, u32[]{:S(2)}) collective-permute-start(bf16[2,32,1792]{2,1,0:T(8,128)(2,1)S(1)} %get-tuple-element.54.refs_3_.refs_0_), channel_id=1, source_target_pairs={{0,48},{16,0},{32,16},{48,32},{1,49},{17,1},{33,17},{49,33},{2,50}... | collective-permute-start | bytes 688136 | tf_op jit(solution)/shard_map/ppermute | solution.py:23
  52.7 16.8 %collective-permute-start.10 = (bf16[2,32,1792]{2,1,0:T(8,128)(2,1)S(1)}, bf16[2,32,1792]{2,1,0:T(8,128)(2,1)S(1)}, u32[]{:S(2)}, u32[]{:S(2)}) collective-permute-start(bf16[2,32,1792]{2,1,0:T(8,128)(2,1)S(1)} %get-tuple-element.55.refs_0_), channel_id=1, source_target_pairs={{0,48},{16,0},{32,16},{48,32},{1,49},{17,1},{33,17},{49,33},{2,50}... | collective-permute-start | bytes 688136 | tf_op jit(solution)/shard_map/ppermute | solution.py:23
  57.5 12.6 %collective-permute-start.31 = (bf16[2,32,1792]{2,1,0:T(8,128)(2,1)S(1)}, bf16[2,32,1792]{2,1,0:T(8,128)(2,1)S(1)}, u32[]{:S(2)}, u32[]{:S(2)}) collective-permute-start(bf16[2,32,1792]{2,1,0:T(8,128)(2,1)S(1)} %get-tuple-element.54.refs_3_.refs_0_), channel_id=1, source_target_pairs={{0,8},{8,0},{1,9},{9,1},{2,10},{10,2},{3,11},{11,3},{4,12},{12,4},... | collective-permute-start | bytes 688136 | tf_op jit(solution)/shard_map/ppermute | solution.py:23
  73.8 14.1 %collective-permute-start.35 = (bf16[512,256]{1,0:T(8,128)(2,1)S(1)}, bf16[512,256]{1,0:T(8,128)(2,1)S(1)}, u32[]{:S(2)}, u32[]{:S(2)}) collective-permute-start(bf16[512,256]{1,0:T(8,128)(2,1)S(1)} %get-tuple-element.69), channel_id=1, source_target_pairs={{0,2},{2,4},{4,6},{6,0},{1,3},{3,5},{5,7},{7,1},{8,10},{10,12},{12... | collective-permute-start | bytes 786440 | tf_op jit(solution)/shard_map/ppermute | solution.py:23
  75.4 15.0 %collective-permute-start.36 = (bf16[512,256]{1,0:T(8,128)(2,1)S(1)}, bf16[512,256]{1,0:T(8,128)(2,1)S(1)}, u32[]{:S(2)}, u32[]{:S(2)}) collective-permute-start(bf16[512,256]{1,0:T(8,128)(2,1)S(1)} %get-tuple-element.70), channel_id=1, source_target_pairs={{0,4},{2,6},{4,0},{6,2},{1,5},{3,7},{5,1},{7,3},{8,12},{10,14},{12... | collective-permute-start | bytes 786440 | tf_op jit(solution)/shard_map/ppermute | solution.py:23
  87.4 14.3 %collective-permute-start.18 = (bf16[512,256]{1,0:T(8,128)(2,1)S(1)}, bf16[512,256]{1,0:T(8,128)(2,1)S(1)}, u32[]{:S(2)}, u32[]{:S(2)}) collective-permute-start(bf16[512,256]{1,0:T(8,128)(2,1)S(1)} %get-tuple-element.58), channel_id=1, source_target_pairs={{0,4},{2,6},{4,0},{6,2},{1,5},{3,7},{5,1},{7,3},{8,12},{10,14},{12... | collective-permute-start | bytes 786440 | tf_op jit(solution)/shard_map/ppermute | solution.py:23
  87.8 13.9 %collective-permute-start.19 = (bf16[512,256]{1,0:T(8,128)(2,1)S(1)}, bf16[512,256]{1,0:T(8,128)(2,1)S(1)}, u32[]{:S(2)}, u32[]{:S(2)}) collective-permute-start(bf16[512,256]{1,0:T(8,128)(2,1)S(1)} %get-tuple-element.59), channel_id=1, source_target_pairs={{0,6},{2,0},{4,2},{6,4},{1,7},{3,1},{5,3},{7,5},{8,14},{10,8},{12,... | collective-permute-start | bytes 786440 | tf_op jit(solution)/shard_map/ppermute | solution.py:23
  91.1 14.0 %collective-permute-start.38 = (bf16[512,256]{1,0:T(8,128)(2,1)S(1)}, bf16[512,256]{1,0:T(8,128)(2,1)S(1)}, u32[]{:S(2)}, u32[]{:S(2)}) collective-permute-start(bf16[512,256]{1,0:T(8,128)(2,1)S(1)} %sum_z.3.refs_0_), channel_id=1, source_target_pairs={{0,1},{1,0},{2,3},{3,2},{4,5},{5,4},{6,7},{7,6},{8,9},{9,8},{10,11... | collective-permute-start | bytes 786440 | tf_op jit(solution)/shard_map/ppermute | solution.py:23
  94.0 25.9 %collective-permute-start = (bf16[512,512]{1,0:T(8,128)(2,1)S(1)}, bf16[512,512]{1,0:T(8,128)(2,1)S(1)}, u32[]{:S(2)}, u32[]{:S(2)}) collective-permute-start(bf16[512,512]{1,0:T(8,128)(2,1)S(1)} %constant_dynamic-slice_fusion), channel_id=1, source_target_pairs={{0,64},{64,0},{1,65},{65,1},{2,66},{66,2},{3,67},{67,3},{4,68},{68... | collective-permute-start | bytes 1572872 | tf_op jit(solution)/shard_map/ppermute | solution.py:23
  102.4 13.1 %collective-permute-start.20 = (bf16[512,256]{1,0:T(8,128)(2,1)S(1)}, bf16[512,256]{1,0:T(8,128)(2,1)S(1)}, u32[]{:S(2)}, u32[]{:S(2)}) collective-permute-start(bf16[512,256]{1,0:T(8,128)(2,1)S(1)} %sum_z.2.refs_0_), channel_id=1, source_target_pairs={{0,1},{1,0},{2,3},{3,2},{4,5},{5,4},{6,7},{7,6},{8,9},{9,8},{10,11... | collective-permute-start | bytes 786440 | tf_op jit(solution)/shard_map/ppermute | solution.py:23
  105.8 15.6 %collective-permute-start.41 = (bf16[512,256]{1,0:T(8,128)(2,1)S(1)}, bf16[512,256]{1,0:T(8,128)(2,1)S(1)}, u32[]{:S(2)}, u32[]{:S(2)}) collective-permute-start(bf16[512,256]{1,0:T(8,128)(2,1)S(1)} %residual.3.refs_0_), channel_id=1, source_target_pairs={{0,2},{2,4},{4,6},{6,0},{1,3},{3,5},{5,7},{7,1},{8,10},{10,12},{12... | collective-permute-start | bytes 786440 | tf_op jit(solution)/shard_map/ppermute | solution.py:23
  107.7 15.6 %collective-permute-start.40 = (bf16[512,256]{1,0:T(8,128)(2,1)S(1)}, bf16[512,256]{1,0:T(8,128)(2,1)S(1)}, u32[]{:S(2)}, u32[]{:S(2)}) collective-permute-start(bf16[512,256]{1,0:T(8,128)(2,1)S(1)} %residual.3.refs_0_), channel_id=1, source_target_pairs={{0,4},{2,6},{4,0},{6,2},{1,5},{3,7},{5,1},{7,3},{8,12},{10,14},{12... | collective-permute-start | bytes 786440 | tf_op jit(solution)/shard_map/ppermute | solution.py:23
  110.0 13.3 %collective-permute-start.39 = (bf16[512,256]{1,0:T(8,128)(2,1)S(1)}, bf16[512,256]{1,0:T(8,128)(2,1)S(1)}, u32[]{:S(2)}, u32[]{:S(2)}) collective-permute-start(bf16[512,256]{1,0:T(8,128)(2,1)S(1)} %residual.3.refs_0_), channel_id=1, source_target_pairs={{0,6},{2,0},{4,2},{6,4},{1,7},{3,1},{5,3},{7,5},{8,14},{10,8},{12,... | collective-permute-start | bytes 786440 | tf_op jit(solution)/shard_map/ppermute | solution.py:23
  116.1 12.5 %collective-permute-start.23 = (bf16[512,256]{1,0:T(8,128)(2,1)S(1)}, bf16[512,256]{1,0:T(8,128)(2,1)S(1)}, u32[]{:S(2)}, u32[]{:S(2)}) collective-permute-start(bf16[512,256]{1,0:T(8,128)(2,1)S(1)} %residual.2.refs_0_), channel_id=1, source_target_pairs={{0,2},{2,4},{4,6},{6,0},{1,3},{3,5},{5,7},{7,1},{8,10},{10,12},{12... | collective-permute-start | bytes 786440 | tf_op jit(solution)/shard_map/ppermute | solution.py:23
  138.6 13.3 %collective-permute-start.44 = (bf16[2,32,1792]{2,1,0:T(8,128)(2,1)S(1)}, bf16[2,32,1792]{2,1,0:T(8,128)(2,1)S(1)}, u32[]{:S(2)}, u32[]{:S(2)}) collective-permute-start(bf16[2,32,1792]{2,1,0:T(8,128)(2,1)S(1)} %get-tuple-element.76), channel_id=1, source_target_pairs={{0,32},{16,48},{32,0},{48,16},{1,33},{17,49},{33,1},{49,17},{2,34}... | collective-permute-start | bytes 688136 | tf_op jit(solution)/shard_map/ppermute | solution.py:23
  142.1 14.1 %collective-permute-start.25 = (bf16[2,32,1792]{2,1,0:T(8,128)(2,1)S(1)}, bf16[2,32,1792]{2,1,0:T(8,128)(2,1)S(1)}, u32[]{:S(2)}, u32[]{:S(2)}) collective-permute-start(bf16[2,32,1792]{2,1,0:T(8,128)(2,1)S(1)} %get-tuple-element.63), channel_id=1, source_target_pairs={{0,16},{16,32},{32,48},{48,0},{1,17},{17,33},{33,49},{49,1},{2,18}... | collective-permute-start | bytes 688136 | tf_op jit(solution)/shard_map/ppermute | solution.py:23
  143.5 18.2 %collective-permute-start.26 = (bf16[2,32,1792]{2,1,0:T(8,128)(2,1)S(1)}, bf16[2,32,1792]{2,1,0:T(8,128)(2,1)S(1)}, u32[]{:S(2)}, u32[]{:S(2)}) collective-permute-start(bf16[2,32,1792]{2,1,0:T(8,128)(2,1)S(1)} %get-tuple-element.64), channel_id=1, source_target_pairs={{0,32},{16,48},{32,0},{48,16},{1,33},{17,49},{33,1},{49,17},{2,34}... | collective-permute-start | bytes 688136 | tf_op jit(solution)/shard_map/ppermute | solution.py:23
  146.4 15.4 %collective-permute-start.27 = (bf16[2,32,1792]{2,1,0:T(8,128)(2,1)S(1)}, bf16[2,32,1792]{2,1,0:T(8,128)(2,1)S(1)}, u32[]{:S(2)}, u32[]{:S(2)}) collective-permute-start(bf16[2,32,1792]{2,1,0:T(8,128)(2,1)S(1)} %get-tuple-element.65), channel_id=1, source_target_pairs={{0,48},{16,0},{32,16},{48,32},{1,49},{17,1},{33,17},{49,33},{2,50}... | collective-permute-start | bytes 688136 | tf_op jit(solution)/shard_map/ppermute | solution.py:23
  162.5 12.1 %collective-permute-start.47 = (bf16[2,64,1792]{2,1,0:T(8,128)(2,1)S(1)}, bf16[2,64,1792]{2,1,0:T(8,128)(2,1)S(1)}, u32[]{:S(2)}, u32[]{:S(2)}) collective-permute-start(bf16[2,64,1792]{2,1,0:T(8,128)(2,1)S(1)} %errors.3.refs_1_), channel_id=1, source_target_pairs={{0,48},{16,0},{32,16},{48,32},{1,49},{17,1},{33,17},{49,33},{2,50}... | collective-permute-start | bytes 1376264 | tf_op jit(solution)/shard_map/ppermute | solution.py:23
  165.2 12.8 %collective-permute-start.49 = (bf16[2,64,1792]{2,1,0:T(8,128)(2,1)S(1)}, bf16[2,64,1792]{2,1,0:T(8,128)(2,1)S(1)}, u32[]{:S(2)}, u32[]{:S(2)}) collective-permute-start(bf16[2,64,1792]{2,1,0:T(8,128)(2,1)S(1)} %errors.3.refs_1_), channel_id=1, source_target_pairs={{0,16},{16,32},{32,48},{48,0},{1,17},{17,33},{33,49},{49,1},{2,18}... | collective-permute-start | bytes 1376264 | tf_op jit(solution)/shard_map/ppermute | solution.py:23
  165.2 14.4 %collective-permute-start.46 = (bf16[2,64,1792]{2,1,0:T(8,128)(2,1)S(1)}, bf16[2,64,1792]{2,1,0:T(8,128)(2,1)S(1)}, u32[]{:S(2)}, u32[]{:S(2)}) collective-permute-start(bf16[2,64,1792]{2,1,0:T(8,128)(2,1)S(1)} %errors.3.refs_1_), channel_id=1, source_target_pairs={{0,64},{64,0},{1,65},{65,1},{2,66},{66,2},{3,67},{67,3},{4,68},{68... | collective-permute-start | bytes 1376264 | tf_op jit(solution)/shard_map/ppermute | solution.py:23
  166.4 13.2 %collective-permute-start.51 = (bf16[2,64,1792]{2,1,0:T(8,128)(2,1)S(1)}, bf16[2,64,1792]{2,1,0:T(8,128)(2,1)S(1)}, u32[]{:S(2)}, u32[]{:S(2)}) collective-permute-start(bf16[2,64,1792]{2,1,0:T(8,128)(2,1)S(1)} %errors.3.refs_1_), channel_id=1, source_target_pairs={{0,8},{8,0},{1,9},{9,1},{2,10},{10,2},{3,11},{11,3},{4,12},{12,4},... | collective-permute-start | bytes 1376264 | tf_op jit(solution)/shard_map/ppermute | solution.py:23
  179.7 12.5 %collective-permute-start.53 = (bf16[2,64,1792]{2,1,0:T(8,128)(2,1)S(1)}, bf16[2,64,1792]{2,1,0:T(8,128)(2,1)S(1)}, u32[]{:S(2)}, u32[]{:S(2)}) collective-permute-start(bf16[2,64,1792]{2,1,0:T(8,128)(2,1)S(1)} %collective-permute-done.47.refs_3_), channel_id=1, source_target_pairs={{0,8},{8,0},{1,9},{9,1},{2,10},{10,2},{3,11},{11,3},{4,12},{12,4},... | collective-permute-start | bytes 1376264 | tf_op jit(solution)/shard_map/ppermute | solution.py:23
  179.7 12.8 %collective-permute-start.50 = (bf16[2,64,1792]{2,1,0:T(8,128)(2,1)S(1)}, bf16[2,64,1792]{2,1,0:T(8,128)(2,1)S(1)}, u32[]{:S(2)}, u32[]{:S(2)}) collective-permute-start(bf16[2,64,1792]{2,1,0:T(8,128)(2,1)S(1)} %collective-permute-done.46.refs_2_), channel_id=1, source_target_pairs={{0,16},{16,32},{32,48},{48,0},{1,17},{17,33},{33,49},{49,1},{2,18}... | collective-permute-start | bytes 1376264 | tf_op jit(solution)/shard_map/ppermute | solution.py:23
  179.7 16.7 %collective-permute-start.48 = (bf16[2,64,1792]{2,1,0:T(8,128)(2,1)S(1)}, bf16[2,64,1792]{2,1,0:T(8,128)(2,1)S(1)}, u32[]{:S(2)}, u32[]{:S(2)}) collective-permute-start(bf16[2,64,1792]{2,1,0:T(8,128)(2,1)S(1)} %collective-permute-done.46.refs_2_), channel_id=1, source_target_pairs={{0,48},{16,0},{32,16},{48,32},{1,49},{17,1},{33,17},{49,33},{2,50}... | collective-permute-start | bytes 1376264 | tf_op jit(solution)/shard_map/ppermute | solution.py:23
  (41 other events, 426.1 us)
